TPU v7x, 256 devices: a whole 4x4x8 slice. The times are simulated.
256 devices in a mesh: image: 16 (over x_lo, z), domain: 16 (over y, x_hi, core).
Axes of the slice: x: 4 (x_hi: 2, x_lo: 2; x = x_hi * 2 + x_lo), y: 4, z: 8, core: 2. Of those that a mesh axis runs over, the one named last changes fastest.
Arguments:
- field: float32 [16, 64, 64, 128], P('image', 'domain'), may hold values from -0.9 to 1.1
- mobility: float32 [64, 64, 128], P('domain'), may hold values from 0.2 to 1
- lower: int32 [2, 16], P(None, 'image'), may hold values from 0 to 14, as said below
- weights: float32 [2, 16], P(None, 'image'), may hold values from 0 to 1
Outputs:
- evolved: float32 [16, 64, 64, 128], P('image', 'domain')
- arclength: float32 [2, 16], P(None, 'image')
Inputs may be any that keep to these rules, and one draw needn't show every extreme that they name: lower[c, i] is i - 1 or i.
All inputs are finite; a program needn't handle non-finite values.
Results may differ from a plain program's by a relative error of at most 0.0001.
Values sent between devices are 32-bit elements; how exact they have to be, the bound alone decides.
No kernel may reach another device: no remote copies, remote signals or barrier semaphores. Data moves between devices by JAX's collectives and lax.ppermute only.
A program may use at most 64 MiB of HBM per device.

v0:
```python
import jax
import jax.numpy as jnp
from jax import lax
from jax.experimental import pallas as pl
from jax.experimental.pallas import tpu as pltpu
from jax.sharding import PartitionSpec as P

STEPS = 8
CYCLES = 2

stiffness = 1.0
time_step = 0.008
epsilon = 1e-06

VMEM = pl.BlockSpec(memory_space=pltpu.VMEM)
SMEM = pl.BlockSpec(memory_space=pltpu.SMEM)


def fetched(value, offset):
    size = lax.axis_size("domain")
    return lax.ppermute(value, "domain", [((i + offset) % size, i) for i in range(size)])


def partnered(value):
    size = lax.axis_size("domain")
    return lax.ppermute(value, "domain", [(i ^ 1, i) for i in range(size)])


def passed_along(value, steps):
    count = lax.axis_size("image")
    first, last = (max(0, -steps), min(count, count - steps))
    return lax.ppermute(value, "image", [(i, i + steps) for i in range(first, last)])


def halo_pieces(own, parity):
    after2, before2 = fetched(own, 2), fetched(own, -2)
    after4, before4 = fetched(own, 4), fetched(own, -4)
    chosen = jnp.where(parity == 0, after4, before4)
    return (own, before4, before2, after2, after4) + tuple(
        partnered(piece) for piece in (chosen, before2, own, after2)
    )


def fill(window, parity, pieces, rows):
    own, before4, before2, after2, after4, *others = pieces
    for place, piece in ((0, before4), (2, before2), (4, own), (6, after2), (8, after4)):
        window[pl.ds(place * rows, rows)] = piece[...]

    @pl.when(parity == 0)
    def _():
        for place, piece in zip((1, 3, 5, 7), others):
            window[pl.ds(place * rows, rows)] = piece[...]

    @pl.when(parity != 0)
    def _():
        for place, piece in zip((7, 1, 3, 5), others):
            window[pl.ds(place * rows, rows)] = piece[...]


def shifted(plane, offset, dimension):
    return pltpu.roll(plane, offset % plane.shape[dimension], dimension)


def potential_and_motion(field, mobile, row):
    here = field[row]
    square = here * here
    around = field[row - 1] + field[row + 1]
    for dimension in (0, 1):
        around = around + (shifted(here, 1, dimension) + shifted(here, -1, dimension))
    potential = here * (square + 5.0) - around
    motion = mobile[row] / (1.0 + square)
    return potential, motion


def take_steps(field, mobile, length):
    for step in range(STEPS):
        first, last = 2 * step + 2, length - 2 * step - 2
        before = potential_and_motion(field, mobile, first - 1)
        now = potential_and_motion(field, mobile, first)
        inflow = (before[1] + now[1]) * (now[0] - before[0])

        def one_row(row, carried):
            potential, motion, inflow = carried
            ahead = potential_and_motion(field, mobile, row + 1)
            outflow = (motion + ahead[1]) * (ahead[0] - potential)
            change = outflow - inflow
            for dimension in (0, 1):
                flow = (motion + shifted(motion, 1, dimension)) * (
                    potential - shifted(potential, 1, dimension)
                )
                change = change + (shifted(flow, -1, dimension) - flow)
            field[row] = field[row] + change
            return ahead[0], ahead[1], outflow

        lax.fori_loop(first, last, one_row, (now[0], now[1], inflow))


def first_kernel(parity_ref, *refs):
    fields, mobiles = refs[:9], refs[9:18]
    out, mobile_out, window = refs[18:]
    rows = out.shape[0]
    parity = parity_ref[0]
    fill(window, parity, fields, rows)
    fill(mobile_out, parity, mobiles, rows)
    mobile_out[...] = mobile_out[...] * (0.5 * time_step)
    take_steps(window, mobile_out, 9 * rows)
    out[...] = window[pl.ds(4 * rows, rows)]


def later_kernel(parity_ref, *refs):
    fields, mobile, out, window = refs[:9], refs[9], refs[10], refs[11]
    rows = out.shape[0]
    fill(window, parity_ref[0], fields, rows)
    take_steps(window, mobile, 9 * rows)
    out[...] = window[pl.ds(4 * rows, rows)]


def mix_kernel(scalar_ref, weight_ref, own, left, right, out, total):
    weight = weight_ref[0]
    here, after = own[...], right[...]
    total[...] = jnp.zeros_like(total) + jnp.sum(jnp.square(after - here))

    @pl.when(scalar_ref[0] == 0)
    def _():
        out[...] = weight * left[...] + (1.0 - weight) * here

    @pl.when(scalar_ref[0] != 0)
    def _():
        out[...] = weight * here + (1.0 - weight) * after


def length_kernel(cells, images, index_ref, gaps, out):
    distance = jnp.sqrt(
        jnp.sum(gaps[...].reshape(images, -1, CYCLES, 128), axis=1) / cells + epsilon
    )
    position = lax.broadcasted_iota(jnp.int32, distance.shape, 0)
    kept = jnp.where(position < index_ref[0], distance, 0.0)
    out[...] = jnp.sum(kept, axis=0)[:, :1]


def per_device(field, mobility, lower, weights):
    shape = field.shape[1:]
    rows = shape[0]
    image_count, domain_count = lax.axis_size("image"), lax.axis_size("domain")
    image_index = lax.axis_index("image")
    parity = lax.rem(lax.axis_index("domain"), 2)
    parities = parity[None]
    cells = rows * domain_count * shape[1] * shape[2]
    plane = jax.ShapeDtypeStruct(shape, jnp.float32)
    wide = (9 * rows,) + shape[1:]
    window = pltpu.VMEM(wide, jnp.float32)

    both = halo_pieces(jnp.stack([field[0], mobility]), parity)
    phase, mobile = pl.pallas_call(
        first_kernel,
        out_shape=(plane, jax.ShapeDtypeStruct(wide, jnp.float32)),
        in_specs=[SMEM] + [VMEM] * 18,
        out_specs=(VMEM, VMEM),
        scratch_shapes=[window],
    )(parities, *(piece[0] for piece in both), *(piece[1] for piece in both))

    totals = []
    for cycle in range(CYCLES):
        if cycle:
            phase = pl.pallas_call(
                later_kernel,
                out_shape=plane,
                in_specs=[SMEM] + [VMEM] * 10,
                out_specs=VMEM,
                scratch_shapes=[window],
            )(parities, *halo_pieces(phase, parity), mobile)
        left, right = passed_along(phase, 1), passed_along(phase, -1)
        from_left = (lower[cycle] >= image_index).astype(jnp.int32)
        phase, total = pl.pallas_call(
            mix_kernel,
            out_shape=(plane, jax.ShapeDtypeStruct((1, 128), jnp.float32)),
            in_specs=[SMEM, SMEM] + [VMEM] * 3,
            out_specs=(VMEM, VMEM),
        )(from_left, weights[cycle], phase, left, right)
        totals.append(total)
    mine = jnp.concatenate(totals, axis=0)
    everyone = jnp.broadcast_to(mine[None], (image_count * domain_count, CYCLES, 128))
    gaps = lax.all_to_all(everyone, ("image", "domain"), 0, 0)
    arclength = pl.pallas_call(
        lambda *refs: length_kernel(cells, image_count, *refs),
        out_shape=jax.ShapeDtypeStruct((CYCLES, 1), jnp.float32),
        in_specs=[SMEM, VMEM],
        out_specs=VMEM,
    )(image_index[None], gaps)
    return phase[None], arclength


def solution(mesh):
    return jax.shard_map(
        per_device,
        mesh=mesh,
        in_specs=(
            P("image", "domain", None, None),
            P("domain", None, None),
            P(None, "image"),
            P(None, "image"),
        ),
        out_specs=(P("image", "domain", None, None), P(None, "image")),
        check_vma=False,
    )
```

profile of v0, /device:TPU:1, one launch (start us, length us, event | category | flops | bytes accessed | tf_op | source)
XLA Modules:
  0.0 155.1 jit_solution(9381023382610299229)
XLA Ops:
  0.6 1.0 pad_maximum_fusion
  1.6 2.2 %collective-permute-start = (f32[2,4,64,128]{3,2,1,0:T(8,128)S(1)}, f32[2,4,64,128]{3,2,1,0:T(8,128)S(1)}, u32[]{:S(2)}, u32[]{:S(2)}) collective-permute-start(f32[2,4,64,128]{3,2,1,0:T(8,128)S(1)} %pad_maximum_fusion), channel_id=1, source_target_pairs={{12,0},{13,1},{14,2},{15,3},{0,4},{1,5},{2,6},{3,7},{4,8},{5,9},{6... | collective-permute-start | bytes 786440 | tf_op jit(solution)/shard_map/ppermute | solution.py:21
  3.8 1.5 collective-permute-start.3
  5.3 3.8 %collective-permute-start.2 = (f32[2,4,64,128]{3,2,1,0:T(8,128)S(1)}, f32[2,4,64,128]{3,2,1,0:T(8,128)S(1)}, u32[]{:S(2)}, u32[]{:S(2)}) collective-permute-start(f32[2,4,64,128]{3,2,1,0:T(8,128)S(1)} %pad_maximum_fusion), channel_id=1, source_target_pairs={{2,0},{3,1},{4,2},{5,3},{6,4},{7,5},{8,6},{9,7},{10,8},{11,9},{12,... | collective-permute-start | bytes 786440 | tf_op jit(solution)/shard_map/ppermute | solution.py:21
  9.2 0.0 collective-permute-start.1
  9.2 2.5 %collective-permute-start.6 = (f32[2,4,64,128]{3,2,1,0:T(8,128)S(1)}, f32[2,4,64,128]{3,2,1,0:T(8,128)S(1)}, u32[]{:S(2)}, u32[]{:S(2)}) collective-permute-start(f32[2,4,64,128]{3,2,1,0:T(8,128)S(1)} %pad_maximum_fusion), channel_id=1, source_target_pairs={{1,0},{0,1},{3,2},{2,3},{5,4},{4,5},{7,6},{6,7},{9,8},{8,9},{11,10... | collective-permute-start | bytes 786440 | tf_op jit(solution)/shard_map/ppermute | solution.py:26
  11.7 0.0 collective-permute-done
  11.7 0.0 collective-permute-done.3
  11.7 0.9 collective-permute-start.4
  12.7 0.7 slice_bitcast_fusion.4
  13.4 0.2 collective-permute-done.2
  13.6 4.8 %collective-permute-start.7 = (f32[2,4,64,128]{3,2,1,0:T(8,128)S(1)}, f32[2,4,64,128]{3,2,1,0:T(8,128)S(1)}, u32[]{:S(2)}, u32[]{:S(2)}) collective-permute-start(f32[2,4,64,128]{3,2,1,0:T(8,128)S(1)} %collective-permute-done.2), channel_id=1, source_target_pairs={{1,0},{0,1},{3,2},{2,3},{5,4},{4,5},{7,6},{6,7},{9,8},{8,9},{11,10... | collective-permute-start | bytes 786440 | tf_op jit(solution)/shard_map/ppermute | solution.py:26
  18.4 0.7 slice_bitcast_fusion.5
  19.2 1.5 collective-permute-done.1
  20.7 1.6 %collective-permute-start.5 = (f32[2,4,64,128]{3,2,1,0:T(8,128)S(1)}, f32[2,4,64,128]{3,2,1,0:T(8,128)S(1)}, u32[]{:S(2)}, u32[]{:S(2)}) collective-permute-start(f32[2,4,64,128]{3,2,1,0:T(8,128)S(1)} %collective-permute-done.1), channel_id=1, source_target_pairs={{1,0},{0,1},{3,2},{2,3},{5,4},{4,5},{7,6},{6,7},{9,8},{8,9},{11,10... | collective-permute-start | bytes 786440 | tf_op jit(solution)/shard_map/ppermute | solution.py:26
  22.3 0.7 slice_bitcast_fusion.6
  23.0 0.7 slice_bitcast_fusion.7
  23.7 0.0 collective-permute-done.6
  23.7 0.7 slice_bitcast_fusion.1
  24.4 0.0 collective-permute-done.4
  24.4 0.7 slice_bitcast_fusion.3
  25.2 0.0 collective-permute-done.7
  25.2 0.7 slice_bitcast_fusion
  25.9 0.0 collective-permute-done.5
  25.9 0.7 slice_bitcast_fusion.2
  26.6 26.1 %shard_map.59 = (f32[4,64,128]{2,1,0:T(8,128)}, f32[36,64,128]{2,1,0:T(8,128)}) custom-call(s32[1]{0:T(128)} %bitcast.3.parity_ref, f32[4,64,128]{2,1,0:T(8,128)} %bitcast.41, f32[4,64,128]{2,1,0:T(8,128)} %get-tuple-element.31.refs_1_, f32[4,64,128]{2,1,0:T(8,128)} %get-tuple-element.29.refs_2_, f32[4,64,128]{2,1,0:T(8,128)} %get-tuple-element.27.refs_3_, ...), custom_call_target="tpu_custom_call" | custom-call | tf_op jit(solution)/shard_map/pallas_call | solution.py:154
  52.7 3.5 %collective-permute-start.8 = (f32[4,64,128]{2,1,0:T(8,128)}, f32[4,64,128]{2,1,0:T(8,128)S(1)}, u32[]{:S(2)}, u32[]{:S(2)}) collective-permute-start(f32[4,64,128]{2,1,0:T(8,128)} %get-tuple-element.8.own), channel_id=1, source_target_pairs={{0,16},{16,32},{32,48},{48,64},{64,80},{80,96},{96,112},{112,128},... | collective-permute-start | bytes 393224 | tf_op jit(solution)/shard_map/ppermute | solution.py:32
  56.3 1.3 collective-permute-start.9
  57.6 0.6 fusion.1
  58.8 0.7 fusion
  59.5 0.0 collective-permute-done.8.left
  59.5 4.0 %collective-permute-done.9.right = f32[4,64,128]{2,1,0:T(8,128)S(1)} collective-permute-done((f32[4,64,128]{2,1,0:T(8,128)}, f32[4,64,128]{2,1,0:T(8,128)S(1)}, u32[]{:S(2)}, u32[]{:S(2)}) %collective-permute-start.9) | collective-permute-done | bytes 131104 | tf_op jit(solution)/shard_map/ppermute | solution.py:32
  63.5 0.6 copy-done.3
  64.2 2.5 %shard_map.60 = (f32[4,64,128]{2,1,0:T(8,128)}, f32[1,128]{1,0:T(1,128)}) custom-call(s32[1]{0:T(128)S(6)} %convert_element_type.7.scalar_ref, f32[1]{0:T(128)} %bitcast.5.weight_ref, f32[4,64,128]{2,1,0:T(8,128)} %get-tuple-element.8.own, f32[4,64,128]{2,1,0:T(8,128)} %copy-done.2, f32[4,64,128]{2,1,0:T(8,128)} %copy-done.3), custom_call_target="tpu_custom_call" | custom-call | tf_op jit(solution)/shard_map/pallas_call | solution.py:174
  66.7 0.1 collective-permute-start.10
  66.7 2.6 %collective-permute-start.13 = (f32[4,64,128]{2,1,0:T(8,128)}, f32[4,64,128]{2,1,0:T(8,128)S(1)}, u32[]{:S(2)}, u32[]{:S(2)}) collective-permute-start(f32[4,64,128]{2,1,0:T(8,128)} %get-tuple-element.9.refs_0_), channel_id=1, source_target_pairs={{4,0},{5,1},{6,2},{7,3},{8,4},{9,5},{10,6},{11,7},{12,8},{13,9},{1... | collective-permute-start | bytes 393224 | tf_op jit(solution)/shard_map/ppermute | solution.py:21
  69.3 2.8 %collective-permute-start.11 = (f32[4,64,128]{2,1,0:T(8,128)}, f32[4,64,128]{2,1,0:T(8,128)S(1)}, u32[]{:S(2)}, u32[]{:S(2)}) collective-permute-start(f32[4,64,128]{2,1,0:T(8,128)} %get-tuple-element.9.refs_0_), channel_id=1, source_target_pairs={{14,0},{15,1},{0,2},{1,3},{2,4},{3,5},{4,6},{5,7},{6,8},{7,9},{8,1... | collective-permute-start | bytes 393224 | tf_op jit(solution)/shard_map/ppermute | solution.py:21
  72.1 2.3 %collective-permute-start.12 = (f32[4,64,128]{2,1,0:T(8,128)}, f32[4,64,128]{2,1,0:T(8,128)S(1)}, u32[]{:S(2)}, u32[]{:S(2)}) collective-permute-start(f32[4,64,128]{2,1,0:T(8,128)} %get-tuple-element.9.refs_0_), channel_id=1, source_target_pairs={{2,0},{3,1},{4,2},{5,3},{6,4},{7,5},{8,6},{9,7},{10,8},{11,9},{12,... | collective-permute-start | bytes 393224 | tf_op jit(solution)/shard_map/ppermute | solution.py:21
  74.4 2.1 %collective-permute-start.16 = (f32[4,64,128]{2,1,0:T(8,128)}, f32[4,64,128]{2,1,0:T(8,128)S(1)}, u32[]{:S(2)}, u32[]{:S(2)}) collective-permute-start(f32[4,64,128]{2,1,0:T(8,128)} %get-tuple-element.9.refs_0_), channel_id=1, source_target_pairs={{1,0},{0,1},{3,2},{2,3},{5,4},{4,5},{7,6},{6,7},{9,8},{8,9},{11,10... | collective-permute-start | bytes 393224 | tf_op jit(solution)/shard_map/ppermute | solution.py:26
  76.5 0.0 collective-permute-done.10.refs_1_
  76.5 0.0 collective-permute-done.13.refs_4_
  76.5 0.1 collective-permute-start.14
  76.6 0.3 collective-permute-done.11.refs_2_
  77.0 3.5 %collective-permute-start.15 = (f32[4,64,128]{2,1,0:T(8,128)S(1)}, f32[4,64,128]{2,1,0:T(8,128)S(1)}, u32[]{:S(2)}, u32[]{:S(2)}) collective-permute-start(f32[4,64,128]{2,1,0:T(8,128)S(1)} %collective-permute-done.11.refs_2_), channel_id=1, source_target_pairs={{1,0},{0,1},{3,2},{2,3},{5,4},{4,5},{7,6},{6,7},{9,8},{8,9},{11,10... | collective-permute-start | bytes 393224 | tf_op jit(solution)/shard_map/ppermute | solution.py:26
  80.5 0.0 collective-permute-done.12.refs_3_
  80.5 0.3 collective-permute-start.17
  80.8 0.0 collective-permute-done.16.refs_7_
  80.8 0.0 collective-permute-done.14.refs_5_
  80.8 0.7 collective-permute-done.15.refs_6_
  81.5 0.4 collective-permute-done.17.refs_8_
  81.9 0.2 copy-done.10
  82.1 0.4 copy-done.11
  82.5 25.8 %shard_map.61.own = f32[4,64,128]{2,1,0:T(8,128)} custom-call(s32[1]{0:T(128)} %bitcast.3.parity_ref, f32[4,64,128]{2,1,0:T(8,128)} %get-tuple-element.9.refs_0_, f32[4,64,128]{2,1,0:T(8,128)} %copy-done, f32[4,64,128]{2,1,0:T(8,128)} %copy-done.6, f32[4,64,128]{2,1,0:T(8,128)} %copy-done.7, f32[4,64,128]{2,1,0:T(8,128)} %copy-done.1, ...), custom_call_target="tpu_custom_call" | custom-call | tf_op jit(solution)/shard_map/pallas_call | solution.py:165
  108.2 3.5 %collective-permute-start.18 = (f32[4,64,128]{2,1,0:T(8,128)}, f32[4,64,128]{2,1,0:T(8,128)S(1)}, u32[]{:S(2)}, u32[]{:S(2)}) collective-permute-start(f32[4,64,128]{2,1,0:T(8,128)} %shard_map.61.own), channel_id=1, source_target_pairs={{0,16},{16,32},{32,48},{48,64},{64,80},{80,96},{96,112},{112,128},... | collective-permute-start | bytes 393224 | tf_op jit(solution)/shard_map/ppermute | solution.py:32
  111.8 1.3 collective-permute-start.19
  113.7 1.0 collective-permute-done.18.left
  114.7 5.5 %collective-permute-done.19.right = f32[4,64,128]{2,1,0:T(8,128)S(1)} collective-permute-done((f32[4,64,128]{2,1,0:T(8,128)}, f32[4,64,128]{2,1,0:T(8,128)S(1)}, u32[]{:S(2)}, u32[]{:S(2)}) %collective-permute-start.19) | collective-permute-done | bytes 131104 | tf_op jit(solution)/shard_map/ppermute | solution.py:32
  120.2 0.7 copy-done.5
  120.8 2.5 %shard_map.62 = (f32[4,64,128]{2,1,0:T(8,128)}, f32[1,128]{1,0:T(1,128)}) custom-call(s32[1]{0:T(128)S(6)} %convert_element_type.6.scalar_ref, f32[1]{0:T(128)} %bitcast.2.weight_ref, f32[4,64,128]{2,1,0:T(8,128)} %shard_map.61.own, f32[4,64,128]{2,1,0:T(8,128)} %copy-done.4, f32[4,64,128]{2,1,0:T(8,128)} %copy-done.5), custom_call_target="tpu_custom_call" | custom-call | tf_op jit(solution)/shard_map/pallas_call | solution.py:174
  123.4 0.7 pad_maximum_fusion.1
  124.0 0.1 broadcast_in_dim.15
  124.1 28.1 %all_to_all.5.refs_1_ = f32[256,2,128]{2,1,0:T(2,128)} all-to-all(f32[256,2,128]{2,1,0:T(2,128)S(1)} %broadcast_in_dim.15), channel_id=1, replica_groups=mesh['image'=16,'domain'=16] {'image','domain'}, dimensions={0} | all-to-all | bytes 524288 | tf_op jit(solution)/shard_map/all_to_all | solution.py:183
  152.2 1.6 %shard_map.63 = f32[2,1]{1,0:T(2,128)} custom-call(s32[1]{0:T(128)} %bitcast.1.refs_0_, f32[256,2,128]{2,1,0:T(2,128)} %all_to_all.5.refs_1_), custom_call_target="tpu_custom_call" | custom-call | tf_op jit(solution)/shard_map/pallas_call | solution.py:184
  153.8 1.3 copy.6
  (28 shorter events, 0.1 us)
Async XLA Ops:
  1.6 10.0 %collective-permute-start = (f32[2,4,64,128]{3,2,1,0:T(8,128)S(1)}, f32[2,4,64,128]{3,2,1,0:T(8,128)S(1)}, u32[]{:S(2)}, u32[]{:S(2)}) collective-permute-start(f32[2,4,64,128]{3,2,1,0:T(8,128)S(1)} %pad_maximum_fusion), channel_id=1, source_target_pairs={{12,0},{13,1},{14,2},{15,3},{0,4},{1,5},{2,6},{3,7},{4,8},{5,9},{6... | collective-permute-start | bytes 786440 | tf_op jit(solution)/shard_map/ppermute | solution.py:21
  3.8 7.9 %collective-permute-start.3 = (f32[2,4,64,128]{3,2,1,0:T(8,128)S(1)}, f32[2,4,64,128]{3,2,1,0:T(8,128)S(1)}, u32[]{:S(2)}, u32[]{:S(2)}) collective-permute-start(f32[2,4,64,128]{3,2,1,0:T(8,128)S(1)} %pad_maximum_fusion), channel_id=1, source_target_pairs={{4,0},{5,1},{6,2},{7,3},{8,4},{9,5},{10,6},{11,7},{12,8},{13,9},{1... | collective-permute-start | bytes 786440 | tf_op jit(solution)/shard_map/ppermute | solution.py:21
  5.3 8.3 %collective-permute-start.2 = (f32[2,4,64,128]{3,2,1,0:T(8,128)S(1)}, f32[2,4,64,128]{3,2,1,0:T(8,128)S(1)}, u32[]{:S(2)}, u32[]{:S(2)}) collective-permute-start(f32[2,4,64,128]{3,2,1,0:T(8,128)S(1)} %pad_maximum_fusion), channel_id=1, source_target_pairs={{2,0},{3,1},{4,2},{5,3},{6,4},{7,5},{8,6},{9,7},{10,8},{11,9},{12,... | collective-permute-start | bytes 786440 | tf_op jit(solution)/shard_map/ppermute | solution.py:21
  9.2 11.5 %collective-permute-start.1 = (f32[2,4,64,128]{3,2,1,0:T(8,128)S(1)}, f32[2,4,64,128]{3,2,1,0:T(8,128)S(1)}, u32[]{:S(2)}, u32[]{:S(2)}) collective-permute-start(f32[2,4,64,128]{3,2,1,0:T(8,128)S(1)} %pad_maximum_fusion), channel_id=1, source_target_pairs={{14,0},{15,1},{0,2},{1,3},{2,4},{3,5},{4,6},{5,7},{6,8},{7,9},{8,1... | collective-permute-start | bytes 786440 | tf_op jit(solution)/shard_map/ppermute | solution.py:21
  9.2 14.5 %collective-permute-start.6 = (f32[2,4,64,128]{3,2,1,0:T(8,128)S(1)}, f32[2,4,64,128]{3,2,1,0:T(8,128)S(1)}, u32[]{:S(2)}, u32[]{:S(2)}) collective-permute-start(f32[2,4,64,128]{3,2,1,0:T(8,128)S(1)} %pad_maximum_fusion), channel_id=1, source_target_pairs={{1,0},{0,1},{3,2},{2,3},{5,4},{4,5},{7,6},{6,7},{9,8},{8,9},{11,10... | collective-permute-start | bytes 786440 | tf_op jit(solution)/shard_map/ppermute | solution.py:26
  11.7 12.7 %collective-permute-start.4 = (f32[2,4,64,128]{3,2,1,0:T(8,128)S(1)}, f32[2,4,64,128]{3,2,1,0:T(8,128)S(1)}, u32[]{:S(2)}, u32[]{:S(2)}) collective-permute-start(f32[2,4,64,128]{3,2,1,0:T(8,128)S(1)} %broadcast_select_fusion), channel_id=1, source_target_pairs={{1,0},{0,1},{3,2},{2,3},{5,4},{4,5},{7,6},{6,7},{9,8},{8,9},{11,10... | collective-permute-start | bytes 786440 | tf_op jit(solution)/shard_map/ppermute | solution.py:26
  13.6 11.6 %collective-permute-start.7 = (f32[2,4,64,128]{3,2,1,0:T(8,128)S(1)}, f32[2,4,64,128]{3,2,1,0:T(8,128)S(1)}, u32[]{:S(2)}, u32[]{:S(2)}) collective-permute-start(f32[2,4,64,128]{3,2,1,0:T(8,128)S(1)} %collective-permute-done.2), channel_id=1, source_target_pairs={{1,0},{0,1},{3,2},{2,3},{5,4},{4,5},{7,6},{6,7},{9,8},{8,9},{11,10... | collective-permute-start | bytes 786440 | tf_op jit(solution)/shard_map/ppermute | solution.py:26
  20.7 5.2 %collective-permute-start.5 = (f32[2,4,64,128]{3,2,1,0:T(8,128)S(1)}, f32[2,4,64,128]{3,2,1,0:T(8,128)S(1)}, u32[]{:S(2)}, u32[]{:S(2)}) collective-permute-start(f32[2,4,64,128]{3,2,1,0:T(8,128)S(1)} %collective-permute-done.1), channel_id=1, source_target_pairs={{1,0},{0,1},{3,2},{2,3},{5,4},{4,5},{7,6},{6,7},{9,8},{8,9},{11,10... | collective-permute-start | bytes 786440 | tf_op jit(solution)/shard_map/ppermute | solution.py:26
  26.6 31.0 %copy-start.12 = (s32[2,1]{0,1:T(1,128)S(1)}, s32[2,1]{0,1:T(1,128)}, u32[]{:S(2)}) copy-start(s32[2,1]{0,1:T(1,128)} %param.6) | copy-start | bytes 28
  26.6 32.2 %copy-start.13 = (f32[2,1]{0,1:T(1,128)S(1)}, f32[2,1]{0,1:T(1,128)}, u32[]{:S(2)}) copy-start(f32[2,1]{0,1:T(1,128)} %param.7) | copy-start | bytes 28
  52.7 6.8 %collective-permute-start.8 = (f32[4,64,128]{2,1,0:T(8,128)}, f32[4,64,128]{2,1,0:T(8,128)S(1)}, u32[]{:S(2)}, u32[]{:S(2)}) collective-permute-start(f32[4,64,128]{2,1,0:T(8,128)} %get-tuple-element.8.own), channel_id=1, source_target_pairs={{0,16},{16,32},{32,48},{48,64},{64,80},{80,96},{96,112},{112,128},... | collective-permute-start | bytes 393224 | tf_op jit(solution)/shard_map/ppermute | solution.py:32
  56.3 7.2 %collective-permute-start.9 = (f32[4,64,128]{2,1,0:T(8,128)}, f32[4,64,128]{2,1,0:T(8,128)S(1)}, u32[]{:S(2)}, u32[]{:S(2)}) collective-permute-start(f32[4,64,128]{2,1,0:T(8,128)} %get-tuple-element.8.own), channel_id=1, source_target_pairs={{16,0},{32,16},{48,32},{64,48},{80,64},{96,80},{112,96},{128,112},... | collective-permute-start | bytes 393224 | tf_op jit(solution)/shard_map/ppermute | solution.py:32
  59.5 4.0 %copy-start.2 = (f32[4,64,128]{2,1,0:T(8,128)}, f32[4,64,128]{2,1,0:T(8,128)S(1)}, u32[]{:S(2)}) copy-start(f32[4,64,128]{2,1,0:T(8,128)S(1)} %collective-permute-done.8.left) | copy-start | bytes 393220
  63.5 0.6 copy-start.3
  66.7 9.8 %collective-permute-start.10 = (f32[4,64,128]{2,1,0:T(8,128)}, f32[4,64,128]{2,1,0:T(8,128)S(1)}, u32[]{:S(2)}, u32[]{:S(2)}) collective-permute-start(f32[4,64,128]{2,1,0:T(8,128)} %get-tuple-element.9.refs_0_), channel_id=1, source_target_pairs={{12,0},{13,1},{14,2},{15,3},{0,4},{1,5},{2,6},{3,7},{4,8},{5,9},{6... | collective-permute-start | bytes 393224 | tf_op jit(solution)/shard_map/ppermute | solution.py:21
  66.7 9.8 %collective-permute-start.13 = (f32[4,64,128]{2,1,0:T(8,128)}, f32[4,64,128]{2,1,0:T(8,128)S(1)}, u32[]{:S(2)}, u32[]{:S(2)}) collective-permute-start(f32[4,64,128]{2,1,0:T(8,128)} %get-tuple-element.9.refs_0_), channel_id=1, source_target_pairs={{4,0},{5,1},{6,2},{7,3},{8,4},{9,5},{10,6},{11,7},{12,8},{13,9},{1... | collective-permute-start | bytes 393224 | tf_op jit(solution)/shard_map/ppermute | solution.py:21
  69.3 7.6 %collective-permute-start.11 = (f32[4,64,128]{2,1,0:T(8,128)}, f32[4,64,128]{2,1,0:T(8,128)S(1)}, u32[]{:S(2)}, u32[]{:S(2)}) collective-permute-start(f32[4,64,128]{2,1,0:T(8,128)} %get-tuple-element.9.refs_0_), channel_id=1, source_target_pairs={{14,0},{15,1},{0,2},{1,3},{2,4},{3,5},{4,6},{5,7},{6,8},{7,9},{8,1... | collective-permute-start | bytes 393224 | tf_op jit(solution)/shard_map/ppermute | solution.py:21
  72.1 8.4 %collective-permute-start.12 = (f32[4,64,128]{2,1,0:T(8,128)}, f32[4,64,128]{2,1,0:T(8,128)S(1)}, u32[]{:S(2)}, u32[]{:S(2)}) collective-permute-start(f32[4,64,128]{2,1,0:T(8,128)} %get-tuple-element.9.refs_0_), channel_id=1, source_target_pairs={{2,0},{3,1},{4,2},{5,3},{6,4},{7,5},{8,6},{9,7},{10,8},{11,9},{12,... | collective-permute-start | bytes 393224 | tf_op jit(solution)/shard_map/ppermute | solution.py:21
  74.4 6.4 %collective-permute-start.16 = (f32[4,64,128]{2,1,0:T(8,128)}, f32[4,64,128]{2,1,0:T(8,128)S(1)}, u32[]{:S(2)}, u32[]{:S(2)}) collective-permute-start(f32[4,64,128]{2,1,0:T(8,128)} %get-tuple-element.9.refs_0_), channel_id=1, source_target_pairs={{1,0},{0,1},{3,2},{2,3},{5,4},{4,5},{7,6},{6,7},{9,8},{8,9},{11,10... | collective-permute-start | bytes 393224 | tf_op jit(solution)/shard_map/ppermute | solution.py:26
  76.5 5.3 %copy-start = (f32[4,64,128]{2,1,0:T(8,128)}, f32[4,64,128]{2,1,0:T(8,128)S(1)}, u32[]{:S(2)}) copy-start(f32[4,64,128]{2,1,0:T(8,128)S(1)} %collective-permute-done.10.refs_1_) | copy-start | bytes 393220
  76.5 5.3 %copy-start.1 = (f32[4,64,128]{2,1,0:T(8,128)}, f32[4,64,128]{2,1,0:T(8,128)S(1)}, u32[]{:S(2)}) copy-start(f32[4,64,128]{2,1,0:T(8,128)S(1)} %collective-permute-done.13.refs_4_) | copy-start | bytes 393220
  76.5 4.2 %collective-permute-start.14 = (f32[4,64,128]{2,1,0:T(8,128)S(1)}, f32[4,64,128]{2,1,0:T(8,128)S(1)}, u32[]{:S(2)}, u32[]{:S(2)}) collective-permute-start(f32[4,64,128]{2,1,0:T(8,128)S(1)} %broadcast_select_fusion.1), channel_id=1, source_target_pairs={{1,0},{0,1},{3,2},{2,3},{5,4},{4,5},{7,6},{6,7},{9,8},{8,9},{11,10... | collective-permute-start | bytes 393224 | tf_op jit(solution)/shard_map/ppermute | solution.py:26
  77.0 4.9 %copy-start.6 = (f32[4,64,128]{2,1,0:T(8,128)}, f32[4,64,128]{2,1,0:T(8,128)S(1)}, u32[]{:S(2)}) copy-start(f32[4,64,128]{2,1,0:T(8,128)S(1)} %collective-permute-done.11.refs_2_) | copy-start | bytes 393220
  77.0 4.5 %collective-permute-start.15 = (f32[4,64,128]{2,1,0:T(8,128)S(1)}, f32[4,64,128]{2,1,0:T(8,128)S(1)}, u32[]{:S(2)}, u32[]{:S(2)}) collective-permute-start(f32[4,64,128]{2,1,0:T(8,128)S(1)} %collective-permute-done.11.refs_2_), channel_id=1, source_target_pairs={{1,0},{0,1},{3,2},{2,3},{5,4},{4,5},{7,6},{6,7},{9,8},{8,9},{11,10... | collective-permute-start | bytes 393224 | tf_op jit(solution)/shard_map/ppermute | solution.py:26
  80.5 1.4 copy-start.7
  80.5 1.3 collective-permute-start.17
  80.8 1.1 copy-start.8
  80.8 1.1 copy-start.9
  81.5 0.7 copy-start.10
  81.8 0.7 copy-start.11
  82.5 40.9 %copy-start.14 = (f32[1,128]{1,0:T(1,128)S(1)}, f32[1,128]{1,0:T(1,128)}, u32[]{:S(2)}) copy-start(f32[1,128]{1,0:T(1,128)} %get-tuple-element.12) | copy-start | bytes 1540
  108.2 6.4 %collective-permute-start.18 = (f32[4,64,128]{2,1,0:T(8,128)}, f32[4,64,128]{2,1,0:T(8,128)S(1)}, u32[]{:S(2)}, u32[]{:S(2)}) collective-permute-start(f32[4,64,128]{2,1,0:T(8,128)} %shard_map.61.own), channel_id=1, source_target_pairs={{0,16},{16,32},{32,48},{48,64},{64,80},{80,96},{96,112},{112,128},... | collective-permute-start | bytes 393224 | tf_op jit(solution)/shard_map/ppermute | solution.py:32
  111.8 8.4 %collective-permute-start.19 = (f32[4,64,128]{2,1,0:T(8,128)}, f32[4,64,128]{2,1,0:T(8,128)S(1)}, u32[]{:S(2)}, u32[]{:S(2)}) collective-permute-start(f32[4,64,128]{2,1,0:T(8,128)} %shard_map.61.own), channel_id=1, source_target_pairs={{16,0},{32,16},{48,32},{64,48},{80,64},{96,80},{112,96},{128,112},... | collective-permute-start | bytes 393224 | tf_op jit(solution)/shard_map/ppermute | solution.py:32
  114.7 5.5 %copy-start.4 = (f32[4,64,128]{2,1,0:T(8,128)}, f32[4,64,128]{2,1,0:T(8,128)S(1)}, u32[]{:S(2)}) copy-start(f32[4,64,128]{2,1,0:T(8,128)S(1)} %collective-permute-done.18.left) | copy-start | bytes 393220
  120.2 0.7 copy-start.5
where the time goes:
time: 156 us; the launch traced here: 155 us
  Pallas kernels  58.6 us (38%)
  starting transfers between devices  40.8 us (26%)
  blocking collectives  28.1 us (18%)
  waiting for transfers between devices  13.6 us (9%)
  local copies, waits for them, and re-layouts  10.3 us (7%)
  between operations  2.01 us (1%)
  other arithmetic  1.7 us (1%)
    all_to_all x1, blocking collectives, per_device(): gaps = lax.all_to_all(everyone, ('image', 'domain'), 0, 0)  28.1 us
    pallas_call x1, Pallas kernels, per_device(): pl.pallas_call(first_kernel, out_shape=(plane, jax.ShapeDtypeStruct(wide,...  26.1 us
    pallas_call x1, Pallas kernels, per_device(): pl.pallas_call(later_kernel, out_shape=plane, in_specs=[SMEM] + [VMEM] *...  25.8 us
    ppermute x8, starting transfers between devices, partnered(): return lax.ppermute(value, 'domain', [(i ^ 1, i) for i in range(size)])  15.8 us
    ppermute x8, starting transfers between devices, fetched(): lax.ppermute(value, 'domain', [((i + offset) % size, i) for i in range(si...  15.3 us
    ppermute x4, waiting for transfers between devices, passed_along(): lax.ppermute(value, 'image', [(i, i + steps) for i in range(first, last)])  10.5 us
    ppermute x4, starting transfers between devices, passed_along(): lax.ppermute(value, 'image', [(i, i + steps) for i in range(first, last)])  9.66 us
    squeeze x8, local copies, waits for them, and re-layouts, per_device(): piece[1]  5.75 us
  transfers between devices with their start and end apart: 20, of which 8 were waited for; matrix products, arithmetic and copies ran while one was open for 4% of the time, Pallas kernels for 0%

commit v1 on v0

v1 whole, which is shorter than its diff:
```python
import jax
import jax.numpy as jnp
from jax import lax
from jax.experimental import pallas as pl
from jax.experimental.pallas import tpu as pltpu
from jax.sharding import PartitionSpec as P

STEPS = 8
CYCLES = 2
SUBLANES = 8
UNROLL = 4

stiffness = 1.0
time_step = 0.008
epsilon = 1e-06

VMEM = pl.BlockSpec(memory_space=pltpu.VMEM)
SMEM = pl.BlockSpec(memory_space=pltpu.SMEM)
PARAMS = pltpu.CompilerParams(vmem_limit_bytes=16 << 20)


def fetched(value, offset):
    size = lax.axis_size("domain")
    return lax.ppermute(value, "domain", [((i + offset) % size, i) for i in range(size)])


def partnered(value):
    size = lax.axis_size("domain")
    return lax.ppermute(value, "domain", [(i ^ 1, i) for i in range(size)])


def passed_along(value, steps):
    count = lax.axis_size("image")
    first, last = (max(0, -steps), min(count, count - steps))
    return lax.ppermute(value, "image", [(i, i + steps) for i in range(first, last)])


def halo_pieces(own, parity):
    after2, before2 = fetched(own, 2), fetched(own, -2)
    after4, before4 = fetched(own, 4), fetched(own, -4)
    chosen = jnp.where(parity == 0, after4, before4)
    return [own, before4, before2, after2, after4] + [
        partnered(piece) for piece in (chosen, before2, own, after2)
    ]


def fill(window, parity, pieces, rows):
    own, before4, before2, after2, after4, *others = pieces
    for place, piece in ((0, before4), (2, before2), (4, own), (6, after2), (8, after4)):
        window[pl.ds(place * rows, rows)] = piece[...]

    @pl.when(parity == 0)
    def _():
        for place, piece in zip((1, 3, 5, 7), others):
            window[pl.ds(place * rows, rows)] = piece[...]

    @pl.when(parity != 0)
    def _():
        for place, piece in zip((7, 1, 3, 5), others):
            window[pl.ds(place * rows, rows)] = piece[...]


def folded(source, row, target, place):
    folds = target.shape[-3]
    for v in range(folds):
        target[(*place, v)] = source[row, pl.ds(v, SUBLANES, stride=folds), :]


def y_shifted(value, offset):
    if offset == 1:
        return jnp.concatenate([pltpu.roll(value[-1:], 1, 1), value[:-1]], axis=0)
    return jnp.concatenate([value[1:], pltpu.roll(value[:1], SUBLANES - 1, 1)], axis=0)


def z_shifted(value, offset):
    return pltpu.roll(value, offset % value.shape[2], 2)


def potential_and_motion(field, mobile, row):
    here = field[row]
    square = here * here
    around = field[row - 1] + field[row + 1]
    for shifted in (y_shifted, z_shifted):
        around = around + (shifted(here, 1) + shifted(here, -1))
    potential = here * (square + 5.0) - around
    motion = mobile[row] / (1.0 + square)
    return potential, motion


def take_steps(field, mobile, length):
    for step in range(STEPS):
        first, last = 2 * step + 2, length - 2 * step - 2
        before = potential_and_motion(field, mobile, first - 1)
        now = potential_and_motion(field, mobile, first)
        inflow = (before[1] + now[1]) * (now[0] - before[0])

        def one_row(row, carried):
            potential, motion, inflow = carried
            ahead = potential_and_motion(field, mobile, row + 1)
            outflow = (motion + ahead[1]) * (ahead[0] - potential)
            change = outflow - inflow
            for shifted in (y_shifted, z_shifted):
                flow = (motion + shifted(motion, 1)) * (potential - shifted(potential, 1))
                change = change + (shifted(flow, -1) - flow)
            field[row] = field[row] + change
            return ahead[0], ahead[1], outflow

        lax.fori_loop(first, last, one_row, (now[0], now[1], inflow), unroll=UNROLL)


def pack_kernel(field, mobility, out):
    for row in range(field.shape[0]):
        folded(field, row, out, (0, row))
        folded(mobility, row, out, (1, row))
    out[1] = out[1] * (0.5 * time_step)


def first_kernel(parity_ref, *refs):
    pieces, out, mobile, window = refs[:9], *refs[9:]
    rows = out.shape[0]
    fill(window, parity_ref[0], [piece.at[0] for piece in pieces], rows)
    fill(mobile, parity_ref[0], [piece.at[1] for piece in pieces], rows)
    take_steps(window, mobile, 9 * rows)
    out[...] = window[pl.ds(4 * rows, rows)]


def later_kernel(parity_ref, *refs):
    pieces, mobile, out, window = refs[:9], *refs[9:]
    rows = out.shape[0]
    fill(window, parity_ref[0], pieces, rows)
    take_steps(window, mobile, 9 * rows)
    out[...] = window[pl.ds(4 * rows, rows)]


def mix_kernel(cycle, index_ref, lower_ref, weight_ref, own, left, right, *refs):
    earlier, (out, total) = refs[:-2], refs[-2:]
    weight = weight_ref[cycle, 0]
    from_left = lower_ref[cycle, 0] < index_ref[0]
    squares = jnp.square(right[...] - own[...])
    total[cycle : cycle + 1] = jnp.sum(squares, axis=(0, 1, 2))[None]
    for there in earlier:
        total[:cycle] = there[:cycle]

    def write(first, second):
        for row in range(own.shape[0]):
            mixed = weight * first[row] + (1.0 - weight) * second[row]
            if out.shape == own.shape:
                out[row] = mixed
            else:
                folds = mixed.shape[0]
                for v in range(folds):
                    out[row, pl.ds(v, SUBLANES, stride=folds), :] = mixed[v]

    @pl.when(from_left)
    def _():
        write(left, own)

    @pl.when(jnp.logical_not(from_left))
    def _():
        write(own, right)


def length_kernel(cells, images, index_ref, gaps, out):
    each = jnp.sum(gaps[...].reshape(images, -1, CYCLES, 128), axis=1)
    distance = jnp.sqrt(jnp.sum(each, axis=-1, keepdims=True) / cells + epsilon)
    position = lax.broadcasted_iota(jnp.int32, distance.shape, 0)
    kept = jnp.where(position < index_ref[0], distance, 0.0)
    out[...] = jnp.sum(kept, axis=0)


def shaped(*shape):
    return jax.ShapeDtypeStruct(shape, jnp.float32)


def per_device(field, mobility, lower, weights):
    rows, depth, lanes = field.shape[1:]
    slab = (rows, depth // SUBLANES, SUBLANES, lanes)
    wide = (9 * rows,) + slab[1:]
    window = pltpu.VMEM(wide, jnp.float32)
    image_count, domain_count = lax.axis_size("image"), lax.axis_size("domain")
    image_index = lax.axis_index("image")[None]
    parity = lax.rem(lax.axis_index("domain"), 2)
    parities = parity[None]
    cells = rows * domain_count * depth * lanes

    packed = pl.pallas_call(
        pack_kernel,
        out_shape=shaped(2, *slab),
        in_specs=[VMEM] * 2,
        out_specs=VMEM,
        compiler_params=PARAMS,
    )(field[0], mobility)
    phase, mobile = pl.pallas_call(
        first_kernel,
        out_shape=(shaped(*slab), shaped(*wide)),
        in_specs=[SMEM] + [VMEM] * 9,
        out_specs=(VMEM, VMEM),
        scratch_shapes=[window],
        compiler_params=PARAMS,
    )(parities, *halo_pieces(packed, parity))

    totals = []
    for cycle in range(CYCLES):
        if cycle:
            phase = pl.pallas_call(
                later_kernel,
                out_shape=shaped(*slab),
                in_specs=[SMEM] + [VMEM] * 10,
                out_specs=VMEM,
                scratch_shapes=[window],
                compiler_params=PARAMS,
            )(parities, *halo_pieces(phase, parity), mobile)
        left, right = passed_along(phase, 1), passed_along(phase, -1)
        after = slab if cycle < CYCLES - 1 else (rows, depth, lanes)
        phase, total = pl.pallas_call(
            lambda *refs, cycle=cycle: mix_kernel(cycle, *refs),
            out_shape=(shaped(*after), shaped(CYCLES, lanes)),
            in_specs=[SMEM] * 3 + [VMEM] * (3 + len(totals)),
            out_specs=(VMEM, VMEM),
            compiler_params=PARAMS,
        )(image_index, lower, weights, phase, left, right, *totals)
        totals = [total]
    everyone = jnp.broadcast_to(totals[0][None], (image_count * domain_count, CYCLES, lanes))
    gaps = lax.all_to_all(everyone, ("image", "domain"), 0, 0)
    arclength = pl.pallas_call(
        lambda *refs: length_kernel(cells, image_count, *refs),
        out_shape=shaped(CYCLES, 1),
        in_specs=[SMEM, VMEM],
        out_specs=VMEM,
        compiler_params=PARAMS,
    )(image_index, gaps)
    return phase[None], arclength


def solution(mesh):
    return jax.shard_map(
        per_device,
        mesh=mesh,
        in_specs=(
            P("image", "domain", None, None),
            P("domain", None, None),
            P(None, "image"),
            P(None, "image"),
        ),
        out_specs=(P("image", "domain", None, None), P(None, "image")),
        check_vma=False,
    )
```

time: 156 us -> 116 us (0.74)
  Pallas kernels: 58.6 us -> 26.8 us
  local copies, waits for them, and re-layouts: 10.3 us -> 2.66 us
  starting transfers between devices: 40.8 us -> 43 us
  other arithmetic: 1.7 us -> 0.04 us
    pallas_call x4 -> x5, Pallas kernels: 56.9 us -> 26.6 us  [the longest x1 12.4 us: per_device(): pl.pallas_call(first_kernel, out_shape=(shaped(*slab), shaped(*wide)), in...]
    squeeze x8 -> x0, local copies, waits for them, and re-layouts: 5.75 us -> none  [per_device(): piece[1]]
    ppermute x8, waiting for transfers between devices: 2.08 us -> 0.02 us  [fetched(): lax.ppermute(value, 'domain', [((i + offset) % size, i) for i in range(si...]
    ppermute x4, waiting for transfers between devices: 10.5 us -> 12.1 us  [passed_along(): lax.ppermute(value, 'image', [(i, i + steps) for i in range(first, last)])]
    unnamed x31 -> x11, local copies, waits for them, and re-layouts: 3.22 us -> 2.59 us
  transfers between devices with their start and end apart: 20 -> 20, of which waited for: 8 -> 8; matrix products, arithmetic and copies ran while one was open for 4% -> 0% of each run, Pallas kernels for 0% -> 0%
where the time goes in v1:
time: 116 us
  starting transfers between devices  43 us (37%)
  blocking collectives  27.8 us (24%)
  Pallas kernels  26.8 us (23%)
  waiting for transfers between devices  14.6 us (13%)
  local copies, waits for them, and re-layouts  2.66 us (2%)
    all_to_all x1, blocking collectives, per_device(): gaps = lax.all_to_all(everyone, ('image', 'domain'), 0, 0)  27.8 us
    ppermute x8, starting transfers between devices, fetched(): lax.ppermute(value, 'domain', [((i + offset) % size, i) for i in range(si...  16.7 us
    ppermute x8, starting transfers between devices, partnered(): return lax.ppermute(value, 'domain', [(i ^ 1, i) for i in range(size)])  16.6 us
    pallas_call x1, Pallas kernels, per_device(): pl.pallas_call(first_kernel, out_shape=(shaped(*slab), shaped(*wide)), in...  12.4 us
    pallas_call x1, Pallas kernels, per_device(): pl.pallas_call(later_kernel, out_shape=shaped(*slab), in_specs=[SMEM] + [...  12.3 us
    ppermute x4, waiting for transfers between devices, passed_along(): lax.ppermute(value, 'image', [(i, i + steps) for i in range(first, last)])  12.1 us
    ppermute x4, starting transfers between devices, passed_along(): lax.ppermute(value, 'image', [(i, i + steps) for i in range(first, last)])  9.68 us
    unnamed x11, local copies, waits for them, and re-layouts  2.59 us
  transfers between devices with their start and end apart: 20, of which 8 were waited for; matrix products, arithmetic and copies ran while one was open for 0% of the time, Pallas kernels for 0%

profile of v1, /device:TPU:1, one launch (start us, length us, event | category | flops | bytes accessed | tf_op | source)
XLA Modules:
  0.0 115.6 jit_solution(13506768151776627739)
XLA Ops:
  0.6 0.0 copy-start
  0.6 0.9 copy-done
  1.5 0.0 copy-start.1
  1.5 0.9 copy-done.1
  2.4 0.1 shard_map.59.refs_0_
  2.5 2.2 %collective-permute-start = (f32[2,4,8,8,128]{4,3,2,1,0:T(8,128)S(1)}, f32[2,4,8,8,128]{4,3,2,1,0:T(8,128)S(1)}, u32[]{:S(2)}, u32[]{:S(2)}) collective-permute-start(f32[2,4,8,8,128]{4,3,2,1,0:T(8,128)S(1)} %shard_map.59.refs_0_), channel_id=1, source_target_pairs={{12,0},{13,1},{14,2},{15,3},{0,4},{1,5},{2,6},{3,7},{4,8},{5,9},{6... | collective-permute-start | bytes 786440 | tf_op jit(solution)/shard_map/ppermute | solution.py:24
  4.7 1.5 %collective-permute-start.3 = (f32[2,4,8,8,128]{4,3,2,1,0:T(8,128)S(1)}, f32[2,4,8,8,128]{4,3,2,1,0:T(8,128)S(1)}, u32[]{:S(2)}, u32[]{:S(2)}) collective-permute-start(f32[2,4,8,8,128]{4,3,2,1,0:T(8,128)S(1)} %shard_map.59.refs_0_), channel_id=1, source_target_pairs={{4,0},{5,1},{6,2},{7,3},{8,4},{9,5},{10,6},{11,7},{12,8},{13,9},{1... | collective-permute-start | bytes 786440 | tf_op jit(solution)/shard_map/ppermute | solution.py:24
  6.2 2.7 %collective-permute-start.1 = (f32[2,4,8,8,128]{4,3,2,1,0:T(8,128)S(1)}, f32[2,4,8,8,128]{4,3,2,1,0:T(8,128)S(1)}, u32[]{:S(2)}, u32[]{:S(2)}) collective-permute-start(f32[2,4,8,8,128]{4,3,2,1,0:T(8,128)S(1)} %shard_map.59.refs_0_), channel_id=1, source_target_pairs={{14,0},{15,1},{0,2},{1,3},{2,4},{3,5},{4,6},{5,7},{6,8},{7,9},{8,1... | collective-permute-start | bytes 786440 | tf_op jit(solution)/shard_map/ppermute | solution.py:24
  9.0 2.3 %collective-permute-start.2 = (f32[2,4,8,8,128]{4,3,2,1,0:T(8,128)S(1)}, f32[2,4,8,8,128]{4,3,2,1,0:T(8,128)S(1)}, u32[]{:S(2)}, u32[]{:S(2)}) collective-permute-start(f32[2,4,8,8,128]{4,3,2,1,0:T(8,128)S(1)} %shard_map.59.refs_0_), channel_id=1, source_target_pairs={{2,0},{3,1},{4,2},{5,3},{6,4},{7,5},{8,6},{9,7},{10,8},{11,9},{12,... | collective-permute-start | bytes 786440 | tf_op jit(solution)/shard_map/ppermute | solution.py:24
  11.3 3.4 %collective-permute-start.6 = (f32[2,4,8,8,128]{4,3,2,1,0:T(8,128)S(1)}, f32[2,4,8,8,128]{4,3,2,1,0:T(8,128)S(1)}, u32[]{:S(2)}, u32[]{:S(2)}) collective-permute-start(f32[2,4,8,8,128]{4,3,2,1,0:T(8,128)S(1)} %shard_map.59.refs_0_), channel_id=1, source_target_pairs={{1,0},{0,1},{3,2},{2,3},{5,4},{4,5},{7,6},{6,7},{9,8},{8,9},{11,10... | collective-permute-start | bytes 786440 | tf_op jit(solution)/shard_map/ppermute | solution.py:29
  14.7 0.0 collective-permute-done.refs_1_
  14.7 0.0 collective-permute-done.3.refs_4_
  14.7 1.9 %collective-permute-start.4 = (f32[2,4,8,8,128]{4,3,2,1,0:T(8,128)S(1)}, f32[2,4,8,8,128]{4,3,2,1,0:T(8,128)S(1)}, u32[]{:S(2)}, u32[]{:S(2)}) collective-permute-start(f32[2,4,8,8,128]{4,3,2,1,0:T(8,128)S(1)} %broadcast_select_fusion), channel_id=1, source_target_pairs={{1,0},{0,1},{3,2},{2,3},{5,4},{4,5},{7,6},{6,7},{9,8},{8,9},{11,10... | collective-permute-start | bytes 786440 | tf_op jit(solution)/shard_map/ppermute | solution.py:29
  16.6 0.0 collective-permute-done.1.refs_2_
  16.6 4.8 %collective-permute-start.5 = (f32[2,4,8,8,128]{4,3,2,1,0:T(8,128)S(1)}, f32[2,4,8,8,128]{4,3,2,1,0:T(8,128)S(1)}, u32[]{:S(2)}, u32[]{:S(2)}) collective-permute-start(f32[2,4,8,8,128]{4,3,2,1,0:T(8,128)S(1)} %collective-permute-done.1.refs_2_), channel_id=1, source_target_pairs={{1,0},{0,1},{3,2},{2,3},{5,4},{4,5},{7,6},{6,7},{9,8},{8,9},{11,10... | collective-permute-start | bytes 786440 | tf_op jit(solution)/shard_map/ppermute | solution.py:29
  21.4 0.0 collective-permute-done.2.refs_3_
  21.4 0.5 collective-permute-start.7
  21.9 0.0 collective-permute-done.6.refs_7_
  21.9 0.0 collective-permute-done.4.refs_5_
  21.9 0.7 collective-permute-done.5.refs_6_
  22.6 0.5 collective-permute-done.7.refs_8_
  23.0 0.0 copy-start.2
  23.0 0.0 copy-start.3
  23.0 12.4 %shard_map.60 = (f32[4,8,8,128]{3,2,1,0:T(8,128)S(1)}, f32[36,8,8,128]{3,2,1,0:T(8,128)S(1)}) custom-call(s32[1]{0:T(128)} %bitcast.1.parity_ref, f32[2,4,8,8,128]{4,3,2,1,0:T(8,128)S(1)} %shard_map.59.refs_0_, f32[2,4,8,8,128]{4,3,2,1,0:T(8,128)S(1)} %collective-permute-done.refs_1_, f32[2,4,8,8,128]{4,3,2,1,0:T(8,128)S(1)} %collective-permute-done.1.refs_2_, ...), custom_call_target="tpu_custom_call" | custom-call | tf_op jit(solution)/shard_map/pallas_call | solution.py:193
  35.4 3.5 %collective-permute-start.8 = (f32[4,8,8,128]{3,2,1,0:T(8,128)S(1)}, f32[4,8,8,128]{3,2,1,0:T(8,128)S(1)}, u32[]{:S(2)}, u32[]{:S(2)}) collective-permute-start(f32[4,8,8,128]{3,2,1,0:T(8,128)S(1)} %get-tuple-element.8.refs_3_), channel_id=1, source_target_pairs={{0,16},{16,32},{32,48},{48,64},{64,80},{80,96},{96,112},{112,128},... | collective-permute-start | bytes 393224 | tf_op jit(solution)/shard_map/ppermute | solution.py:35
  39.0 1.3 %collective-permute-start.9 = (f32[4,8,8,128]{3,2,1,0:T(8,128)S(1)}, f32[4,8,8,128]{3,2,1,0:T(8,128)S(1)}, u32[]{:S(2)}, u32[]{:S(2)}) collective-permute-start(f32[4,8,8,128]{3,2,1,0:T(8,128)S(1)} %get-tuple-element.8.refs_3_), channel_id=1, source_target_pairs={{16,0},{32,16},{48,32},{64,48},{80,64},{96,80},{112,96},{128,112},... | collective-permute-start | bytes 393224 | tf_op jit(solution)/shard_map/ppermute | solution.py:35
  40.3 0.0 copy-done.2
  40.3 0.1 copy.8.refs_1_
  40.4 0.0 copy-done.3
  40.4 0.1 copy.9.refs_2_
  40.5 0.9 collective-permute-done.8.refs_4_
  41.4 4.2 %collective-permute-done.9.refs_5_ = f32[4,8,8,128]{3,2,1,0:T(8,128)S(1)} collective-permute-done((f32[4,8,8,128]{3,2,1,0:T(8,128)S(1)}, f32[4,8,8,128]{3,2,1,0:T(8,128)S(1)}, u32[]{:S(2)}, u32[]{:S(2)}) %collective-permute-start.9) | collective-permute-done | bytes 131104 | tf_op jit(solution)/shard_map/ppermute | solution.py:35
  45.6 0.6 shard_map.61
  46.2 1.3 %collective-permute-start.10 = (f32[4,8,8,128]{3,2,1,0:T(8,128)S(1)}, f32[4,8,8,128]{3,2,1,0:T(8,128)S(1)}, u32[]{:S(2)}, u32[]{:S(2)}) collective-permute-start(f32[4,8,8,128]{3,2,1,0:T(8,128)S(1)} %get-tuple-element.9.refs_0_), channel_id=1, source_target_pairs={{12,0},{13,1},{14,2},{15,3},{0,4},{1,5},{2,6},{3,7},{4,8},{5,9},{6... | collective-permute-start | bytes 393224 | tf_op jit(solution)/shard_map/ppermute | solution.py:24
  47.5 1.5 %collective-permute-start.13 = (f32[4,8,8,128]{3,2,1,0:T(8,128)S(1)}, f32[4,8,8,128]{3,2,1,0:T(8,128)S(1)}, u32[]{:S(2)}, u32[]{:S(2)}) collective-permute-start(f32[4,8,8,128]{3,2,1,0:T(8,128)S(1)} %get-tuple-element.9.refs_0_), channel_id=1, source_target_pairs={{4,0},{5,1},{6,2},{7,3},{8,4},{9,5},{10,6},{11,7},{12,8},{13,9},{1... | collective-permute-start | bytes 393224 | tf_op jit(solution)/shard_map/ppermute | solution.py:24
  49.0 2.7 %collective-permute-start.11 = (f32[4,8,8,128]{3,2,1,0:T(8,128)S(1)}, f32[4,8,8,128]{3,2,1,0:T(8,128)S(1)}, u32[]{:S(2)}, u32[]{:S(2)}) collective-permute-start(f32[4,8,8,128]{3,2,1,0:T(8,128)S(1)} %get-tuple-element.9.refs_0_), channel_id=1, source_target_pairs={{14,0},{15,1},{0,2},{1,3},{2,4},{3,5},{4,6},{5,7},{6,8},{7,9},{8,1... | collective-permute-start | bytes 393224 | tf_op jit(solution)/shard_map/ppermute | solution.py:24
  51.7 2.4 %collective-permute-start.12 = (f32[4,8,8,128]{3,2,1,0:T(8,128)S(1)}, f32[4,8,8,128]{3,2,1,0:T(8,128)S(1)}, u32[]{:S(2)}, u32[]{:S(2)}) collective-permute-start(f32[4,8,8,128]{3,2,1,0:T(8,128)S(1)} %get-tuple-element.9.refs_0_), channel_id=1, source_target_pairs={{2,0},{3,1},{4,2},{5,3},{6,4},{7,5},{8,6},{9,7},{10,8},{11,9},{12,... | collective-permute-start | bytes 393224 | tf_op jit(solution)/shard_map/ppermute | solution.py:24
  54.1 2.4 %collective-permute-start.16 = (f32[4,8,8,128]{3,2,1,0:T(8,128)S(1)}, f32[4,8,8,128]{3,2,1,0:T(8,128)S(1)}, u32[]{:S(2)}, u32[]{:S(2)}) collective-permute-start(f32[4,8,8,128]{3,2,1,0:T(8,128)S(1)} %get-tuple-element.9.refs_0_), channel_id=1, source_target_pairs={{1,0},{0,1},{3,2},{2,3},{5,4},{4,5},{7,6},{6,7},{9,8},{8,9},{11,10... | collective-permute-start | bytes 393224 | tf_op jit(solution)/shard_map/ppermute | solution.py:29
  56.5 0.0 collective-permute-done.10.refs_1_
  56.5 0.0 collective-permute-done.13.refs_4_
  56.6 0.3 collective-permute-start.14
  56.8 0.0 collective-permute-done.11.refs_2_
  56.9 3.4 %collective-permute-start.15 = (f32[4,8,8,128]{3,2,1,0:T(8,128)S(1)}, f32[4,8,8,128]{3,2,1,0:T(8,128)S(1)}, u32[]{:S(2)}, u32[]{:S(2)}) collective-permute-start(f32[4,8,8,128]{3,2,1,0:T(8,128)S(1)} %collective-permute-done.11.refs_2_), channel_id=1, source_target_pairs={{1,0},{0,1},{3,2},{2,3},{5,4},{4,5},{7,6},{6,7},{9,8},{8,9},{11,10... | collective-permute-start | bytes 393224 | tf_op jit(solution)/shard_map/ppermute | solution.py:29
  60.2 0.0 collective-permute-done.12.refs_3_
  60.2 0.0 collective-permute-start.17
  60.3 0.0 collective-permute-done.16.refs_7_
  60.3 0.0 collective-permute-done.14.refs_5_
  60.3 1.0 collective-permute-done.15.refs_6_
  61.2 0.4 collective-permute-done.17.refs_8_
  61.6 12.3 %shard_map.62.refs_3_ = f32[4,8,8,128]{3,2,1,0:T(8,128)S(1)} custom-call(s32[1]{0:T(128)} %bitcast.1.parity_ref, f32[4,8,8,128]{3,2,1,0:T(8,128)S(1)} %get-tuple-element.9.refs_0_, f32[4,8,8,128]{3,2,1,0:T(8,128)S(1)} %collective-permute-done.10.refs_1_, f32[4,8,8,128]{3,2,1,0:T(8,128)S(1)} %collective-permute-done.11.refs_2_, ...), custom_call_target="tpu_custom_call" | custom-call | tf_op jit(solution)/shard_map/pallas_call | solution.py:205
  73.9 3.5 %collective-permute-start.18 = (f32[4,8,8,128]{3,2,1,0:T(8,128)S(1)}, f32[4,8,8,128]{3,2,1,0:T(8,128)S(1)}, u32[]{:S(2)}, u32[]{:S(2)}) collective-permute-start(f32[4,8,8,128]{3,2,1,0:T(8,128)S(1)} %shard_map.62.refs_3_), channel_id=1, source_target_pairs={{0,16},{16,32},{32,48},{48,64},{64,80},{80,96},{96,112},{112,128},... | collective-permute-start | bytes 393224 | tf_op jit(solution)/shard_map/ppermute | solution.py:35
  77.4 1.3 %collective-permute-start.19 = (f32[4,8,8,128]{3,2,1,0:T(8,128)S(1)}, f32[4,8,8,128]{3,2,1,0:T(8,128)S(1)}, u32[]{:S(2)}, u32[]{:S(2)}) collective-permute-start(f32[4,8,8,128]{3,2,1,0:T(8,128)S(1)} %shard_map.62.refs_3_), channel_id=1, source_target_pairs={{16,0},{32,16},{48,32},{64,48},{80,64},{96,80},{112,96},{128,112},... | collective-permute-start | bytes 393224 | tf_op jit(solution)/shard_map/ppermute | solution.py:35
  78.7 1.3 %collective-permute-done.18.refs_4_ = f32[4,8,8,128]{3,2,1,0:T(8,128)S(1)} collective-permute-done((f32[4,8,8,128]{3,2,1,0:T(8,128)S(1)}, f32[4,8,8,128]{3,2,1,0:T(8,128)S(1)}, u32[]{:S(2)}, u32[]{:S(2)}) %collective-permute-start.18) | collective-permute-done | bytes 131104 | tf_op jit(solution)/shard_map/ppermute | solution.py:35
  80.1 5.6 %collective-permute-done.19.refs_5_ = f32[4,8,8,128]{3,2,1,0:T(8,128)S(1)} collective-permute-done((f32[4,8,8,128]{3,2,1,0:T(8,128)S(1)}, f32[4,8,8,128]{3,2,1,0:T(8,128)S(1)}, u32[]{:S(2)}, u32[]{:S(2)}) %collective-permute-start.19) | collective-permute-done | bytes 131104 | tf_op jit(solution)/shard_map/ppermute | solution.py:35
  85.7 1.3 %shard_map.63 = (f32[4,64,128]{2,1,0:T(8,128)}, f32[2,128]{1,0:T(2,128)S(1)}) custom-call(s32[1]{0:T(128)} %bitcast.refs_0_, s32[2,1]{1,0:T(2,128)S(1)} %copy.8.refs_1_, f32[2,1]{1,0:T(2,128)S(1)} %copy.9.refs_2_, f32[4,8,8,128]{3,2,1,0:T(8,128)S(1)} %shard_map.62.refs_3_, f32[4,8,8,128]{3,2,1,0:T(8,128)S(1)} %collective-permute-done.18.refs_4_, ...), custom_call_target="tpu_custom_call" | custom-call | tf_op jit(solution)/shard_map/pallas_call | solution.py:215
  87.0 0.1 broadcast_in_dim.18
  87.1 27.8 %all_to_all.5.refs_1_ = f32[256,2,128]{2,1,0:T(2,128)S(1)} all-to-all(f32[256,2,128]{2,1,0:T(2,128)S(1)} %broadcast_in_dim.18), channel_id=1, replica_groups=mesh['image'=16,'domain'=16] {'image','domain'}, dimensions={0} | all-to-all | bytes 524288 | tf_op jit(solution)/shard_map/all_to_all | solution.py:224
  114.9 0.2 shard_map.64
  115.0 0.6 copy.10
  (2 shorter events, 0.0 us)
Async XLA Ops:
  0.6 0.9 copy-start
  1.5 0.9 copy-start.1
  2.5 12.2 %collective-permute-start = (f32[2,4,8,8,128]{4,3,2,1,0:T(8,128)S(1)}, f32[2,4,8,8,128]{4,3,2,1,0:T(8,128)S(1)}, u32[]{:S(2)}, u32[]{:S(2)}) collective-permute-start(f32[2,4,8,8,128]{4,3,2,1,0:T(8,128)S(1)} %shard_map.59.refs_0_), channel_id=1, source_target_pairs={{12,0},{13,1},{14,2},{15,3},{0,4},{1,5},{2,6},{3,7},{4,8},{5,9},{6... | collective-permute-start | bytes 786440 | tf_op jit(solution)/shard_map/ppermute | solution.py:24
  4.7 10.0 %collective-permute-start.3 = (f32[2,4,8,8,128]{4,3,2,1,0:T(8,128)S(1)}, f32[2,4,8,8,128]{4,3,2,1,0:T(8,128)S(1)}, u32[]{:S(2)}, u32[]{:S(2)}) collective-permute-start(f32[2,4,8,8,128]{4,3,2,1,0:T(8,128)S(1)} %shard_map.59.refs_0_), channel_id=1, source_target_pairs={{4,0},{5,1},{6,2},{7,3},{8,4},{9,5},{10,6},{11,7},{12,8},{13,9},{1... | collective-permute-start | bytes 786440 | tf_op jit(solution)/shard_map/ppermute | solution.py:24
  6.2 10.4 %collective-permute-start.1 = (f32[2,4,8,8,128]{4,3,2,1,0:T(8,128)S(1)}, f32[2,4,8,8,128]{4,3,2,1,0:T(8,128)S(1)}, u32[]{:S(2)}, u32[]{:S(2)}) collective-permute-start(f32[2,4,8,8,128]{4,3,2,1,0:T(8,128)S(1)} %shard_map.59.refs_0_), channel_id=1, source_target_pairs={{14,0},{15,1},{0,2},{1,3},{2,4},{3,5},{4,6},{5,7},{6,8},{7,9},{8,1... | collective-permute-start | bytes 786440 | tf_op jit(solution)/shard_map/ppermute | solution.py:24
  9.0 12.4 %collective-permute-start.2 = (f32[2,4,8,8,128]{4,3,2,1,0:T(8,128)S(1)}, f32[2,4,8,8,128]{4,3,2,1,0:T(8,128)S(1)}, u32[]{:S(2)}, u32[]{:S(2)}) collective-permute-start(f32[2,4,8,8,128]{4,3,2,1,0:T(8,128)S(1)} %shard_map.59.refs_0_), channel_id=1, source_target_pairs={{2,0},{3,1},{4,2},{5,3},{6,4},{7,5},{8,6},{9,7},{10,8},{11,9},{12,... | collective-permute-start | bytes 786440 | tf_op jit(solution)/shard_map/ppermute | solution.py:24
  11.3 10.6 %collective-permute-start.6 = (f32[2,4,8,8,128]{4,3,2,1,0:T(8,128)S(1)}, f32[2,4,8,8,128]{4,3,2,1,0:T(8,128)S(1)}, u32[]{:S(2)}, u32[]{:S(2)}) collective-permute-start(f32[2,4,8,8,128]{4,3,2,1,0:T(8,128)S(1)} %shard_map.59.refs_0_), channel_id=1, source_target_pairs={{1,0},{0,1},{3,2},{2,3},{5,4},{4,5},{7,6},{6,7},{9,8},{8,9},{11,10... | collective-permute-start | bytes 786440 | tf_op jit(solution)/shard_map/ppermute | solution.py:29
  14.7 7.2 %collective-permute-start.4 = (f32[2,4,8,8,128]{4,3,2,1,0:T(8,128)S(1)}, f32[2,4,8,8,128]{4,3,2,1,0:T(8,128)S(1)}, u32[]{:S(2)}, u32[]{:S(2)}) collective-permute-start(f32[2,4,8,8,128]{4,3,2,1,0:T(8,128)S(1)} %broadcast_select_fusion), channel_id=1, source_target_pairs={{1,0},{0,1},{3,2},{2,3},{5,4},{4,5},{7,6},{6,7},{9,8},{8,9},{11,10... | collective-permute-start | bytes 786440 | tf_op jit(solution)/shard_map/ppermute | solution.py:29
  16.6 6.0 %collective-permute-start.5 = (f32[2,4,8,8,128]{4,3,2,1,0:T(8,128)S(1)}, f32[2,4,8,8,128]{4,3,2,1,0:T(8,128)S(1)}, u32[]{:S(2)}, u32[]{:S(2)}) collective-permute-start(f32[2,4,8,8,128]{4,3,2,1,0:T(8,128)S(1)} %collective-permute-done.1.refs_2_), channel_id=1, source_target_pairs={{1,0},{0,1},{3,2},{2,3},{5,4},{4,5},{7,6},{6,7},{9,8},{8,9},{11,10... | collective-permute-start | bytes 786440 | tf_op jit(solution)/shard_map/ppermute | solution.py:29
  21.4 1.6 %collective-permute-start.7 = (f32[2,4,8,8,128]{4,3,2,1,0:T(8,128)S(1)}, f32[2,4,8,8,128]{4,3,2,1,0:T(8,128)S(1)}, u32[]{:S(2)}, u32[]{:S(2)}) collective-permute-start(f32[2,4,8,8,128]{4,3,2,1,0:T(8,128)S(1)} %collective-permute-done.2.refs_3_), channel_id=1, source_target_pairs={{1,0},{0,1},{3,2},{2,3},{5,4},{4,5},{7,6},{6,7},{9,8},{8,9},{11,10... | collective-permute-start | bytes 786440 | tf_op jit(solution)/shard_map/ppermute | solution.py:29
  23.0 17.2 %copy-start.2 = (s32[2,1]{0,1:T(1,128)S(1)}, s32[2,1]{0,1:T(1,128)}, u32[]{:S(2)}) copy-start(s32[2,1]{0,1:T(1,128)} %param.6) | copy-start | bytes 28
  23.0 17.3 %copy-start.3 = (f32[2,1]{0,1:T(1,128)S(1)}, f32[2,1]{0,1:T(1,128)}, u32[]{:S(2)}) copy-start(f32[2,1]{0,1:T(1,128)} %param.7) | copy-start | bytes 28
  35.4 6.0 %collective-permute-start.8 = (f32[4,8,8,128]{3,2,1,0:T(8,128)S(1)}, f32[4,8,8,128]{3,2,1,0:T(8,128)S(1)}, u32[]{:S(2)}, u32[]{:S(2)}) collective-permute-start(f32[4,8,8,128]{3,2,1,0:T(8,128)S(1)} %get-tuple-element.8.refs_3_), channel_id=1, source_target_pairs={{0,16},{16,32},{32,48},{48,64},{64,80},{80,96},{96,112},{112,128},... | collective-permute-start | bytes 393224 | tf_op jit(solution)/shard_map/ppermute | solution.py:35
  39.0 6.7 %collective-permute-start.9 = (f32[4,8,8,128]{3,2,1,0:T(8,128)S(1)}, f32[4,8,8,128]{3,2,1,0:T(8,128)S(1)}, u32[]{:S(2)}, u32[]{:S(2)}) collective-permute-start(f32[4,8,8,128]{3,2,1,0:T(8,128)S(1)} %get-tuple-element.8.refs_3_), channel_id=1, source_target_pairs={{16,0},{32,16},{48,32},{64,48},{80,64},{96,80},{112,96},{128,112},... | collective-permute-start | bytes 393224 | tf_op jit(solution)/shard_map/ppermute | solution.py:35
  46.2 10.3 %collective-permute-start.10 = (f32[4,8,8,128]{3,2,1,0:T(8,128)S(1)}, f32[4,8,8,128]{3,2,1,0:T(8,128)S(1)}, u32[]{:S(2)}, u32[]{:S(2)}) collective-permute-start(f32[4,8,8,128]{3,2,1,0:T(8,128)S(1)} %get-tuple-element.9.refs_0_), channel_id=1, source_target_pairs={{12,0},{13,1},{14,2},{15,3},{0,4},{1,5},{2,6},{3,7},{4,8},{5,9},{6... | collective-permute-start | bytes 393224 | tf_op jit(solution)/shard_map/ppermute | solution.py:24
  47.5 9.0 %collective-permute-start.13 = (f32[4,8,8,128]{3,2,1,0:T(8,128)S(1)}, f32[4,8,8,128]{3,2,1,0:T(8,128)S(1)}, u32[]{:S(2)}, u32[]{:S(2)}) collective-permute-start(f32[4,8,8,128]{3,2,1,0:T(8,128)S(1)} %get-tuple-element.9.refs_0_), channel_id=1, source_target_pairs={{4,0},{5,1},{6,2},{7,3},{8,4},{9,5},{10,6},{11,7},{12,8},{13,9},{1... | collective-permute-start | bytes 393224 | tf_op jit(solution)/shard_map/ppermute | solution.py:24
  49.0 7.8 %collective-permute-start.11 = (f32[4,8,8,128]{3,2,1,0:T(8,128)S(1)}, f32[4,8,8,128]{3,2,1,0:T(8,128)S(1)}, u32[]{:S(2)}, u32[]{:S(2)}) collective-permute-start(f32[4,8,8,128]{3,2,1,0:T(8,128)S(1)} %get-tuple-element.9.refs_0_), channel_id=1, source_target_pairs={{14,0},{15,1},{0,2},{1,3},{2,4},{3,5},{4,6},{5,7},{6,8},{7,9},{8,1... | collective-permute-start | bytes 393224 | tf_op jit(solution)/shard_map/ppermute | solution.py:24
  51.7 8.5 %collective-permute-start.12 = (f32[4,8,8,128]{3,2,1,0:T(8,128)S(1)}, f32[4,8,8,128]{3,2,1,0:T(8,128)S(1)}, u32[]{:S(2)}, u32[]{:S(2)}) collective-permute-start(f32[4,8,8,128]{3,2,1,0:T(8,128)S(1)} %get-tuple-element.9.refs_0_), channel_id=1, source_target_pairs={{2,0},{3,1},{4,2},{5,3},{6,4},{7,5},{8,6},{9,7},{10,8},{11,9},{12,... | collective-permute-start | bytes 393224 | tf_op jit(solution)/shard_map/ppermute | solution.py:24
  54.1 6.1 %collective-permute-start.16 = (f32[4,8,8,128]{3,2,1,0:T(8,128)S(1)}, f32[4,8,8,128]{3,2,1,0:T(8,128)S(1)}, u32[]{:S(2)}, u32[]{:S(2)}) collective-permute-start(f32[4,8,8,128]{3,2,1,0:T(8,128)S(1)} %get-tuple-element.9.refs_0_), channel_id=1, source_target_pairs={{1,0},{0,1},{3,2},{2,3},{5,4},{4,5},{7,6},{6,7},{9,8},{8,9},{11,10... | collective-permute-start | bytes 393224 | tf_op jit(solution)/shard_map/ppermute | solution.py:29
  56.6 3.7 %collective-permute-start.14 = (f32[4,8,8,128]{3,2,1,0:T(8,128)S(1)}, f32[4,8,8,128]{3,2,1,0:T(8,128)S(1)}, u32[]{:S(2)}, u32[]{:S(2)}) collective-permute-start(f32[4,8,8,128]{3,2,1,0:T(8,128)S(1)} %broadcast_select_fusion.1), channel_id=1, source_target_pairs={{1,0},{0,1},{3,2},{2,3},{5,4},{4,5},{7,6},{6,7},{9,8},{8,9},{11,10... | collective-permute-start | bytes 393224 | tf_op jit(solution)/shard_map/ppermute | solution.py:29
  56.9 4.4 %collective-permute-start.15 = (f32[4,8,8,128]{3,2,1,0:T(8,128)S(1)}, f32[4,8,8,128]{3,2,1,0:T(8,128)S(1)}, u32[]{:S(2)}, u32[]{:S(2)}) collective-permute-start(f32[4,8,8,128]{3,2,1,0:T(8,128)S(1)} %collective-permute-done.11.refs_2_), channel_id=1, source_target_pairs={{1,0},{0,1},{3,2},{2,3},{5,4},{4,5},{7,6},{6,7},{9,8},{8,9},{11,10... | collective-permute-start | bytes 393224 | tf_op jit(solution)/shard_map/ppermute | solution.py:29
  60.2 1.3 %collective-permute-start.17 = (f32[4,8,8,128]{3,2,1,0:T(8,128)S(1)}, f32[4,8,8,128]{3,2,1,0:T(8,128)S(1)}, u32[]{:S(2)}, u32[]{:S(2)}) collective-permute-start(f32[4,8,8,128]{3,2,1,0:T(8,128)S(1)} %collective-permute-done.12.refs_3_), channel_id=1, source_target_pairs={{1,0},{0,1},{3,2},{2,3},{5,4},{4,5},{7,6},{6,7},{9,8},{8,9},{11,10... | collective-permute-start | bytes 393224 | tf_op jit(solution)/shard_map/ppermute | solution.py:29
  73.9 6.2 %collective-permute-start.18 = (f32[4,8,8,128]{3,2,1,0:T(8,128)S(1)}, f32[4,8,8,128]{3,2,1,0:T(8,128)S(1)}, u32[]{:S(2)}, u32[]{:S(2)}) collective-permute-start(f32[4,8,8,128]{3,2,1,0:T(8,128)S(1)} %shard_map.62.refs_3_), channel_id=1, source_target_pairs={{0,16},{16,32},{32,48},{48,64},{64,80},{80,96},{96,112},{112,128},... | collective-permute-start | bytes 393224 | tf_op jit(solution)/shard_map/ppermute | solution.py:35
  77.4 8.3 %collective-permute-start.19 = (f32[4,8,8,128]{3,2,1,0:T(8,128)S(1)}, f32[4,8,8,128]{3,2,1,0:T(8,128)S(1)}, u32[]{:S(2)}, u32[]{:S(2)}) collective-permute-start(f32[4,8,8,128]{3,2,1,0:T(8,128)S(1)} %shard_map.62.refs_3_), channel_id=1, source_target_pairs={{16,0},{32,16},{48,32},{64,48},{80,64},{96,80},{112,96},{128,112},... | collective-permute-start | bytes 393224 | tf_op jit(solution)/shard_map/ppermute | solution.py:35

commit v2 on v1

v2 whole, which is shorter than its diff:
```python
import jax
import jax.numpy as jnp
from jax import lax
from jax.experimental import pallas as pl
from jax.experimental.pallas import tpu as pltpu
from jax.sharding import PartitionSpec as P

STEPS = 8
CYCLES = 2
SUBLANES = 8
UNROLL = 4

stiffness = 1.0
time_step = 0.008
epsilon = 1e-06

VMEM = pl.BlockSpec(memory_space=pltpu.VMEM)
SMEM = pl.BlockSpec(memory_space=pltpu.SMEM)
PARAMS = pltpu.CompilerParams(vmem_limit_bytes=16 << 20)


def exchanged(value, axis, partner):
    size = lax.axis_size(axis)
    pairs = [(i, partner(i, size)) for i in range(size)]
    return lax.ppermute(value, axis, [(i, j) for i, j in pairs if 0 <= j < size])


def passed_along(value, steps):
    count = lax.axis_size("image")
    first, last = (max(0, -steps), min(count, count - steps))
    return lax.ppermute(value, "image", [(i, i + steps) for i in range(first, last)])


def side(index, stride):
    return 1 - 2 * (index // stride % 2)


def partner_inside(stride):
    return lambda i, size: i + side(i, stride) * stride


def partner_across(stride):
    return lambda i, size: (i - side(i, stride) * stride) % size


def halo_pieces(own, index):
    twos = [exchanged(own, "domain", partner(2)) for partner in (partner_across, partner_inside)]
    fours = [exchanged(own, "domain", partner(4)) for partner in (partner_across, partner_inside)]
    chosen = jnp.where(side(index, 4) == side(index, 1), fours[1], fours[0])
    return [own, *twos, *fours] + [
        exchanged(piece, "domain", partner_inside(1)) for piece in (own, *twos, chosen)
    ]


def slab_offsets(index):
    core, two, four = (side(index, stride) for stride in (1, 2, 4))
    straight = (0, -2 * two, 2 * two, -4 * four, 4 * four)
    return straight + (core, core - 2 * two, core + 2 * two, -3 * core)


def fill(window, index, pieces, rows):
    for offset, piece in zip(slab_offsets(index), pieces):
        start = pl.multiple_of((4 + offset) * rows, rows)
        window[pl.ds(start, rows)] = piece[...]


def fold(plane, target, place, scale=None):
    folds = target.shape[-3]
    for v in range(folds):
        part = plane[pl.ds(v, SUBLANES, stride=folds), :]
        target[(*place, v)] = part if scale is None else part * scale


def unfold(value, target):
    for v in range(value.shape[0]):
        target[pl.ds(v, SUBLANES, stride=value.shape[0]), :] = value[v]


def y_shifted(value, offset):
    if offset == 1:
        return jnp.concatenate([pltpu.roll(value[-1:], 1, 1), value[:-1]], axis=0)
    return jnp.concatenate([value[1:], pltpu.roll(value[:1], SUBLANES - 1, 1)], axis=0)


def z_shifted(value, offset):
    return pltpu.roll(value, offset % value.shape[2], 2)


def potential_and_motion(field, mobile, row):
    here = field[row]
    square = here * here
    around = field[row - 1] + field[row + 1]
    for shifted in (y_shifted, z_shifted):
        around = around + (shifted(here, 1) + shifted(here, -1))
    potential = here * (square + 5.0) - around
    motion = mobile[row] / (1.0 + square)
    return potential, motion


def take_steps(field, mobile, length):
    for step in range(STEPS):
        first, last = 2 * step + 2, length - 2 * step - 2
        before = potential_and_motion(field, mobile, first - 1)
        now = potential_and_motion(field, mobile, first)
        inflow = (before[1] + now[1]) * (now[0] - before[0])

        def one_row(row, carried):
            potential, motion, inflow = carried
            ahead = potential_and_motion(field, mobile, row + 1)
            outflow = (motion + ahead[1]) * (ahead[0] - potential)
            change = outflow - inflow
            for shifted in (y_shifted, z_shifted):
                flow = (motion + shifted(motion, 1)) * (potential - shifted(potential, 1))
                change = change + (shifted(flow, -1) - flow)
            field[row] = field[row] + change
            return ahead[0], ahead[1], outflow

        lax.fori_loop(first, last, one_row, (now[0], now[1], inflow), unroll=UNROLL)


def pack_kernel(field, mobility, out, held, semaphores):
    copies = [
        pltpu.make_async_copy(source, held.at[i], semaphores.at[i])
        for i, source in enumerate((field, mobility))
    ]
    for copy in copies:
        copy.start()
    for i, copy in enumerate(copies):
        copy.wait()
        for row in range(field.shape[0]):
            fold(held.at[i, row], out, (i, row), 0.5 * time_step if i else None)


def first_kernel(index_ref, *refs):
    pieces, out, mobile, window = refs[:9], *refs[9:]
    rows = out.shape[0]
    fill(window, index_ref[0], [piece.at[0] for piece in pieces], rows)
    fill(mobile, index_ref[0], [piece.at[1] for piece in pieces], rows)
    take_steps(window, mobile, 9 * rows)
    out[...] = window[pl.ds(4 * rows, rows)]


def later_kernel(index_ref, *refs):
    pieces, mobile, out, window = refs[:9], *refs[9:]
    rows = out.shape[0]
    fill(window, index_ref[0], pieces, rows)
    take_steps(window, mobile, 9 * rows)
    out[...] = window[pl.ds(4 * rows, rows)]


def squares_of(own, after):
    return jnp.sum(jnp.square(after[...] - own[...]), axis=(0, 1, 2))[None]


def mixing(cycle, image, lower_ref, weight_ref):
    from_left = lower_ref[0, cycle] < image
    weight = weight_ref[0, cycle]
    rest = 1.0 - weight
    return from_left, jnp.where(from_left, weight, rest), jnp.where(from_left, rest, weight)


def mix_kernel(cycle, index_ref, lower_ref, weight_ref, own, inside, across, out, total):
    image = index_ref[0]
    even = lax.rem(image, 2) == 0
    from_left, of_other, of_own = mixing(cycle, image, lower_ref, weight_ref)

    def when(condition, do, *refs):
        pl.when(condition)(lambda: do(*refs))

    def measure(after):
        total[...] = squares_of(own, after)

    def write(other):
        for row in range(own.shape[0]):
            out[row] = of_other * other[row] + of_own * own[row]

    when(even, measure, inside)
    when(jnp.logical_not(even), measure, across)
    when(from_left != even, write, inside)
    when(from_left == even, write, across)


def gap_kernel(own, right, earlier, total):
    total[: CYCLES - 1] = earlier[...]
    total[CYCLES - 1 :] = squares_of(own, right)


def last_kernel(cells, images, index_ref, lower_ref, weight_ref, gaps, own, left, right, out, length):
    image = index_ref[0]
    from_left, of_other, of_own = mixing(CYCLES - 1, image, lower_ref, weight_ref)

    def write(other):
        for row in range(own.shape[0]):
            unfold(of_other * other[row] + of_own * own[row], out.at[row])

    @pl.when(from_left)
    def _():
        write(left)

    @pl.when(jnp.logical_not(from_left))
    def _():
        write(right)

    each = jnp.sum(gaps[...].reshape(images, -1, CYCLES, gaps.shape[-1]), axis=1)
    distance = jnp.sqrt(jnp.sum(each, axis=-1, keepdims=True) / cells + epsilon)
    position = lax.broadcasted_iota(jnp.int32, distance.shape, 0)
    reached = jnp.sum(jnp.where(position < image, distance, 0.0), axis=0)
    lane = lax.broadcasted_iota(jnp.int32, length.shape, 1)
    result = jnp.zeros(length.shape, jnp.float32)
    for cycle in range(CYCLES):
        result = jnp.where(lane == cycle, reached[cycle : cycle + 1], result)
    length[...] = result


def shaped(*shape):
    return jax.ShapeDtypeStruct(shape, jnp.float32)


def per_device(field, mobility, lower, weights):
    rows, depth, lanes = field.shape[1:]
    slab = (rows, depth // SUBLANES, SUBLANES, lanes)
    wide = (9 * rows,) + slab[1:]
    window = pltpu.VMEM(wide, jnp.float32)
    image_count, domain_count = lax.axis_size("image"), lax.axis_size("domain")
    image_index = lax.axis_index("image")[None]
    index = lax.axis_index("domain")
    lower, weights = lower.T, weights.T
    cells = rows * domain_count * depth * lanes

    packed = pl.pallas_call(
        pack_kernel,
        out_shape=shaped(2, *slab),
        in_specs=[pl.BlockSpec(memory_space=pltpu.HBM)] * 2,
        out_specs=VMEM,
        scratch_shapes=[
            pltpu.VMEM((2, rows, depth, lanes), jnp.float32),
            pltpu.SemaphoreType.DMA((2,)),
        ],
        compiler_params=PARAMS,
    )(field[0], mobility)
    phase, mobile = pl.pallas_call(
        first_kernel,
        out_shape=(shaped(*slab), shaped(*wide)),
        in_specs=[SMEM] + [VMEM] * 9,
        out_specs=(VMEM, VMEM),
        scratch_shapes=[window],
        compiler_params=PARAMS,
    )(index[None], *halo_pieces(packed, index))

    totals = []
    for cycle in range(CYCLES - 1):
        across = exchanged(phase, "image", lambda i, size: i - side(i, 1))
        inside = exchanged(phase, "image", partner_inside(1))
        phase, total = pl.pallas_call(
            lambda *refs, cycle=cycle: mix_kernel(cycle, *refs),
            out_shape=(shaped(*slab), shaped(1, lanes)),
            in_specs=[SMEM] * 3 + [VMEM] * 3,
            out_specs=(VMEM, VMEM),
            compiler_params=PARAMS,
        )(image_index, lower, weights, phase, inside, across)
        totals.append(total)
        phase = pl.pallas_call(
            later_kernel,
            out_shape=shaped(*slab),
            in_specs=[SMEM] + [VMEM] * 10,
            out_specs=VMEM,
            scratch_shapes=[window],
            compiler_params=PARAMS,
        )(index[None], *halo_pieces(phase, index), mobile)
    right, left = passed_along(phase, -1), passed_along(phase, 1)
    mine = pl.pallas_call(
        gap_kernel,
        out_shape=shaped(CYCLES, lanes),
        in_specs=[VMEM] * 3,
        out_specs=VMEM,
        compiler_params=PARAMS,
    )(phase, right, jnp.concatenate(totals, axis=0))
    everyone = jnp.broadcast_to(mine[None], (image_count * domain_count, CYCLES, lanes))
    gaps = lax.all_to_all(everyone, ("image", "domain"), 0, 0)
    evolved, arclength = pl.pallas_call(
        lambda *refs: last_kernel(cells, image_count, *refs),
        out_shape=(shaped(rows, depth, lanes), shaped(1, CYCLES)),
        in_specs=[SMEM] * 3 + [VMEM] * 4,
        out_specs=(VMEM, VMEM),
        compiler_params=PARAMS,
    )(image_index, lower, weights, gaps, phase, left, right)
    return evolved[None], arclength.T


def solution(mesh):
    return jax.shard_map(
        per_device,
        mesh=mesh,
        in_specs=(
            P("image", "domain", None, None),
            P("domain", None, None),
            P(None, "image"),
            P(None, "image"),
        ),
        out_specs=(P("image", "domain", None, None), P(None, "image")),
        check_vma=False,
    )
```

time: 116 us -> 113 us (0.974)
  blocking collectives: 27.8 us -> 0 us
  waiting for transfers between devices: 14.6 us -> 31.4 us
  starting transfers between devices: 43 us -> 51.4 us
    all_to_all x1 -> x0, blocking collectives: 27.8 us -> none  [per_device(): gaps = lax.all_to_all(everyone, ('image', 'domain'), 0, 0)]
    all_to_all x0 -> x1, starting transfers between devices: none -> 13.8 us  [per_device(): gaps = lax.all_to_all(everyone, ('image', 'domain'), 0, 0)]
    ppermute x16 -> x18, waiting for transfers between devices: 2.52 us -> 13.9 us  [exchanged(): lax.ppermute(value, axis, [(i, j) for i, j in pairs if 0 <= j < size])]
    all_to_all x0 -> x1, waiting for transfers between devices: none -> 7.24 us  [per_device(): gaps = lax.all_to_all(everyone, ('image', 'domain'), 0, 0)]
    ppermute x4 -> x2, starting transfers between devices: 9.68 us -> 4.69 us  [passed_along(): lax.ppermute(value, 'image', [(i, i + steps) for i in range(first, last)])]
    ppermute x4 -> x2, waiting for transfers between devices: 12.1 us -> 10.3 us  [passed_along(): lax.ppermute(value, 'image', [(i, i + steps) for i in range(first, last)])]
    pallas_call x2 -> x3, Pallas kernels: 0.22 us -> 1.73 us  [the longest x1 1.3 us: per_device(): pl.pallas_call(lambda *refs: last_kernel(cells, image_count, *refs), out_...]
    pallas_call x2 -> x1, Pallas kernels: 1.91 us -> 0.61 us  [per_device(): pl.pallas_call(lambda *refs, cycle=cycle: mix_kernel(cycle, *refs), out_s...]
  transfers between devices with their start and end apart: 20 -> 21, of which waited for: 8 -> 10; matrix products, arithmetic and copies ran while one was open for 0% -> 0% of each run, Pallas kernels for 0% -> 0%
where the time goes in v2:
time: 113 us
  starting transfers between devices  51.4 us (45%)
  waiting for transfers between devices  31.4 us (28%)
  Pallas kernels  26.9 us (24%)
  local copies, waits for them, and re-layouts  2.59 us (2%)
    ppermute x18, starting transfers between devices, exchanged(): lax.ppermute(value, axis, [(i, j) for i, j in pairs if 0 <= j < size])  33 us
    ppermute x18, waiting for transfers between devices, exchanged(): lax.ppermute(value, axis, [(i, j) for i, j in pairs if 0 <= j < size])  13.9 us
    all_to_all x1, starting transfers between devices, per_device(): gaps = lax.all_to_all(everyone, ('image', 'domain'), 0, 0)  13.8 us
    pallas_call x1, Pallas kernels, per_device(): pl.pallas_call(first_kernel, out_shape=(shaped(*slab), shaped(*wide)), in...  12.3 us
    pallas_call x1, Pallas kernels, per_device(): pl.pallas_call(later_kernel, out_shape=shaped(*slab), in_specs=[SMEM] + [...  12.3 us
    ppermute x2, waiting for transfers between devices, passed_along(): lax.ppermute(value, 'image', [(i, i + steps) for i in range(first, last)])  10.3 us
    all_to_all x1, waiting for transfers between devices, per_device(): gaps = lax.all_to_all(everyone, ('image', 'domain'), 0, 0)  7.24 us
    ppermute x2, starting transfers between devices, passed_along(): lax.ppermute(value, 'image', [(i, i + steps) for i in range(first, last)])  4.69 us
  transfers between devices with their start and end apart: 21, of which 10 were waited for; matrix products, arithmetic and copies ran while one was open for 0% of the time, Pallas kernels for 0%

profile of v2, /device:TPU:1, one launch (start us, length us, event | category | flops | bytes accessed | tf_op | source)
XLA Modules:
  0.0 113.2 jit_solution(11511002086183172873)
XLA Ops:
  0.6 0.0 copy-start
  0.6 0.9 copy-done
  1.5 0.0 copy-start.1
  1.5 0.9 copy-done.1
  2.4 0.4 shard_map.59.refs_0_
  2.8 2.2 %collective-permute-start.3 = (f32[2,4,8,8,128]{4,3,2,1,0:T(8,128)S(1)}, f32[2,4,8,8,128]{4,3,2,1,0:T(8,128)S(1)}, u32[]{:S(2)}, u32[]{:S(2)}) collective-permute-start(f32[2,4,8,8,128]{4,3,2,1,0:T(8,128)S(1)} %shard_map.59.refs_0_), channel_id=1, source_target_pairs={{0,4},{1,5},{2,6},{3,7},{4,0},{5,1},{6,2},{7,3},{8,12},{9,13},{10,... | collective-permute-start | bytes 786440 | tf_op jit(solution)/shard_map/ppermute | solution.py:25
  5.0 1.9 %collective-permute-start.2 = (f32[2,4,8,8,128]{4,3,2,1,0:T(8,128)S(1)}, f32[2,4,8,8,128]{4,3,2,1,0:T(8,128)S(1)}, u32[]{:S(2)}, u32[]{:S(2)}) collective-permute-start(f32[2,4,8,8,128]{4,3,2,1,0:T(8,128)S(1)} %shard_map.59.refs_0_), channel_id=1, source_target_pairs={{0,12},{1,13},{2,14},{3,15},{4,8},{5,9},{6,10},{7,11},{8,4},{9,5},... | collective-permute-start | bytes 786440 | tf_op jit(solution)/shard_map/ppermute | solution.py:25
  6.9 2.7 %collective-permute-start.1 = (f32[2,4,8,8,128]{4,3,2,1,0:T(8,128)S(1)}, f32[2,4,8,8,128]{4,3,2,1,0:T(8,128)S(1)}, u32[]{:S(2)}, u32[]{:S(2)}) collective-permute-start(f32[2,4,8,8,128]{4,3,2,1,0:T(8,128)S(1)} %shard_map.59.refs_0_), channel_id=1, source_target_pairs={{0,2},{1,3},{2,0},{3,1},{4,6},{5,7},{6,4},{7,5},{8,10},{9,11},{10,... | collective-permute-start | bytes 786440 | tf_op jit(solution)/shard_map/ppermute | solution.py:25
  9.7 0.7 collective-permute-start
  10.4 2.0 %collective-permute-start.4 = (f32[2,4,8,8,128]{4,3,2,1,0:T(8,128)S(1)}, f32[2,4,8,8,128]{4,3,2,1,0:T(8,128)S(1)}, u32[]{:S(2)}, u32[]{:S(2)}) collective-permute-start(f32[2,4,8,8,128]{4,3,2,1,0:T(8,128)S(1)} %shard_map.59.refs_0_), channel_id=1, source_target_pairs={{0,1},{1,0},{2,3},{3,2},{4,5},{5,4},{6,7},{7,6},{8,9},{9,8},{10,11... | collective-permute-start | bytes 786440 | tf_op jit(solution)/shard_map/ppermute | solution.py:25
  12.4 0.0 collective-permute-done.3.refs_4_
  12.4 0.5 collective-permute-done.2.refs_3_
  12.9 2.1 %collective-permute-start.7 = (f32[2,4,8,8,128]{4,3,2,1,0:T(8,128)S(1)}, f32[2,4,8,8,128]{4,3,2,1,0:T(8,128)S(1)}, u32[]{:S(2)}, u32[]{:S(2)}) collective-permute-start(f32[2,4,8,8,128]{4,3,2,1,0:T(8,128)S(1)} %broadcast_select_fusion), channel_id=1, source_target_pairs={{0,1},{1,0},{2,3},{3,2},{4,5},{5,4},{6,7},{7,6},{8,9},{9,8},{10,11... | collective-permute-start | bytes 786440 | tf_op jit(solution)/shard_map/ppermute | solution.py:25
  15.1 0.0 collective-permute-done.1.refs_2_
  15.1 3.8 %collective-permute-start.6 = (f32[2,4,8,8,128]{4,3,2,1,0:T(8,128)S(1)}, f32[2,4,8,8,128]{4,3,2,1,0:T(8,128)S(1)}, u32[]{:S(2)}, u32[]{:S(2)}) collective-permute-start(f32[2,4,8,8,128]{4,3,2,1,0:T(8,128)S(1)} %collective-permute-done.1.refs_2_), channel_id=1, source_target_pairs={{0,1},{1,0},{2,3},{3,2},{4,5},{5,4},{6,7},{7,6},{8,9},{9,8},{10,11... | collective-permute-start | bytes 786440 | tf_op jit(solution)/shard_map/ppermute | solution.py:25
  18.9 2.8 %collective-permute-done.refs_1_ = f32[2,4,8,8,128]{4,3,2,1,0:T(8,128)S(1)} collective-permute-done((f32[2,4,8,8,128]{4,3,2,1,0:T(8,128)S(1)}, f32[2,4,8,8,128]{4,3,2,1,0:T(8,128)S(1)}, u32[]{:S(2)}, u32[]{:S(2)}) %collective-permute-start) | collective-permute-done | bytes 262176 | tf_op jit(solution)/shard_map/ppermute | solution.py:25
  21.6 1.7 %collective-permute-start.5 = (f32[2,4,8,8,128]{4,3,2,1,0:T(8,128)S(1)}, f32[2,4,8,8,128]{4,3,2,1,0:T(8,128)S(1)}, u32[]{:S(2)}, u32[]{:S(2)}) collective-permute-start(f32[2,4,8,8,128]{4,3,2,1,0:T(8,128)S(1)} %collective-permute-done.refs_1_), channel_id=1, source_target_pairs={{0,1},{1,0},{2,3},{3,2},{4,5},{5,4},{6,7},{7,6},{8,9},{9,8},{10,11... | collective-permute-start | bytes 786440 | tf_op jit(solution)/shard_map/ppermute | solution.py:25
  23.3 0.0 collective-permute-done.4.refs_5_
  23.3 0.0 collective-permute-done.7.refs_8_
  23.3 0.0 collective-permute-done.6.refs_7_
  23.3 1.1 %collective-permute-done.5.refs_6_ = f32[2,4,8,8,128]{4,3,2,1,0:T(8,128)S(1)} collective-permute-done((f32[2,4,8,8,128]{4,3,2,1,0:T(8,128)S(1)}, f32[2,4,8,8,128]{4,3,2,1,0:T(8,128)S(1)}, u32[]{:S(2)}, u32[]{:S(2)}) %collective-permute-start.5) | collective-permute-done | bytes 262176 | tf_op jit(solution)/shard_map/ppermute | solution.py:25
  24.4 0.0 copy-start.2
  24.4 0.0 copy-start.3
  24.4 12.3 %shard_map.60 = (f32[4,8,8,128]{3,2,1,0:T(8,128)S(1)}, f32[36,8,8,128]{3,2,1,0:T(8,128)S(1)}) custom-call(s32[1]{0:T(128)} %bitcast.3.index_ref, f32[2,4,8,8,128]{4,3,2,1,0:T(8,128)S(1)} %shard_map.59.refs_0_, f32[2,4,8,8,128]{4,3,2,1,0:T(8,128)S(1)} %collective-permute-done.refs_1_, f32[2,4,8,8,128]{4,3,2,1,0:T(8,128)S(1)} %collective-permute-done.1.refs_2_, ...), custom_call_target="tpu_custom_call" | custom-call | tf_op jit(solution)/shard_map/pallas_call | solution.py:241
  36.8 0.7 collective-permute-start.9
  37.4 4.6 %collective-permute-start.8 = (f32[4,8,8,128]{3,2,1,0:T(8,128)S(1)}, f32[4,8,8,128]{3,2,1,0:T(8,128)S(1)}, u32[]{:S(2)}, u32[]{:S(2)}) collective-permute-start(f32[4,8,8,128]{3,2,1,0:T(8,128)S(1)} %get-tuple-element.8.refs_3_), channel_id=1, source_target_pairs={{0,16},{16,0},{32,48},{48,32},{64,80},{80,64},{96,112},{112,96},{1... | collective-permute-start | bytes 393224 | tf_op jit(solution)/shard_map/ppermute | solution.py:25
  42.0 0.0 collective-permute-done.9.refs_5_
  42.0 3.2 %collective-permute-done.8.refs_4_ = f32[4,8,8,128]{3,2,1,0:T(8,128)S(1)} collective-permute-done((f32[4,8,8,128]{3,2,1,0:T(8,128)S(1)}, f32[4,8,8,128]{3,2,1,0:T(8,128)S(1)}, u32[]{:S(2)}, u32[]{:S(2)}) %collective-permute-start.8) | collective-permute-done | bytes 131104 | tf_op jit(solution)/shard_map/ppermute | solution.py:25
  45.3 0.0 copy-done.2
  45.3 0.0 copy-done.3
  45.3 0.6 shard_map.61
  45.9 0.8 collective-permute-start.13
  46.7 1.0 collective-permute-start.12
  47.7 1.8 %collective-permute-start.14 = (f32[4,8,8,128]{3,2,1,0:T(8,128)S(1)}, f32[4,8,8,128]{3,2,1,0:T(8,128)S(1)}, u32[]{:S(2)}, u32[]{:S(2)}) collective-permute-start(f32[4,8,8,128]{3,2,1,0:T(8,128)S(1)} %get-tuple-element.9.refs_0_), channel_id=1, source_target_pairs={{0,1},{1,0},{2,3},{3,2},{4,5},{5,4},{6,7},{7,6},{8,9},{9,8},{10,11... | collective-permute-start | bytes 393224 | tf_op jit(solution)/shard_map/ppermute | solution.py:25
  49.4 2.8 %collective-permute-start.11 = (f32[4,8,8,128]{3,2,1,0:T(8,128)S(1)}, f32[4,8,8,128]{3,2,1,0:T(8,128)S(1)}, u32[]{:S(2)}, u32[]{:S(2)}) collective-permute-start(f32[4,8,8,128]{3,2,1,0:T(8,128)S(1)} %get-tuple-element.9.refs_0_), channel_id=1, source_target_pairs={{0,2},{1,3},{2,0},{3,1},{4,6},{5,7},{6,4},{7,5},{8,10},{9,11},{10,... | collective-permute-start | bytes 393224 | tf_op jit(solution)/shard_map/ppermute | solution.py:25
  52.2 1.6 %collective-permute-start.10 = (f32[4,8,8,128]{3,2,1,0:T(8,128)S(1)}, f32[4,8,8,128]{3,2,1,0:T(8,128)S(1)}, u32[]{:S(2)}, u32[]{:S(2)}) collective-permute-start(f32[4,8,8,128]{3,2,1,0:T(8,128)S(1)} %get-tuple-element.9.refs_0_), channel_id=1, source_target_pairs={{0,14},{1,15},{2,4},{3,5},{4,2},{5,3},{6,8},{7,9},{8,6},{9,7},{10,... | collective-permute-start | bytes 393224 | tf_op jit(solution)/shard_map/ppermute | solution.py:25
  53.8 0.0 collective-permute-done.13.refs_4_
  53.8 0.0 collective-permute-done.12.refs_3_
  53.8 0.6 collective-permute-start.17
  54.5 1.5 %collective-permute-done.11.refs_2_ = f32[4,8,8,128]{3,2,1,0:T(8,128)S(1)} collective-permute-done((f32[4,8,8,128]{3,2,1,0:T(8,128)S(1)}, f32[4,8,8,128]{3,2,1,0:T(8,128)S(1)}, u32[]{:S(2)}, u32[]{:S(2)}) %collective-permute-start.11) | collective-permute-done | bytes 131104 | tf_op jit(solution)/shard_map/ppermute | solution.py:25
  56.0 0.9 collective-permute-start.16
  56.9 3.7 %collective-permute-done.10.refs_1_ = f32[4,8,8,128]{3,2,1,0:T(8,128)S(1)} collective-permute-done((f32[4,8,8,128]{3,2,1,0:T(8,128)S(1)}, f32[4,8,8,128]{3,2,1,0:T(8,128)S(1)}, u32[]{:S(2)}, u32[]{:S(2)}) %collective-permute-start.10) | collective-permute-done | bytes 131104 | tf_op jit(solution)/shard_map/ppermute | solution.py:25
  60.6 1.1 %collective-permute-start.15 = (f32[4,8,8,128]{3,2,1,0:T(8,128)S(1)}, f32[4,8,8,128]{3,2,1,0:T(8,128)S(1)}, u32[]{:S(2)}, u32[]{:S(2)}) collective-permute-start(f32[4,8,8,128]{3,2,1,0:T(8,128)S(1)} %collective-permute-done.10.refs_1_), channel_id=1, source_target_pairs={{0,1},{1,0},{2,3},{3,2},{4,5},{5,4},{6,7},{7,6},{8,9},{9,8},{10,11... | collective-permute-start | bytes 393224 | tf_op jit(solution)/shard_map/ppermute | solution.py:25
  61.7 0.0 collective-permute-done.14.refs_5_
  61.7 0.0 collective-permute-done.17.refs_8_
  61.8 0.0 collective-permute-done.16.refs_7_
  61.8 1.0 collective-permute-done.15.refs_6_
  62.7 12.3 %shard_map.62.own.refs_4_ = f32[4,8,8,128]{3,2,1,0:T(8,128)S(1)} custom-call(s32[1]{0:T(128)} %bitcast.3.index_ref, f32[4,8,8,128]{3,2,1,0:T(8,128)S(1)} %get-tuple-element.9.refs_0_, f32[4,8,8,128]{3,2,1,0:T(8,128)S(1)} %collective-permute-done.10.refs_1_, f32[4,8,8,128]{3,2,1,0:T(8,128)S(1)} %collective-permute-done.11.refs_2_, ...), custom_call_target="tpu_custom_call" | custom-call | tf_op jit(solution)/shard_map/pallas_call | solution.py:262
  75.0 1.3 %collective-permute-start.18 = (f32[4,8,8,128]{3,2,1,0:T(8,128)S(1)}, f32[4,8,8,128]{3,2,1,0:T(8,128)S(1)}, u32[]{:S(2)}, u32[]{:S(2)}) collective-permute-start(f32[4,8,8,128]{3,2,1,0:T(8,128)S(1)} %shard_map.62.own.refs_4_), channel_id=1, source_target_pairs={{16,0},{32,16},{48,32},{64,48},{80,64},{96,80},{112,96},{128,112},... | collective-permute-start | bytes 393224 | tf_op jit(solution)/shard_map/ppermute | solution.py:31
  76.3 5.3 %collective-permute-done.18.right.refs_6_ = f32[4,8,8,128]{3,2,1,0:T(8,128)S(1)} collective-permute-done((f32[4,8,8,128]{3,2,1,0:T(8,128)S(1)}, f32[4,8,8,128]{3,2,1,0:T(8,128)S(1)}, u32[]{:S(2)}, u32[]{:S(2)}) %collective-permute-start.18) | collective-permute-done | bytes 131104 | tf_op jit(solution)/shard_map/ppermute | solution.py:31
  81.7 0.8 broadcast_in_dim.18
  82.5 13.8 %all-to-all-start = ((f32[256,2,128]{2,1,0:T(2,128)}), f32[256,2,128]{2,1,0:T(2,128)S(1)}, u32[]{:S(2)}, u32[]{:S(2)}) async-start(f32[256,2,128]{2,1,0:T(2,128)} %broadcast_in_dim.18), calls=%async_computation | async-start | bytes 524288 | tf_op jit(solution)/shard_map/all_to_all | solution.py:279
  96.2 3.4 %collective-permute-start.19 = (f32[4,8,8,128]{3,2,1,0:T(8,128)S(1)}, f32[4,8,8,128]{3,2,1,0:T(8,128)S(1)}, u32[]{:S(2)}, u32[]{:S(2)}) collective-permute-start(f32[4,8,8,128]{3,2,1,0:T(8,128)S(1)} %shard_map.62.own.refs_4_), channel_id=1, source_target_pairs={{0,16},{16,32},{32,48},{48,64},{64,80},{80,96},{96,112},{112,128},... | collective-permute-start | bytes 393224 | tf_op jit(solution)/shard_map/ppermute | solution.py:31
  99.6 5.0 %collective-permute-done.19.refs_5_ = f32[4,8,8,128]{3,2,1,0:T(8,128)S(1)} collective-permute-done((f32[4,8,8,128]{3,2,1,0:T(8,128)S(1)}, f32[4,8,8,128]{3,2,1,0:T(8,128)S(1)}, u32[]{:S(2)}, u32[]{:S(2)}) %collective-permute-start.19) | collective-permute-done | bytes 131104 | tf_op jit(solution)/shard_map/ppermute | solution.py:31
  104.6 7.2 %all-to-all-done.refs_3_ = f32[256,2,128]{2,1,0:T(2,128)S(1)} async-done(((f32[256,2,128]{2,1,0:T(2,128)}), f32[256,2,128]{2,1,0:T(2,128)S(1)}, u32[]{:S(2)}, u32[]{:S(2)}) %all-to-all-start) | async-done | bytes 262176 | tf_op jit(solution)/shard_map/all_to_all | solution.py:279
  111.9 1.3 %shard_map.64 = (f32[4,64,128]{2,1,0:T(8,128)}, f32[1,2]{1,0:T(1,128)}) custom-call(s32[1]{0:T(128)} %bitcast.refs_0_, s32[1,2]{1,0:T(1,128)S(1)} %bitcast.9, f32[1,2]{1,0:T(1,128)S(1)} %bitcast.11, f32[256,2,128]{2,1,0:T(2,128)S(1)} %all-to-all-done.refs_3_, f32[4,8,8,128]{3,2,1,0:T(8,128)S(1)} %shard_map.62.own.refs_4_, ...), custom_call_target="tpu_custom_call" | custom-call | tf_op jit(solution)/shard_map/pallas_call | solution.py:280
  (3 shorter events, 0.1 us)
Async XLA Ops:
  0.6 0.9 copy-start
  1.5 0.9 copy-start.1
  2.8 9.6 %collective-permute-start.3 = (f32[2,4,8,8,128]{4,3,2,1,0:T(8,128)S(1)}, f32[2,4,8,8,128]{4,3,2,1,0:T(8,128)S(1)}, u32[]{:S(2)}, u32[]{:S(2)}) collective-permute-start(f32[2,4,8,8,128]{4,3,2,1,0:T(8,128)S(1)} %shard_map.59.refs_0_), channel_id=1, source_target_pairs={{0,4},{1,5},{2,6},{3,7},{4,0},{5,1},{6,2},{7,3},{8,12},{9,13},{10,... | collective-permute-start | bytes 786440 | tf_op jit(solution)/shard_map/ppermute | solution.py:25
  5.0 7.9 %collective-permute-start.2 = (f32[2,4,8,8,128]{4,3,2,1,0:T(8,128)S(1)}, f32[2,4,8,8,128]{4,3,2,1,0:T(8,128)S(1)}, u32[]{:S(2)}, u32[]{:S(2)}) collective-permute-start(f32[2,4,8,8,128]{4,3,2,1,0:T(8,128)S(1)} %shard_map.59.refs_0_), channel_id=1, source_target_pairs={{0,12},{1,13},{2,14},{3,15},{4,8},{5,9},{6,10},{7,11},{8,4},{9,5},... | collective-permute-start | bytes 786440 | tf_op jit(solution)/shard_map/ppermute | solution.py:25
  6.9 8.2 %collective-permute-start.1 = (f32[2,4,8,8,128]{4,3,2,1,0:T(8,128)S(1)}, f32[2,4,8,8,128]{4,3,2,1,0:T(8,128)S(1)}, u32[]{:S(2)}, u32[]{:S(2)}) collective-permute-start(f32[2,4,8,8,128]{4,3,2,1,0:T(8,128)S(1)} %shard_map.59.refs_0_), channel_id=1, source_target_pairs={{0,2},{1,3},{2,0},{3,1},{4,6},{5,7},{6,4},{7,5},{8,10},{9,11},{10,... | collective-permute-start | bytes 786440 | tf_op jit(solution)/shard_map/ppermute | solution.py:25
  9.7 11.9 %collective-permute-start = (f32[2,4,8,8,128]{4,3,2,1,0:T(8,128)S(1)}, f32[2,4,8,8,128]{4,3,2,1,0:T(8,128)S(1)}, u32[]{:S(2)}, u32[]{:S(2)}) collective-permute-start(f32[2,4,8,8,128]{4,3,2,1,0:T(8,128)S(1)} %shard_map.59.refs_0_), channel_id=1, source_target_pairs={{0,14},{1,15},{2,4},{3,5},{4,2},{5,3},{6,8},{7,9},{8,6},{9,7},{10,... | collective-permute-start | bytes 786440 | tf_op jit(solution)/shard_map/ppermute | solution.py:25
  10.4 12.9 %collective-permute-start.4 = (f32[2,4,8,8,128]{4,3,2,1,0:T(8,128)S(1)}, f32[2,4,8,8,128]{4,3,2,1,0:T(8,128)S(1)}, u32[]{:S(2)}, u32[]{:S(2)}) collective-permute-start(f32[2,4,8,8,128]{4,3,2,1,0:T(8,128)S(1)} %shard_map.59.refs_0_), channel_id=1, source_target_pairs={{0,1},{1,0},{2,3},{3,2},{4,5},{5,4},{6,7},{7,6},{8,9},{9,8},{10,11... | collective-permute-start | bytes 786440 | tf_op jit(solution)/shard_map/ppermute | solution.py:25
  12.9 10.3 %collective-permute-start.7 = (f32[2,4,8,8,128]{4,3,2,1,0:T(8,128)S(1)}, f32[2,4,8,8,128]{4,3,2,1,0:T(8,128)S(1)}, u32[]{:S(2)}, u32[]{:S(2)}) collective-permute-start(f32[2,4,8,8,128]{4,3,2,1,0:T(8,128)S(1)} %broadcast_select_fusion), channel_id=1, source_target_pairs={{0,1},{1,0},{2,3},{3,2},{4,5},{5,4},{6,7},{7,6},{8,9},{9,8},{10,11... | collective-permute-start | bytes 786440 | tf_op jit(solution)/shard_map/ppermute | solution.py:25
  15.1 8.2 %collective-permute-start.6 = (f32[2,4,8,8,128]{4,3,2,1,0:T(8,128)S(1)}, f32[2,4,8,8,128]{4,3,2,1,0:T(8,128)S(1)}, u32[]{:S(2)}, u32[]{:S(2)}) collective-permute-start(f32[2,4,8,8,128]{4,3,2,1,0:T(8,128)S(1)} %collective-permute-done.1.refs_2_), channel_id=1, source_target_pairs={{0,1},{1,0},{2,3},{3,2},{4,5},{5,4},{6,7},{7,6},{8,9},{9,8},{10,11... | collective-permute-start | bytes 786440 | tf_op jit(solution)/shard_map/ppermute | solution.py:25
  21.6 2.8 %collective-permute-start.5 = (f32[2,4,8,8,128]{4,3,2,1,0:T(8,128)S(1)}, f32[2,4,8,8,128]{4,3,2,1,0:T(8,128)S(1)}, u32[]{:S(2)}, u32[]{:S(2)}) collective-permute-start(f32[2,4,8,8,128]{4,3,2,1,0:T(8,128)S(1)} %collective-permute-done.refs_1_), channel_id=1, source_target_pairs={{0,1},{1,0},{2,3},{3,2},{4,5},{5,4},{6,7},{7,6},{8,9},{9,8},{10,11... | collective-permute-start | bytes 786440 | tf_op jit(solution)/shard_map/ppermute | solution.py:25
  24.4 20.8 %copy-start.2 = (s32[2,1]{0,1:T(1,128)S(1)}, s32[2,1]{0,1:T(1,128)}, u32[]{:S(2)}) copy-start(s32[2,1]{0,1:T(1,128)} %param.6) | copy-start | bytes 28
  24.4 20.8 %copy-start.3 = (f32[2,1]{0,1:T(1,128)S(1)}, f32[2,1]{0,1:T(1,128)}, u32[]{:S(2)}) copy-start(f32[2,1]{0,1:T(1,128)} %param.7) | copy-start | bytes 28
  36.8 5.3 %collective-permute-start.9 = (f32[4,8,8,128]{3,2,1,0:T(8,128)S(1)}, f32[4,8,8,128]{3,2,1,0:T(8,128)S(1)}, u32[]{:S(2)}, u32[]{:S(2)}) collective-permute-start(f32[4,8,8,128]{3,2,1,0:T(8,128)S(1)} %get-tuple-element.8.refs_3_), channel_id=1, source_target_pairs={{16,32},{32,16},{48,64},{64,48},{80,96},{96,80},{112,128},{128,112... | collective-permute-start | bytes 393224 | tf_op jit(solution)/shard_map/ppermute | solution.py:25
  37.4 7.8 %collective-permute-start.8 = (f32[4,8,8,128]{3,2,1,0:T(8,128)S(1)}, f32[4,8,8,128]{3,2,1,0:T(8,128)S(1)}, u32[]{:S(2)}, u32[]{:S(2)}) collective-permute-start(f32[4,8,8,128]{3,2,1,0:T(8,128)S(1)} %get-tuple-element.8.refs_3_), channel_id=1, source_target_pairs={{0,16},{16,0},{32,48},{48,32},{64,80},{80,64},{96,112},{112,96},{1... | collective-permute-start | bytes 393224 | tf_op jit(solution)/shard_map/ppermute | solution.py:25
  45.9 7.9 %collective-permute-start.13 = (f32[4,8,8,128]{3,2,1,0:T(8,128)S(1)}, f32[4,8,8,128]{3,2,1,0:T(8,128)S(1)}, u32[]{:S(2)}, u32[]{:S(2)}) collective-permute-start(f32[4,8,8,128]{3,2,1,0:T(8,128)S(1)} %get-tuple-element.9.refs_0_), channel_id=1, source_target_pairs={{0,4},{1,5},{2,6},{3,7},{4,0},{5,1},{6,2},{7,3},{8,12},{9,13},{10,... | collective-permute-start | bytes 393224 | tf_op jit(solution)/shard_map/ppermute | solution.py:25
  46.7 7.2 %collective-permute-start.12 = (f32[4,8,8,128]{3,2,1,0:T(8,128)S(1)}, f32[4,8,8,128]{3,2,1,0:T(8,128)S(1)}, u32[]{:S(2)}, u32[]{:S(2)}) collective-permute-start(f32[4,8,8,128]{3,2,1,0:T(8,128)S(1)} %get-tuple-element.9.refs_0_), channel_id=1, source_target_pairs={{0,12},{1,13},{2,14},{3,15},{4,8},{5,9},{6,10},{7,11},{8,4},{9,5},... | collective-permute-start | bytes 393224 | tf_op jit(solution)/shard_map/ppermute | solution.py:25
  47.7 14.1 %collective-permute-start.14 = (f32[4,8,8,128]{3,2,1,0:T(8,128)S(1)}, f32[4,8,8,128]{3,2,1,0:T(8,128)S(1)}, u32[]{:S(2)}, u32[]{:S(2)}) collective-permute-start(f32[4,8,8,128]{3,2,1,0:T(8,128)S(1)} %get-tuple-element.9.refs_0_), channel_id=1, source_target_pairs={{0,1},{1,0},{2,3},{3,2},{4,5},{5,4},{6,7},{7,6},{8,9},{9,8},{10,11... | collective-permute-start | bytes 393224 | tf_op jit(solution)/shard_map/ppermute | solution.py:25
  49.4 6.6 %collective-permute-start.11 = (f32[4,8,8,128]{3,2,1,0:T(8,128)S(1)}, f32[4,8,8,128]{3,2,1,0:T(8,128)S(1)}, u32[]{:S(2)}, u32[]{:S(2)}) collective-permute-start(f32[4,8,8,128]{3,2,1,0:T(8,128)S(1)} %get-tuple-element.9.refs_0_), channel_id=1, source_target_pairs={{0,2},{1,3},{2,0},{3,1},{4,6},{5,7},{6,4},{7,5},{8,10},{9,11},{10,... | collective-permute-start | bytes 393224 | tf_op jit(solution)/shard_map/ppermute | solution.py:25
  52.2 8.4 %collective-permute-start.10 = (f32[4,8,8,128]{3,2,1,0:T(8,128)S(1)}, f32[4,8,8,128]{3,2,1,0:T(8,128)S(1)}, u32[]{:S(2)}, u32[]{:S(2)}) collective-permute-start(f32[4,8,8,128]{3,2,1,0:T(8,128)S(1)} %get-tuple-element.9.refs_0_), channel_id=1, source_target_pairs={{0,14},{1,15},{2,4},{3,5},{4,2},{5,3},{6,8},{7,9},{8,6},{9,7},{10,... | collective-permute-start | bytes 393224 | tf_op jit(solution)/shard_map/ppermute | solution.py:25
  53.8 7.9 %collective-permute-start.17 = (f32[4,8,8,128]{3,2,1,0:T(8,128)S(1)}, f32[4,8,8,128]{3,2,1,0:T(8,128)S(1)}, u32[]{:S(2)}, u32[]{:S(2)}) collective-permute-start(f32[4,8,8,128]{3,2,1,0:T(8,128)S(1)} %broadcast_select_fusion.1), channel_id=1, source_target_pairs={{0,1},{1,0},{2,3},{3,2},{4,5},{5,4},{6,7},{7,6},{8,9},{9,8},{10,11... | collective-permute-start | bytes 393224 | tf_op jit(solution)/shard_map/ppermute | solution.py:25
  56.0 5.8 %collective-permute-start.16 = (f32[4,8,8,128]{3,2,1,0:T(8,128)S(1)}, f32[4,8,8,128]{3,2,1,0:T(8,128)S(1)}, u32[]{:S(2)}, u32[]{:S(2)}) collective-permute-start(f32[4,8,8,128]{3,2,1,0:T(8,128)S(1)} %collective-permute-done.11.refs_2_), channel_id=1, source_target_pairs={{0,1},{1,0},{2,3},{3,2},{4,5},{5,4},{6,7},{7,6},{8,9},{9,8},{10,11... | collective-permute-start | bytes 393224 | tf_op jit(solution)/shard_map/ppermute | solution.py:25
  60.6 2.1 %collective-permute-start.15 = (f32[4,8,8,128]{3,2,1,0:T(8,128)S(1)}, f32[4,8,8,128]{3,2,1,0:T(8,128)S(1)}, u32[]{:S(2)}, u32[]{:S(2)}) collective-permute-start(f32[4,8,8,128]{3,2,1,0:T(8,128)S(1)} %collective-permute-done.10.refs_1_), channel_id=1, source_target_pairs={{0,1},{1,0},{2,3},{3,2},{4,5},{5,4},{6,7},{7,6},{8,9},{9,8},{10,11... | collective-permute-start | bytes 393224 | tf_op jit(solution)/shard_map/ppermute | solution.py:25
  75.0 6.6 %collective-permute-start.18 = (f32[4,8,8,128]{3,2,1,0:T(8,128)S(1)}, f32[4,8,8,128]{3,2,1,0:T(8,128)S(1)}, u32[]{:S(2)}, u32[]{:S(2)}) collective-permute-start(f32[4,8,8,128]{3,2,1,0:T(8,128)S(1)} %shard_map.62.own.refs_4_), channel_id=1, source_target_pairs={{16,0},{32,16},{48,32},{64,48},{80,64},{96,80},{112,96},{128,112},... | collective-permute-start | bytes 393224 | tf_op jit(solution)/shard_map/ppermute | solution.py:31
  82.5 29.4 %all-to-all-start = ((f32[256,2,128]{2,1,0:T(2,128)}), f32[256,2,128]{2,1,0:T(2,128)S(1)}, u32[]{:S(2)}, u32[]{:S(2)}) async-start(f32[256,2,128]{2,1,0:T(2,128)} %broadcast_in_dim.18), calls=%async_computation | async-start | bytes 524288 | tf_op jit(solution)/shard_map/all_to_all | solution.py:279
  96.2 8.4 %collective-permute-start.19 = (f32[4,8,8,128]{3,2,1,0:T(8,128)S(1)}, f32[4,8,8,128]{3,2,1,0:T(8,128)S(1)}, u32[]{:S(2)}, u32[]{:S(2)}) collective-permute-start(f32[4,8,8,128]{3,2,1,0:T(8,128)S(1)} %shard_map.62.own.refs_4_), channel_id=1, source_target_pairs={{0,16},{16,32},{32,48},{48,64},{64,80},{80,96},{96,112},{112,128},... | collective-permute-start | bytes 393224 | tf_op jit(solution)/shard_map/ppermute | solution.py:31

commit v3 on v2

--- a/solution.py
+++ b/solution.py
@@ -10,7 +10,6 @@
 SUBLANES = 8
 UNROLL = 4
 
-stiffness = 1.0
 time_step = 0.008
 epsilon = 1e-06
 
@@ -44,12 +43,14 @@
 
 
 def halo_pieces(own, index):
-    twos = [exchanged(own, "domain", partner(2)) for partner in (partner_across, partner_inside)]
-    fours = [exchanged(own, "domain", partner(4)) for partner in (partner_across, partner_inside)]
-    chosen = jnp.where(side(index, 4) == side(index, 1), fours[1], fours[0])
-    return [own, *twos, *fours] + [
-        exchanged(piece, "domain", partner_inside(1)) for piece in (own, *twos, chosen)
-    ]
+    straight = []
+    for partner, stride in zip((partner_across, partner_inside) * 2, (2, 2, 4, 4)):
+        straight.append(exchanged(own, "domain", partner(stride)))
+    *twos, across, inside = straight
+    chosen = jnp.where(side(index, 4) == side(index, 1), inside, across)
+    beside = exchanged(own, "domain", partner_inside(1))
+    others = [exchanged(piece, "domain", partner_inside(1)) for piece in (*twos, chosen)]
+    return [own, *straight, beside, *others]
 
 
 def slab_offsets(index):
@@ -216,7 +217,7 @@
     return jax.ShapeDtypeStruct(shape, jnp.float32)
 
 
-def per_device(field, mobility, lower, weights):
+def cycles(field, mobility, lower, weights):
     rows, depth, lanes = field.shape[1:]
     slab = (rows, depth // SUBLANES, SUBLANES, lanes)
     wide = (9 * rows,) + slab[1:]
@@ -267,7 +268,8 @@
             scratch_shapes=[window],
             compiler_params=PARAMS,
         )(index[None], *halo_pieces(phase, index), mobile)
-    right, left = passed_along(phase, -1), passed_along(phase, 1)
+    right = passed_along(phase, -1)
+    left = passed_along(phase, 1)
     mine = pl.pallas_call(
         gap_kernel,
         out_shape=shaped(CYCLES, lanes),
@@ -289,7 +291,7 @@
 
 def solution(mesh):
     return jax.shard_map(
-        per_device,
+        cycles,
         mesh=mesh,
         in_specs=(
             P("image", "domain", None, None),

time: 113 us -> 113 us (level)
  no operation moved by 1% of the time
where the time goes in v3:
time: 113 us
  starting transfers between devices  51.4 us (45%)
  waiting for transfers between devices  31.4 us (28%)
  Pallas kernels  26.9 us (24%)
  local copies, waits for them, and re-layouts  2.59 us (2%)
    ppermute x18, starting transfers between devices, exchanged(): lax.ppermute(value, axis, [(i, j) for i, j in pairs if 0 <= j < size])  33 us
    ppermute x18, waiting for transfers between devices, exchanged(): lax.ppermute(value, axis, [(i, j) for i, j in pairs if 0 <= j < size])  13.9 us
    all_to_all x1, starting transfers between devices, cycles(): gaps = lax.all_to_all(everyone, ('image', 'domain'), 0, 0)  13.8 us
    pallas_call x1, Pallas kernels, cycles(): pl.pallas_call(first_kernel, out_shape=(shaped(*slab), shaped(*wide)), in...  12.3 us
    pallas_call x1, Pallas kernels, cycles(): pl.pallas_call(later_kernel, out_shape=shaped(*slab), in_specs=[SMEM] + [...  12.3 us
    ppermute x2, waiting for transfers between devices, passed_along(): lax.ppermute(value, 'image', [(i, i + steps) for i in range(first, last)])  10.3 us
    all_to_all x1, waiting for transfers between devices, cycles(): gaps = lax.all_to_all(everyone, ('image', 'domain'), 0, 0)  7.24 us
    ppermute x2, starting transfers between devices, passed_along(): lax.ppermute(value, 'image', [(i, i + steps) for i in range(first, last)])  4.69 us
  transfers between devices with their start and end apart: 21, of which 10 were waited for; matrix products, arithmetic and copies ran while one was open for 0% of the time, Pallas kernels for 0%

profile of v3, /device:TPU:1, one launch (start us, length us, event | category | flops | bytes accessed | tf_op | source)
XLA Modules:
  0.0 113.2 jit_solution(11511002086183172873)
XLA Ops:
  0.6 0.0 copy-start
  0.6 0.9 copy-done
  1.5 0.0 copy-start.1
  1.5 0.9 copy-done.1
  2.4 0.4 shard_map.59.refs_0_
  2.8 2.2 %collective-permute-start.3 = (f32[2,4,8,8,128]{4,3,2,1,0:T(8,128)S(1)}, f32[2,4,8,8,128]{4,3,2,1,0:T(8,128)S(1)}, u32[]{:S(2)}, u32[]{:S(2)}) collective-permute-start(f32[2,4,8,8,128]{4,3,2,1,0:T(8,128)S(1)} %shard_map.59.refs_0_), channel_id=1, source_target_pairs={{0,4},{1,5},{2,6},{3,7},{4,0},{5,1},{6,2},{7,3},{8,12},{9,13},{10,... | collective-permute-start | bytes 786440 | tf_op jit(solution)/shard_map/ppermute | solution.py:24
  5.0 1.9 %collective-permute-start.2 = (f32[2,4,8,8,128]{4,3,2,1,0:T(8,128)S(1)}, f32[2,4,8,8,128]{4,3,2,1,0:T(8,128)S(1)}, u32[]{:S(2)}, u32[]{:S(2)}) collective-permute-start(f32[2,4,8,8,128]{4,3,2,1,0:T(8,128)S(1)} %shard_map.59.refs_0_), channel_id=1, source_target_pairs={{0,12},{1,13},{2,14},{3,15},{4,8},{5,9},{6,10},{7,11},{8,4},{9,5},... | collective-permute-start | bytes 786440 | tf_op jit(solution)/shard_map/ppermute | solution.py:24
  6.9 2.7 %collective-permute-start.1 = (f32[2,4,8,8,128]{4,3,2,1,0:T(8,128)S(1)}, f32[2,4,8,8,128]{4,3,2,1,0:T(8,128)S(1)}, u32[]{:S(2)}, u32[]{:S(2)}) collective-permute-start(f32[2,4,8,8,128]{4,3,2,1,0:T(8,128)S(1)} %shard_map.59.refs_0_), channel_id=1, source_target_pairs={{0,2},{1,3},{2,0},{3,1},{4,6},{5,7},{6,4},{7,5},{8,10},{9,11},{10,... | collective-permute-start | bytes 786440 | tf_op jit(solution)/shard_map/ppermute | solution.py:24
  9.7 0.7 collective-permute-start
  10.4 2.0 %collective-permute-start.4 = (f32[2,4,8,8,128]{4,3,2,1,0:T(8,128)S(1)}, f32[2,4,8,8,128]{4,3,2,1,0:T(8,128)S(1)}, u32[]{:S(2)}, u32[]{:S(2)}) collective-permute-start(f32[2,4,8,8,128]{4,3,2,1,0:T(8,128)S(1)} %shard_map.59.refs_0_), channel_id=1, source_target_pairs={{0,1},{1,0},{2,3},{3,2},{4,5},{5,4},{6,7},{7,6},{8,9},{9,8},{10,11... | collective-permute-start | bytes 786440 | tf_op jit(solution)/shard_map/ppermute | solution.py:24
  12.4 0.0 collective-permute-done.3.refs_4_
  12.4 0.5 collective-permute-done.2.refs_3_
  12.9 2.1 %collective-permute-start.7 = (f32[2,4,8,8,128]{4,3,2,1,0:T(8,128)S(1)}, f32[2,4,8,8,128]{4,3,2,1,0:T(8,128)S(1)}, u32[]{:S(2)}, u32[]{:S(2)}) collective-permute-start(f32[2,4,8,8,128]{4,3,2,1,0:T(8,128)S(1)} %broadcast_select_fusion), channel_id=1, source_target_pairs={{0,1},{1,0},{2,3},{3,2},{4,5},{5,4},{6,7},{7,6},{8,9},{9,8},{10,11... | collective-permute-start | bytes 786440 | tf_op jit(solution)/shard_map/ppermute | solution.py:24
  15.1 0.0 collective-permute-done.1.refs_2_
  15.1 3.8 %collective-permute-start.6 = (f32[2,4,8,8,128]{4,3,2,1,0:T(8,128)S(1)}, f32[2,4,8,8,128]{4,3,2,1,0:T(8,128)S(1)}, u32[]{:S(2)}, u32[]{:S(2)}) collective-permute-start(f32[2,4,8,8,128]{4,3,2,1,0:T(8,128)S(1)} %collective-permute-done.1.refs_2_), channel_id=1, source_target_pairs={{0,1},{1,0},{2,3},{3,2},{4,5},{5,4},{6,7},{7,6},{8,9},{9,8},{10,11... | collective-permute-start | bytes 786440 | tf_op jit(solution)/shard_map/ppermute | solution.py:24
  18.9 2.8 %collective-permute-done.refs_1_ = f32[2,4,8,8,128]{4,3,2,1,0:T(8,128)S(1)} collective-permute-done((f32[2,4,8,8,128]{4,3,2,1,0:T(8,128)S(1)}, f32[2,4,8,8,128]{4,3,2,1,0:T(8,128)S(1)}, u32[]{:S(2)}, u32[]{:S(2)}) %collective-permute-start) | collective-permute-done | bytes 262176 | tf_op jit(solution)/shard_map/ppermute | solution.py:24
  21.6 1.7 %collective-permute-start.5 = (f32[2,4,8,8,128]{4,3,2,1,0:T(8,128)S(1)}, f32[2,4,8,8,128]{4,3,2,1,0:T(8,128)S(1)}, u32[]{:S(2)}, u32[]{:S(2)}) collective-permute-start(f32[2,4,8,8,128]{4,3,2,1,0:T(8,128)S(1)} %collective-permute-done.refs_1_), channel_id=1, source_target_pairs={{0,1},{1,0},{2,3},{3,2},{4,5},{5,4},{6,7},{7,6},{8,9},{9,8},{10,11... | collective-permute-start | bytes 786440 | tf_op jit(solution)/shard_map/ppermute | solution.py:24
  23.3 0.0 collective-permute-done.4.refs_5_
  23.3 0.0 collective-permute-done.7.refs_8_
  23.3 0.0 collective-permute-done.6.refs_7_
  23.3 1.1 %collective-permute-done.5.refs_6_ = f32[2,4,8,8,128]{4,3,2,1,0:T(8,128)S(1)} collective-permute-done((f32[2,4,8,8,128]{4,3,2,1,0:T(8,128)S(1)}, f32[2,4,8,8,128]{4,3,2,1,0:T(8,128)S(1)}, u32[]{:S(2)}, u32[]{:S(2)}) %collective-permute-start.5) | collective-permute-done | bytes 262176 | tf_op jit(solution)/shard_map/ppermute | solution.py:24
  24.4 0.0 copy-start.2
  24.4 0.0 copy-start.3
  24.4 12.3 %shard_map.60 = (f32[4,8,8,128]{3,2,1,0:T(8,128)S(1)}, f32[36,8,8,128]{3,2,1,0:T(8,128)S(1)}) custom-call(s32[1]{0:T(128)} %bitcast.3.index_ref, f32[2,4,8,8,128]{4,3,2,1,0:T(8,128)S(1)} %shard_map.59.refs_0_, f32[2,4,8,8,128]{4,3,2,1,0:T(8,128)S(1)} %collective-permute-done.refs_1_, f32[2,4,8,8,128]{4,3,2,1,0:T(8,128)S(1)} %collective-permute-done.1.refs_2_, ...), custom_call_target="tpu_custom_call" | custom-call | tf_op jit(solution)/shard_map/pallas_call | solution.py:242
  36.8 0.7 collective-permute-start.9
  37.4 4.6 %collective-permute-start.8 = (f32[4,8,8,128]{3,2,1,0:T(8,128)S(1)}, f32[4,8,8,128]{3,2,1,0:T(8,128)S(1)}, u32[]{:S(2)}, u32[]{:S(2)}) collective-permute-start(f32[4,8,8,128]{3,2,1,0:T(8,128)S(1)} %get-tuple-element.8.refs_3_), channel_id=1, source_target_pairs={{0,16},{16,0},{32,48},{48,32},{64,80},{80,64},{96,112},{112,96},{1... | collective-permute-start | bytes 393224 | tf_op jit(solution)/shard_map/ppermute | solution.py:24
  42.0 0.0 collective-permute-done.9.refs_5_
  42.0 3.2 %collective-permute-done.8.refs_4_ = f32[4,8,8,128]{3,2,1,0:T(8,128)S(1)} collective-permute-done((f32[4,8,8,128]{3,2,1,0:T(8,128)S(1)}, f32[4,8,8,128]{3,2,1,0:T(8,128)S(1)}, u32[]{:S(2)}, u32[]{:S(2)}) %collective-permute-start.8) | collective-permute-done | bytes 131104 | tf_op jit(solution)/shard_map/ppermute | solution.py:24
  45.3 0.0 copy-done.2
  45.3 0.0 copy-done.3
  45.3 0.6 shard_map.61
  45.9 0.8 collective-permute-start.13
  46.7 1.0 collective-permute-start.12
  47.7 1.8 %collective-permute-start.14 = (f32[4,8,8,128]{3,2,1,0:T(8,128)S(1)}, f32[4,8,8,128]{3,2,1,0:T(8,128)S(1)}, u32[]{:S(2)}, u32[]{:S(2)}) collective-permute-start(f32[4,8,8,128]{3,2,1,0:T(8,128)S(1)} %get-tuple-element.9.refs_0_), channel_id=1, source_target_pairs={{0,1},{1,0},{2,3},{3,2},{4,5},{5,4},{6,7},{7,6},{8,9},{9,8},{10,11... | collective-permute-start | bytes 393224 | tf_op jit(solution)/shard_map/ppermute | solution.py:24
  49.4 2.8 %collective-permute-start.11 = (f32[4,8,8,128]{3,2,1,0:T(8,128)S(1)}, f32[4,8,8,128]{3,2,1,0:T(8,128)S(1)}, u32[]{:S(2)}, u32[]{:S(2)}) collective-permute-start(f32[4,8,8,128]{3,2,1,0:T(8,128)S(1)} %get-tuple-element.9.refs_0_), channel_id=1, source_target_pairs={{0,2},{1,3},{2,0},{3,1},{4,6},{5,7},{6,4},{7,5},{8,10},{9,11},{10,... | collective-permute-start | bytes 393224 | tf_op jit(solution)/shard_map/ppermute | solution.py:24
  52.2 1.6 %collective-permute-start.10 = (f32[4,8,8,128]{3,2,1,0:T(8,128)S(1)}, f32[4,8,8,128]{3,2,1,0:T(8,128)S(1)}, u32[]{:S(2)}, u32[]{:S(2)}) collective-permute-start(f32[4,8,8,128]{3,2,1,0:T(8,128)S(1)} %get-tuple-element.9.refs_0_), channel_id=1, source_target_pairs={{0,14},{1,15},{2,4},{3,5},{4,2},{5,3},{6,8},{7,9},{8,6},{9,7},{10,... | collective-permute-start | bytes 393224 | tf_op jit(solution)/shard_map/ppermute | solution.py:24
  53.8 0.0 collective-permute-done.13.refs_4_
  53.8 0.0 collective-permute-done.12.refs_3_
  53.8 0.6 collective-permute-start.17
  54.5 1.5 %collective-permute-done.11.refs_2_ = f32[4,8,8,128]{3,2,1,0:T(8,128)S(1)} collective-permute-done((f32[4,8,8,128]{3,2,1,0:T(8,128)S(1)}, f32[4,8,8,128]{3,2,1,0:T(8,128)S(1)}, u32[]{:S(2)}, u32[]{:S(2)}) %collective-permute-start.11) | collective-permute-done | bytes 131104 | tf_op jit(solution)/shard_map/ppermute | solution.py:24
  56.0 0.9 collective-permute-start.16
  56.9 3.7 %collective-permute-done.10.refs_1_ = f32[4,8,8,128]{3,2,1,0:T(8,128)S(1)} collective-permute-done((f32[4,8,8,128]{3,2,1,0:T(8,128)S(1)}, f32[4,8,8,128]{3,2,1,0:T(8,128)S(1)}, u32[]{:S(2)}, u32[]{:S(2)}) %collective-permute-start.10) | collective-permute-done | bytes 131104 | tf_op jit(solution)/shard_map/ppermute | solution.py:24
  60.6 1.1 %collective-permute-start.15 = (f32[4,8,8,128]{3,2,1,0:T(8,128)S(1)}, f32[4,8,8,128]{3,2,1,0:T(8,128)S(1)}, u32[]{:S(2)}, u32[]{:S(2)}) collective-permute-start(f32[4,8,8,128]{3,2,1,0:T(8,128)S(1)} %collective-permute-done.10.refs_1_), channel_id=1, source_target_pairs={{0,1},{1,0},{2,3},{3,2},{4,5},{5,4},{6,7},{7,6},{8,9},{9,8},{10,11... | collective-permute-start | bytes 393224 | tf_op jit(solution)/shard_map/ppermute | solution.py:24
  61.7 0.0 collective-permute-done.14.refs_5_
  61.7 0.0 collective-permute-done.17.refs_8_
  61.8 0.0 collective-permute-done.16.refs_7_
  61.8 1.0 collective-permute-done.15.refs_6_
  62.7 12.3 %shard_map.62.own.refs_4_ = f32[4,8,8,128]{3,2,1,0:T(8,128)S(1)} custom-call(s32[1]{0:T(128)} %bitcast.3.index_ref, f32[4,8,8,128]{3,2,1,0:T(8,128)S(1)} %get-tuple-element.9.refs_0_, f32[4,8,8,128]{3,2,1,0:T(8,128)S(1)} %collective-permute-done.10.refs_1_, f32[4,8,8,128]{3,2,1,0:T(8,128)S(1)} %collective-permute-done.11.refs_2_, ...), custom_call_target="tpu_custom_call" | custom-call | tf_op jit(solution)/shard_map/pallas_call | solution.py:263
  75.0 1.3 %collective-permute-start.18 = (f32[4,8,8,128]{3,2,1,0:T(8,128)S(1)}, f32[4,8,8,128]{3,2,1,0:T(8,128)S(1)}, u32[]{:S(2)}, u32[]{:S(2)}) collective-permute-start(f32[4,8,8,128]{3,2,1,0:T(8,128)S(1)} %shard_map.62.own.refs_4_), channel_id=1, source_target_pairs={{16,0},{32,16},{48,32},{64,48},{80,64},{96,80},{112,96},{128,112},... | collective-permute-start | bytes 393224 | tf_op jit(solution)/shard_map/ppermute | solution.py:30
  76.3 5.3 %collective-permute-done.18.right.refs_6_ = f32[4,8,8,128]{3,2,1,0:T(8,128)S(1)} collective-permute-done((f32[4,8,8,128]{3,2,1,0:T(8,128)S(1)}, f32[4,8,8,128]{3,2,1,0:T(8,128)S(1)}, u32[]{:S(2)}, u32[]{:S(2)}) %collective-permute-start.18) | collective-permute-done | bytes 131104 | tf_op jit(solution)/shard_map/ppermute | solution.py:30
  81.7 0.8 broadcast_in_dim.18
  82.5 13.8 %all-to-all-start = ((f32[256,2,128]{2,1,0:T(2,128)}), f32[256,2,128]{2,1,0:T(2,128)S(1)}, u32[]{:S(2)}, u32[]{:S(2)}) async-start(f32[256,2,128]{2,1,0:T(2,128)} %broadcast_in_dim.18), calls=%async_computation | async-start | bytes 524288 | tf_op jit(solution)/shard_map/all_to_all | solution.py:281
  96.2 3.4 %collective-permute-start.19 = (f32[4,8,8,128]{3,2,1,0:T(8,128)S(1)}, f32[4,8,8,128]{3,2,1,0:T(8,128)S(1)}, u32[]{:S(2)}, u32[]{:S(2)}) collective-permute-start(f32[4,8,8,128]{3,2,1,0:T(8,128)S(1)} %shard_map.62.own.refs_4_), channel_id=1, source_target_pairs={{0,16},{16,32},{32,48},{48,64},{64,80},{80,96},{96,112},{112,128},... | collective-permute-start | bytes 393224 | tf_op jit(solution)/shard_map/ppermute | solution.py:30
  99.6 5.0 %collective-permute-done.19.refs_5_ = f32[4,8,8,128]{3,2,1,0:T(8,128)S(1)} collective-permute-done((f32[4,8,8,128]{3,2,1,0:T(8,128)S(1)}, f32[4,8,8,128]{3,2,1,0:T(8,128)S(1)}, u32[]{:S(2)}, u32[]{:S(2)}) %collective-permute-start.19) | collective-permute-done | bytes 131104 | tf_op jit(solution)/shard_map/ppermute | solution.py:30
  104.7 7.2 %all-to-all-done.refs_3_ = f32[256,2,128]{2,1,0:T(2,128)S(1)} async-done(((f32[256,2,128]{2,1,0:T(2,128)}), f32[256,2,128]{2,1,0:T(2,128)S(1)}, u32[]{:S(2)}, u32[]{:S(2)}) %all-to-all-start) | async-done | bytes 262176 | tf_op jit(solution)/shard_map/all_to_all | solution.py:281
  111.9 1.3 %shard_map.64 = (f32[4,64,128]{2,1,0:T(8,128)}, f32[1,2]{1,0:T(1,128)}) custom-call(s32[1]{0:T(128)} %bitcast.refs_0_, s32[1,2]{1,0:T(1,128)S(1)} %bitcast.9, f32[1,2]{1,0:T(1,128)S(1)} %bitcast.11, f32[256,2,128]{2,1,0:T(2,128)S(1)} %all-to-all-done.refs_3_, f32[4,8,8,128]{3,2,1,0:T(8,128)S(1)} %shard_map.62.own.refs_4_, ...), custom_call_target="tpu_custom_call" | custom-call | tf_op jit(solution)/shard_map/pallas_call | solution.py:282
  (3 shorter events, 0.1 us)
Async XLA Ops:
  0.6 0.9 copy-start
  1.5 0.9 copy-start.1
  2.8 9.6 %collective-permute-start.3 = (f32[2,4,8,8,128]{4,3,2,1,0:T(8,128)S(1)}, f32[2,4,8,8,128]{4,3,2,1,0:T(8,128)S(1)}, u32[]{:S(2)}, u32[]{:S(2)}) collective-permute-start(f32[2,4,8,8,128]{4,3,2,1,0:T(8,128)S(1)} %shard_map.59.refs_0_), channel_id=1, source_target_pairs={{0,4},{1,5},{2,6},{3,7},{4,0},{5,1},{6,2},{7,3},{8,12},{9,13},{10,... | collective-permute-start | bytes 786440 | tf_op jit(solution)/shard_map/ppermute | solution.py:24
  5.0 7.9 %collective-permute-start.2 = (f32[2,4,8,8,128]{4,3,2,1,0:T(8,128)S(1)}, f32[2,4,8,8,128]{4,3,2,1,0:T(8,128)S(1)}, u32[]{:S(2)}, u32[]{:S(2)}) collective-permute-start(f32[2,4,8,8,128]{4,3,2,1,0:T(8,128)S(1)} %shard_map.59.refs_0_), channel_id=1, source_target_pairs={{0,12},{1,13},{2,14},{3,15},{4,8},{5,9},{6,10},{7,11},{8,4},{9,5},... | collective-permute-start | bytes 786440 | tf_op jit(solution)/shard_map/ppermute | solution.py:24
  6.9 8.2 %collective-permute-start.1 = (f32[2,4,8,8,128]{4,3,2,1,0:T(8,128)S(1)}, f32[2,4,8,8,128]{4,3,2,1,0:T(8,128)S(1)}, u32[]{:S(2)}, u32[]{:S(2)}) collective-permute-start(f32[2,4,8,8,128]{4,3,2,1,0:T(8,128)S(1)} %shard_map.59.refs_0_), channel_id=1, source_target_pairs={{0,2},{1,3},{2,0},{3,1},{4,6},{5,7},{6,4},{7,5},{8,10},{9,11},{10,... | collective-permute-start | bytes 786440 | tf_op jit(solution)/shard_map/ppermute | solution.py:24
  9.7 11.9 %collective-permute-start = (f32[2,4,8,8,128]{4,3,2,1,0:T(8,128)S(1)}, f32[2,4,8,8,128]{4,3,2,1,0:T(8,128)S(1)}, u32[]{:S(2)}, u32[]{:S(2)}) collective-permute-start(f32[2,4,8,8,128]{4,3,2,1,0:T(8,128)S(1)} %shard_map.59.refs_0_), channel_id=1, source_target_pairs={{0,14},{1,15},{2,4},{3,5},{4,2},{5,3},{6,8},{7,9},{8,6},{9,7},{10,... | collective-permute-start | bytes 786440 | tf_op jit(solution)/shard_map/ppermute | solution.py:24
  10.4 12.9 %collective-permute-start.4 = (f32[2,4,8,8,128]{4,3,2,1,0:T(8,128)S(1)}, f32[2,4,8,8,128]{4,3,2,1,0:T(8,128)S(1)}, u32[]{:S(2)}, u32[]{:S(2)}) collective-permute-start(f32[2,4,8,8,128]{4,3,2,1,0:T(8,128)S(1)} %shard_map.59.refs_0_), channel_id=1, source_target_pairs={{0,1},{1,0},{2,3},{3,2},{4,5},{5,4},{6,7},{7,6},{8,9},{9,8},{10,11... | collective-permute-start | bytes 786440 | tf_op jit(solution)/shard_map/ppermute | solution.py:24
  12.9 10.3 %collective-permute-start.7 = (f32[2,4,8,8,128]{4,3,2,1,0:T(8,128)S(1)}, f32[2,4,8,8,128]{4,3,2,1,0:T(8,128)S(1)}, u32[]{:S(2)}, u32[]{:S(2)}) collective-permute-start(f32[2,4,8,8,128]{4,3,2,1,0:T(8,128)S(1)} %broadcast_select_fusion), channel_id=1, source_target_pairs={{0,1},{1,0},{2,3},{3,2},{4,5},{5,4},{6,7},{7,6},{8,9},{9,8},{10,11... | collective-permute-start | bytes 786440 | tf_op jit(solution)/shard_map/ppermute | solution.py:24
  15.1 8.2 %collective-permute-start.6 = (f32[2,4,8,8,128]{4,3,2,1,0:T(8,128)S(1)}, f32[2,4,8,8,128]{4,3,2,1,0:T(8,128)S(1)}, u32[]{:S(2)}, u32[]{:S(2)}) collective-permute-start(f32[2,4,8,8,128]{4,3,2,1,0:T(8,128)S(1)} %collective-permute-done.1.refs_2_), channel_id=1, source_target_pairs={{0,1},{1,0},{2,3},{3,2},{4,5},{5,4},{6,7},{7,6},{8,9},{9,8},{10,11... | collective-permute-start | bytes 786440 | tf_op jit(solution)/shard_map/ppermute | solution.py:24
  21.6 2.8 %collective-permute-start.5 = (f32[2,4,8,8,128]{4,3,2,1,0:T(8,128)S(1)}, f32[2,4,8,8,128]{4,3,2,1,0:T(8,128)S(1)}, u32[]{:S(2)}, u32[]{:S(2)}) collective-permute-start(f32[2,4,8,8,128]{4,3,2,1,0:T(8,128)S(1)} %collective-permute-done.refs_1_), channel_id=1, source_target_pairs={{0,1},{1,0},{2,3},{3,2},{4,5},{5,4},{6,7},{7,6},{8,9},{9,8},{10,11... | collective-permute-start | bytes 786440 | tf_op jit(solution)/shard_map/ppermute | solution.py:24
  24.4 20.8 %copy-start.2 = (s32[2,1]{0,1:T(1,128)S(1)}, s32[2,1]{0,1:T(1,128)}, u32[]{:S(2)}) copy-start(s32[2,1]{0,1:T(1,128)} %param.6) | copy-start | bytes 28
  24.4 20.8 %copy-start.3 = (f32[2,1]{0,1:T(1,128)S(1)}, f32[2,1]{0,1:T(1,128)}, u32[]{:S(2)}) copy-start(f32[2,1]{0,1:T(1,128)} %param.7) | copy-start | bytes 28
  36.8 5.3 %collective-permute-start.9 = (f32[4,8,8,128]{3,2,1,0:T(8,128)S(1)}, f32[4,8,8,128]{3,2,1,0:T(8,128)S(1)}, u32[]{:S(2)}, u32[]{:S(2)}) collective-permute-start(f32[4,8,8,128]{3,2,1,0:T(8,128)S(1)} %get-tuple-element.8.refs_3_), channel_id=1, source_target_pairs={{16,32},{32,16},{48,64},{64,48},{80,96},{96,80},{112,128},{128,112... | collective-permute-start | bytes 393224 | tf_op jit(solution)/shard_map/ppermute | solution.py:24
  37.4 7.8 %collective-permute-start.8 = (f32[4,8,8,128]{3,2,1,0:T(8,128)S(1)}, f32[4,8,8,128]{3,2,1,0:T(8,128)S(1)}, u32[]{:S(2)}, u32[]{:S(2)}) collective-permute-start(f32[4,8,8,128]{3,2,1,0:T(8,128)S(1)} %get-tuple-element.8.refs_3_), channel_id=1, source_target_pairs={{0,16},{16,0},{32,48},{48,32},{64,80},{80,64},{96,112},{112,96},{1... | collective-permute-start | bytes 393224 | tf_op jit(solution)/shard_map/ppermute | solution.py:24
  45.9 7.9 %collective-permute-start.13 = (f32[4,8,8,128]{3,2,1,0:T(8,128)S(1)}, f32[4,8,8,128]{3,2,1,0:T(8,128)S(1)}, u32[]{:S(2)}, u32[]{:S(2)}) collective-permute-start(f32[4,8,8,128]{3,2,1,0:T(8,128)S(1)} %get-tuple-element.9.refs_0_), channel_id=1, source_target_pairs={{0,4},{1,5},{2,6},{3,7},{4,0},{5,1},{6,2},{7,3},{8,12},{9,13},{10,... | collective-permute-start | bytes 393224 | tf_op jit(solution)/shard_map/ppermute | solution.py:24
  46.7 7.2 %collective-permute-start.12 = (f32[4,8,8,128]{3,2,1,0:T(8,128)S(1)}, f32[4,8,8,128]{3,2,1,0:T(8,128)S(1)}, u32[]{:S(2)}, u32[]{:S(2)}) collective-permute-start(f32[4,8,8,128]{3,2,1,0:T(8,128)S(1)} %get-tuple-element.9.refs_0_), channel_id=1, source_target_pairs={{0,12},{1,13},{2,14},{3,15},{4,8},{5,9},{6,10},{7,11},{8,4},{9,5},... | collective-permute-start | bytes 393224 | tf_op jit(solution)/shard_map/ppermute | solution.py:24
  47.7 14.1 %collective-permute-start.14 = (f32[4,8,8,128]{3,2,1,0:T(8,128)S(1)}, f32[4,8,8,128]{3,2,1,0:T(8,128)S(1)}, u32[]{:S(2)}, u32[]{:S(2)}) collective-permute-start(f32[4,8,8,128]{3,2,1,0:T(8,128)S(1)} %get-tuple-element.9.refs_0_), channel_id=1, source_target_pairs={{0,1},{1,0},{2,3},{3,2},{4,5},{5,4},{6,7},{7,6},{8,9},{9,8},{10,11... | collective-permute-start | bytes 393224 | tf_op jit(solution)/shard_map/ppermute | solution.py:24
  49.4 6.6 %collective-permute-start.11 = (f32[4,8,8,128]{3,2,1,0:T(8,128)S(1)}, f32[4,8,8,128]{3,2,1,0:T(8,128)S(1)}, u32[]{:S(2)}, u32[]{:S(2)}) collective-permute-start(f32[4,8,8,128]{3,2,1,0:T(8,128)S(1)} %get-tuple-element.9.refs_0_), channel_id=1, source_target_pairs={{0,2},{1,3},{2,0},{3,1},{4,6},{5,7},{6,4},{7,5},{8,10},{9,11},{10,... | collective-permute-start | bytes 393224 | tf_op jit(solution)/shard_map/ppermute | solution.py:24
  52.2 8.4 %collective-permute-start.10 = (f32[4,8,8,128]{3,2,1,0:T(8,128)S(1)}, f32[4,8,8,128]{3,2,1,0:T(8,128)S(1)}, u32[]{:S(2)}, u32[]{:S(2)}) collective-permute-start(f32[4,8,8,128]{3,2,1,0:T(8,128)S(1)} %get-tuple-element.9.refs_0_), channel_id=1, source_target_pairs={{0,14},{1,15},{2,4},{3,5},{4,2},{5,3},{6,8},{7,9},{8,6},{9,7},{10,... | collective-permute-start | bytes 393224 | tf_op jit(solution)/shard_map/ppermute | solution.py:24
  53.8 7.9 %collective-permute-start.17 = (f32[4,8,8,128]{3,2,1,0:T(8,128)S(1)}, f32[4,8,8,128]{3,2,1,0:T(8,128)S(1)}, u32[]{:S(2)}, u32[]{:S(2)}) collective-permute-start(f32[4,8,8,128]{3,2,1,0:T(8,128)S(1)} %broadcast_select_fusion.1), channel_id=1, source_target_pairs={{0,1},{1,0},{2,3},{3,2},{4,5},{5,4},{6,7},{7,6},{8,9},{9,8},{10,11... | collective-permute-start | bytes 393224 | tf_op jit(solution)/shard_map/ppermute | solution.py:24
  56.0 5.8 %collective-permute-start.16 = (f32[4,8,8,128]{3,2,1,0:T(8,128)S(1)}, f32[4,8,8,128]{3,2,1,0:T(8,128)S(1)}, u32[]{:S(2)}, u32[]{:S(2)}) collective-permute-start(f32[4,8,8,128]{3,2,1,0:T(8,128)S(1)} %collective-permute-done.11.refs_2_), channel_id=1, source_target_pairs={{0,1},{1,0},{2,3},{3,2},{4,5},{5,4},{6,7},{7,6},{8,9},{9,8},{10,11... | collective-permute-start | bytes 393224 | tf_op jit(solution)/shard_map/ppermute | solution.py:24
  60.6 2.1 %collective-permute-start.15 = (f32[4,8,8,128]{3,2,1,0:T(8,128)S(1)}, f32[4,8,8,128]{3,2,1,0:T(8,128)S(1)}, u32[]{:S(2)}, u32[]{:S(2)}) collective-permute-start(f32[4,8,8,128]{3,2,1,0:T(8,128)S(1)} %collective-permute-done.10.refs_1_), channel_id=1, source_target_pairs={{0,1},{1,0},{2,3},{3,2},{4,5},{5,4},{6,7},{7,6},{8,9},{9,8},{10,11... | collective-permute-start | bytes 393224 | tf_op jit(solution)/shard_map/ppermute | solution.py:24
  75.0 6.6 %collective-permute-start.18 = (f32[4,8,8,128]{3,2,1,0:T(8,128)S(1)}, f32[4,8,8,128]{3,2,1,0:T(8,128)S(1)}, u32[]{:S(2)}, u32[]{:S(2)}) collective-permute-start(f32[4,8,8,128]{3,2,1,0:T(8,128)S(1)} %shard_map.62.own.refs_4_), channel_id=1, source_target_pairs={{16,0},{32,16},{48,32},{64,48},{80,64},{96,80},{112,96},{128,112},... | collective-permute-start | bytes 393224 | tf_op jit(solution)/shard_map/ppermute | solution.py:30
  82.5 29.4 %all-to-all-start = ((f32[256,2,128]{2,1,0:T(2,128)}), f32[256,2,128]{2,1,0:T(2,128)S(1)}, u32[]{:S(2)}, u32[]{:S(2)}) async-start(f32[256,2,128]{2,1,0:T(2,128)} %broadcast_in_dim.18), calls=%async_computation | async-start | bytes 524288 | tf_op jit(solution)/shard_map/all_to_all | solution.py:281
  96.2 8.4 %collective-permute-start.19 = (f32[4,8,8,128]{3,2,1,0:T(8,128)S(1)}, f32[4,8,8,128]{3,2,1,0:T(8,128)S(1)}, u32[]{:S(2)}, u32[]{:S(2)}) collective-permute-start(f32[4,8,8,128]{3,2,1,0:T(8,128)S(1)} %shard_map.62.own.refs_4_), channel_id=1, source_target_pairs={{0,16},{16,32},{32,48},{48,64},{64,80},{80,96},{96,112},{112,128},... | collective-permute-start | bytes 393224 | tf_op jit(solution)/shard_map/ppermute | solution.py:30

commit v4 on v3

--- a/solution.py
+++ b/solution.py
@@ -1,5 +1,6 @@
 import jax
 import jax.numpy as jnp
+import numpy as np
 from jax import lax
 from jax.experimental import pallas as pl
 from jax.experimental.pallas import tpu as pltpu
@@ -9,6 +10,7 @@
 CYCLES = 2
 SUBLANES = 8
 UNROLL = 4
+CHUNK = 8
 
 time_step = 0.008
 epsilon = 1e-06
@@ -87,36 +89,52 @@
     return pltpu.roll(value, offset % value.shape[2], 2)
 
 
-def potential_and_motion(field, mobile, row):
-    here = field[row]
-    square = here * here
-    around = field[row - 1] + field[row + 1]
-    for shifted in (y_shifted, z_shifted):
-        around = around + (shifted(here, 1) + shifted(here, -1))
-    potential = here * (square + 5.0) - around
-    motion = mobile[row] / (1.0 + square)
-    return potential, motion
-
-
-def take_steps(field, mobile, length):
+def z_neighbours(lanes):
+    before = np.roll(np.eye(lanes), 1, axis=1)
+    return jnp.asarray(np.tile(np.concatenate([before + before.T, before], axis=1), (2, 1)), jnp.bfloat16)
+
+
+def gather(field, around, before, matrix, row, count):
+    here = field[pl.ds(row, count)]
+    lanes = here.shape[-1]
+    flat = here.reshape(-1, lanes)
+    high = flat.astype(jnp.bfloat16)
+    low = (flat - high.astype(jnp.float32)).astype(jnp.bfloat16)
+    found = jnp.dot(
+        jnp.concatenate([high, low], axis=1), matrix[...], preferred_element_type=jnp.float32
+    )
+    around[pl.ds(row, count)] = found[:, :lanes].reshape(here.shape)
+    before[pl.ds(row, count)] = found[:, lanes:].reshape(here.shape)
+
+
+def take_steps(field, mobile, mobile_before, matrix, z_around, z_before, length):
+    def at(row):
+        here, before = field[row], z_before[row]
+        square = here * here
+        around = (field[row - 1] + field[row + 1]) + (y_shifted(here, 1) + y_shifted(here, -1))
+        potential = here * (square + 5.0) - (around + z_around[row])
+        motion = mobile[row] / (1.0 + square)
+        return potential, motion, mobile_before[row] / (1.0 + before * before)
+
+    def one_row(row, carried):
+        potential, motion, motion_before, inflow = carried
+        ahead = at(row + 1)
+        outflow = (motion + ahead[1]) * (ahead[0] - potential)
+        change = outflow - inflow
+        flow = (motion + y_shifted(motion, 1)) * (potential - y_shifted(potential, 1))
+        change = change + (y_shifted(flow, -1) - flow)
+        flow = (motion + motion_before) * (potential - z_shifted(potential, 1))
+        change = change + (z_shifted(flow, -1) - flow)
+        field[row] = field[row] + change
+        return (*ahead, outflow)
+
     for step in range(STEPS):
         first, last = 2 * step + 2, length - 2 * step - 2
-        before = potential_and_motion(field, mobile, first - 1)
-        now = potential_and_motion(field, mobile, first)
+        for row in range(first - 1, last + 1, CHUNK):
+            gather(field, z_around, z_before, matrix, row, min(CHUNK, last + 1 - row))
+        before, now = at(first - 1), at(first)
         inflow = (before[1] + now[1]) * (now[0] - before[0])
-
-        def one_row(row, carried):
-            potential, motion, inflow = carried
-            ahead = potential_and_motion(field, mobile, row + 1)
-            outflow = (motion + ahead[1]) * (ahead[0] - potential)
-            change = outflow - inflow
-            for shifted in (y_shifted, z_shifted):
-                flow = (motion + shifted(motion, 1)) * (potential - shifted(potential, 1))
-                change = change + (shifted(flow, -1) - flow)
-            field[row] = field[row] + change
-            return ahead[0], ahead[1], outflow
-
-        lax.fori_loop(first, last, one_row, (now[0], now[1], inflow), unroll=UNROLL)
+        lax.fori_loop(first, last, one_row, (*now, inflow), unroll=UNROLL)
 
 
 def pack_kernel(field, mobility, out, held, semaphores):
@@ -133,19 +151,25 @@
 
 
 def first_kernel(index_ref, *refs):
-    pieces, out, mobile, window = refs[:9], *refs[9:]
-    rows = out.shape[0]
+    pieces, matrix, out, mobile, mobile_before, *scratch = refs[:9], *refs[9:]
+    window, rows = scratch[0], out.shape[0]
     fill(window, index_ref[0], [piece.at[0] for piece in pieces], rows)
     fill(mobile, index_ref[0], [piece.at[1] for piece in pieces], rows)
-    take_steps(window, mobile, 9 * rows)
+
+    def shift_row(row, carried):
+        mobile_before[row] = z_shifted(mobile[row], 1)
+        return carried
+
+    lax.fori_loop(0, 9 * rows, shift_row, 0, unroll=UNROLL)
+    take_steps(window, mobile, mobile_before, matrix, *scratch[1:], 9 * rows)
     out[...] = window[pl.ds(4 * rows, rows)]
 
 
 def later_kernel(index_ref, *refs):
-    pieces, mobile, out, window = refs[:9], *refs[9:]
-    rows = out.shape[0]
+    pieces, mobile, mobile_before, matrix, out, *scratch = refs[:9], *refs[9:]
+    window, rows = scratch[0], out.shape[0]
     fill(window, index_ref[0], pieces, rows)
-    take_steps(window, mobile, 9 * rows)
+    take_steps(window, mobile, mobile_before, matrix, *scratch[1:], 9 * rows)
     out[...] = window[pl.ds(4 * rows, rows)]
 
 
@@ -181,14 +205,15 @@
     when(from_left == even, write, across)
 
 
-def gap_kernel(own, right, earlier, total):
-    total[: CYCLES - 1] = earlier[...]
-    total[CYCLES - 1 :] = squares_of(own, right)
-
-
-def last_kernel(cells, images, index_ref, lower_ref, weight_ref, gaps, own, left, right, out, length):
-    image = index_ref[0]
-    from_left, of_other, of_own = mixing(CYCLES - 1, image, lower_ref, weight_ref)
+def gap_kernel(own, right, *refs):
+    *earlier, everyone = refs
+    rows = [ref[...] for ref in earlier] + [squares_of(own, right)]
+    for cycle, row in enumerate(rows):
+        everyone[:, cycle : cycle + 1] = jnp.broadcast_to(row[None], (everyone.shape[0], *row.shape))
+
+
+def final_mix_kernel(index_ref, lower_ref, weight_ref, own, left, right, out):
+    from_left, of_other, of_own = mixing(CYCLES - 1, index_ref[0], lower_ref, weight_ref)
 
     def write(other):
         for row in range(own.shape[0]):
@@ -202,10 +227,12 @@
     def _():
         write(right)
 
+
+def length_kernel(cells, images, index_ref, gaps, length):
     each = jnp.sum(gaps[...].reshape(images, -1, CYCLES, gaps.shape[-1]), axis=1)
     distance = jnp.sqrt(jnp.sum(each, axis=-1, keepdims=True) / cells + epsilon)
     position = lax.broadcasted_iota(jnp.int32, distance.shape, 0)
-    reached = jnp.sum(jnp.where(position < image, distance, 0.0), axis=0)
+    reached = jnp.sum(jnp.where(position < index_ref[0], distance, 0.0), axis=0)
     lane = lax.broadcasted_iota(jnp.int32, length.shape, 1)
     result = jnp.zeros(length.shape, jnp.float32)
     for cycle in range(CYCLES):
@@ -221,7 +248,8 @@
     rows, depth, lanes = field.shape[1:]
     slab = (rows, depth // SUBLANES, SUBLANES, lanes)
     wide = (9 * rows,) + slab[1:]
-    window = pltpu.VMEM(wide, jnp.float32)
+    windows = [pltpu.VMEM(wide, jnp.float32)] * 3
+    matrix = z_neighbours(lanes)
     image_count, domain_count = lax.axis_size("image"), lax.axis_size("domain")
     image_index = lax.axis_index("image")[None]
     index = lax.axis_index("domain")
@@ -239,14 +267,14 @@
         ],
         compiler_params=PARAMS,
     )(field[0], mobility)
-    phase, mobile = pl.pallas_call(
+    phase, *mobiles = pl.pallas_call(
         first_kernel,
-        out_shape=(shaped(*slab), shaped(*wide)),
-        in_specs=[SMEM] + [VMEM] * 9,
-        out_specs=(VMEM, VMEM),
-        scratch_shapes=[window],
-        compiler_params=PARAMS,
-    )(index[None], *halo_pieces(packed, index))
+        out_shape=(shaped(*slab), shaped(*wide), shaped(*wide)),
+        in_specs=[SMEM] + [VMEM] * 10,
+        out_specs=(VMEM, VMEM, VMEM),
+        scratch_shapes=windows,
+        compiler_params=PARAMS,
+    )(index[None], *halo_pieces(packed, index), matrix)
 
     totals = []
     for cycle in range(CYCLES - 1):
@@ -263,29 +291,35 @@
         phase = pl.pallas_call(
             later_kernel,
             out_shape=shaped(*slab),
-            in_specs=[SMEM] + [VMEM] * 10,
+            in_specs=[SMEM] + [VMEM] * 12,
             out_specs=VMEM,
-            scratch_shapes=[window],
+            scratch_shapes=windows,
             compiler_params=PARAMS,
-        )(index[None], *halo_pieces(phase, index), mobile)
+        )(index[None], *halo_pieces(phase, index), *mobiles, matrix)
     right = passed_along(phase, -1)
     left = passed_along(phase, 1)
-    mine = pl.pallas_call(
+    everyone = pl.pallas_call(
         gap_kernel,
-        out_shape=shaped(CYCLES, lanes),
-        in_specs=[VMEM] * 3,
+        out_shape=shaped(image_count * domain_count, CYCLES, lanes),
+        in_specs=[VMEM] * (2 + len(totals)),
         out_specs=VMEM,
         compiler_params=PARAMS,
-    )(phase, right, jnp.concatenate(totals, axis=0))
-    everyone = jnp.broadcast_to(mine[None], (image_count * domain_count, CYCLES, lanes))
+    )(phase, right, *totals)
     gaps = lax.all_to_all(everyone, ("image", "domain"), 0, 0)
-    evolved, arclength = pl.pallas_call(
-        lambda *refs: last_kernel(cells, image_count, *refs),
-        out_shape=(shaped(rows, depth, lanes), shaped(1, CYCLES)),
-        in_specs=[SMEM] * 3 + [VMEM] * 4,
-        out_specs=(VMEM, VMEM),
-        compiler_params=PARAMS,
-    )(image_index, lower, weights, gaps, phase, left, right)
+    evolved = pl.pallas_call(
+        final_mix_kernel,
+        out_shape=shaped(rows, depth, lanes),
+        in_specs=[SMEM] * 3 + [VMEM] * 3,
+        out_specs=VMEM,
+        compiler_params=PARAMS,
+    )(image_index, lower, weights, phase, left, right)
+    arclength = pl.pallas_call(
+        lambda *refs: length_kernel(cells, image_count, *refs),
+        out_shape=shaped(1, CYCLES),
+        in_specs=[SMEM, VMEM],
+        out_specs=VMEM,
+        compiler_params=PARAMS,
+    )(image_index, gaps)
     return evolved[None], arclength.T
 
 

time: 113 us -> 111 us (0.982)
  local copies, waits for them, and re-layouts: 2.59 us -> 6.79 us
  Pallas kernels: 26.9 us -> 23.6 us
  waiting for transfers between devices: 31.4 us -> 28.5 us
    unnamed x8 -> x22, local copies, waits for them, and re-layouts: 1.81 us -> 6.79 us
    pallas_call x1, Pallas kernels: 12.3 us -> 9.42 us  [cycles(): pl.pallas_call(later_kernel, out_shape=shaped(*slab), in_specs=[SMEM] + [...]
    ppermute x18, waiting for transfers between devices: 13.9 us -> 12.1 us  [exchanged(): lax.ppermute(value, axis, [(i, j) for i, j in pairs if 0 <= j < size])]
    all_to_all x1, waiting for transfers between devices: 7.24 us -> 6.05 us  [cycles(): gaps = lax.all_to_all(everyone, ('image', 'domain'), 0, 0)]
    pallas_call x3 -> x4, Pallas kernels: 13.7 us -> 13.2 us  [the longest x1 10.4 us: cycles(): pl.pallas_call(first_kernel, out_shape=(shaped(*slab), shaped(*wide), sha...]
  transfers between devices with their start and end apart: 21 -> 21, of which waited for: 10 -> 9; matrix products, arithmetic and copies ran while one was open for 0% -> 0% of each run, Pallas kernels for 0% -> 1%
where the time goes in v4:
time: 111 us
  starting transfers between devices  51.4 us (46%)
  waiting for transfers between devices  28.5 us (26%)
  Pallas kernels  23.6 us (21%)
  local copies, waits for them, and re-layouts  6.79 us (6%)
    ppermute x18, starting transfers between devices, exchanged(): lax.ppermute(value, axis, [(i, j) for i, j in pairs if 0 <= j < size])  32.9 us
    all_to_all x1, starting transfers between devices, cycles(): gaps = lax.all_to_all(everyone, ('image', 'domain'), 0, 0)  13.8 us
    ppermute x18, waiting for transfers between devices, exchanged(): lax.ppermute(value, axis, [(i, j) for i, j in pairs if 0 <= j < size])  12.1 us
    pallas_call x1, Pallas kernels, cycles(): pl.pallas_call(first_kernel, out_shape=(shaped(*slab), shaped(*wide), sha...  10.4 us
    ppermute x2, waiting for transfers between devices, passed_along(): lax.ppermute(value, 'image', [(i, i + steps) for i in range(first, last)])  10.3 us
    pallas_call x1, Pallas kernels, cycles(): pl.pallas_call(later_kernel, out_shape=shaped(*slab), in_specs=[SMEM] + [...  9.42 us
    unnamed x22, local copies, waits for them, and re-layouts  6.79 us
    all_to_all x1, waiting for transfers between devices, cycles(): gaps = lax.all_to_all(everyone, ('image', 'domain'), 0, 0)  6.05 us
  transfers between devices with their start and end apart: 21, of which 9 were waited for; matrix products, arithmetic and copies ran while one was open for 0% of the time, Pallas kernels for 1%

profile of v4, /device:TPU:1, one launch (start us, length us, event | category | flops | bytes accessed | tf_op | source)
XLA Modules:
  0.0 111.0 jit_solution(17241624001438617664)
XLA Ops:
  0.6 0.0 copy-start
  0.6 0.0 copy-start.7
  0.7 0.9 copy-done.7
  1.6 0.0 copy-start.8
  1.6 0.9 copy-done.8
  2.5 0.4 shard_map.68.refs_0_
  2.9 2.2 %collective-permute-start.3 = (f32[2,4,8,8,128]{4,3,2,1,0:T(8,128)S(1)}, f32[2,4,8,8,128]{4,3,2,1,0:T(8,128)S(1)}, u32[]{:S(2)}, u32[]{:S(2)}) collective-permute-start(f32[2,4,8,8,128]{4,3,2,1,0:T(8,128)S(1)} %shard_map.68.refs_0_), channel_id=1, source_target_pairs={{0,4},{1,5},{2,6},{3,7},{4,0},{5,1},{6,2},{7,3},{8,12},{9,13},{10,... | collective-permute-start | bytes 786440 | tf_op jit(solution)/shard_map/ppermute | solution.py:26
  5.1 1.9 %collective-permute-start.2 = (f32[2,4,8,8,128]{4,3,2,1,0:T(8,128)S(1)}, f32[2,4,8,8,128]{4,3,2,1,0:T(8,128)S(1)}, u32[]{:S(2)}, u32[]{:S(2)}) collective-permute-start(f32[2,4,8,8,128]{4,3,2,1,0:T(8,128)S(1)} %shard_map.68.refs_0_), channel_id=1, source_target_pairs={{0,12},{1,13},{2,14},{3,15},{4,8},{5,9},{6,10},{7,11},{8,4},{9,5},... | collective-permute-start | bytes 786440 | tf_op jit(solution)/shard_map/ppermute | solution.py:26
  7.0 2.7 %collective-permute-start.1 = (f32[2,4,8,8,128]{4,3,2,1,0:T(8,128)S(1)}, f32[2,4,8,8,128]{4,3,2,1,0:T(8,128)S(1)}, u32[]{:S(2)}, u32[]{:S(2)}) collective-permute-start(f32[2,4,8,8,128]{4,3,2,1,0:T(8,128)S(1)} %shard_map.68.refs_0_), channel_id=1, source_target_pairs={{0,2},{1,3},{2,0},{3,1},{4,6},{5,7},{6,4},{7,5},{8,10},{9,11},{10,... | collective-permute-start | bytes 786440 | tf_op jit(solution)/shard_map/ppermute | solution.py:26
  9.7 0.7 collective-permute-start
  10.4 2.0 %collective-permute-start.4 = (f32[2,4,8,8,128]{4,3,2,1,0:T(8,128)S(1)}, f32[2,4,8,8,128]{4,3,2,1,0:T(8,128)S(1)}, u32[]{:S(2)}, u32[]{:S(2)}) collective-permute-start(f32[2,4,8,8,128]{4,3,2,1,0:T(8,128)S(1)} %shard_map.68.refs_0_), channel_id=1, source_target_pairs={{0,1},{1,0},{2,3},{3,2},{4,5},{5,4},{6,7},{7,6},{8,9},{9,8},{10,11... | collective-permute-start | bytes 786440 | tf_op jit(solution)/shard_map/ppermute | solution.py:26
  12.5 0.0 collective-permute-done.3.refs_4_
  12.5 0.5 collective-permute-done.2.refs_3_
  13.0 2.1 %collective-permute-start.7 = (f32[2,4,8,8,128]{4,3,2,1,0:T(8,128)S(1)}, f32[2,4,8,8,128]{4,3,2,1,0:T(8,128)S(1)}, u32[]{:S(2)}, u32[]{:S(2)}) collective-permute-start(f32[2,4,8,8,128]{4,3,2,1,0:T(8,128)S(1)} %broadcast_select_fusion), channel_id=1, source_target_pairs={{0,1},{1,0},{2,3},{3,2},{4,5},{5,4},{6,7},{7,6},{8,9},{9,8},{10,11... | collective-permute-start | bytes 786440 | tf_op jit(solution)/shard_map/ppermute | solution.py:26
  15.1 0.0 collective-permute-done.1.refs_2_
  15.1 3.8 %collective-permute-start.6 = (f32[2,4,8,8,128]{4,3,2,1,0:T(8,128)S(1)}, f32[2,4,8,8,128]{4,3,2,1,0:T(8,128)S(1)}, u32[]{:S(2)}, u32[]{:S(2)}) collective-permute-start(f32[2,4,8,8,128]{4,3,2,1,0:T(8,128)S(1)} %collective-permute-done.1.refs_2_), channel_id=1, source_target_pairs={{0,1},{1,0},{2,3},{3,2},{4,5},{5,4},{6,7},{7,6},{8,9},{9,8},{10,11... | collective-permute-start | bytes 786440 | tf_op jit(solution)/shard_map/ppermute | solution.py:26
  18.9 0.7 copy-done.1
  19.6 2.1 %collective-permute-done.refs_1_ = f32[2,4,8,8,128]{4,3,2,1,0:T(8,128)S(1)} collective-permute-done((f32[2,4,8,8,128]{4,3,2,1,0:T(8,128)S(1)}, f32[2,4,8,8,128]{4,3,2,1,0:T(8,128)S(1)}, u32[]{:S(2)}, u32[]{:S(2)}) %collective-permute-start) | collective-permute-done | bytes 262176 | tf_op jit(solution)/shard_map/ppermute | solution.py:26
  21.7 1.7 %collective-permute-start.5 = (f32[2,4,8,8,128]{4,3,2,1,0:T(8,128)S(1)}, f32[2,4,8,8,128]{4,3,2,1,0:T(8,128)S(1)}, u32[]{:S(2)}, u32[]{:S(2)}) collective-permute-start(f32[2,4,8,8,128]{4,3,2,1,0:T(8,128)S(1)} %collective-permute-done.refs_1_), channel_id=1, source_target_pairs={{0,1},{1,0},{2,3},{3,2},{4,5},{5,4},{6,7},{7,6},{8,9},{9,8},{10,11... | collective-permute-start | bytes 786440 | tf_op jit(solution)/shard_map/ppermute | solution.py:26
  23.3 0.7 copy-done.3
  24.0 0.0 collective-permute-done.4.refs_5_
  24.0 0.7 copy-done.5
  24.7 0.0 collective-permute-done.7.refs_8_
  24.7 0.0 collective-permute-done.6.refs_7_
  24.7 0.0 collective-permute-done.5.refs_6_
  24.7 0.0 copy-done
  24.7 0.0 copy-start.2
  24.7 0.9 copy-done.2
  25.7 0.9 copy-done.4
  26.6 0.9 copy-done.6
  27.6 10.4 %shard_map.69 = (f32[4,8,8,128]{3,2,1,0:T(8,128)S(1)}, f32[36,8,8,128]{3,2,1,0:T(8,128)S(1)}, f32[36,8,8,128]{3,2,1,0:T(8,128)S(1)}) custom-call(s32[1]{0:T(128)} %bitcast.3.index_ref, f32[2,4,8,8,128]{4,3,2,1,0:T(8,128)S(1)} %shard_map.68.refs_0_, f32[2,4,8,8,128]{4,3,2,1,0:T(8,128)S(1)} %copy-done.4, f32[2,4,8,8,128]{4,3,2,1,0:T(8,128)S(1)} %copy-done.2, ...), custom_call_target="tpu_custom_call" | custom-call | tf_op jit(solution)/shard_map/pallas_call | solution.py:270
  38.0 0.7 collective-permute-start.9
  38.7 4.6 %collective-permute-start.8 = (f32[4,8,8,128]{3,2,1,0:T(8,128)S(1)}, f32[4,8,8,128]{3,2,1,0:T(8,128)S(1)}, u32[]{:S(2)}, u32[]{:S(2)}) collective-permute-start(f32[4,8,8,128]{3,2,1,0:T(8,128)S(1)} %get-tuple-element.7.refs_3_), channel_id=1, source_target_pairs={{0,16},{16,0},{32,48},{48,32},{64,80},{80,64},{96,112},{112,96},{1... | collective-permute-start | bytes 393224 | tf_op jit(solution)/shard_map/ppermute | solution.py:26
  43.3 0.0 collective-permute-done.9.refs_5_
  43.3 3.5 %collective-permute-done.8.refs_4_ = f32[4,8,8,128]{3,2,1,0:T(8,128)S(1)} collective-permute-done((f32[4,8,8,128]{3,2,1,0:T(8,128)S(1)}, f32[4,8,8,128]{3,2,1,0:T(8,128)S(1)}, u32[]{:S(2)}, u32[]{:S(2)}) %collective-permute-start.8) | collective-permute-done | bytes 131104 | tf_op jit(solution)/shard_map/ppermute | solution.py:26
  46.8 0.0 copy-done.9
  46.8 0.0 copy-done.10
  46.8 0.6 shard_map.70
  47.4 0.8 collective-permute-start.13
  48.2 1.0 collective-permute-start.12
  49.1 1.5 %collective-permute-start.14 = (f32[4,8,8,128]{3,2,1,0:T(8,128)S(1)}, f32[4,8,8,128]{3,2,1,0:T(8,128)S(1)}, u32[]{:S(2)}, u32[]{:S(2)}) collective-permute-start(f32[4,8,8,128]{3,2,1,0:T(8,128)S(1)} %get-tuple-element.8.refs_0_), channel_id=1, source_target_pairs={{0,1},{1,0},{2,3},{3,2},{4,5},{5,4},{6,7},{7,6},{8,9},{9,8},{10,11... | collective-permute-start | bytes 393224 | tf_op jit(solution)/shard_map/ppermute | solution.py:26
  50.7 2.8 %collective-permute-start.11 = (f32[4,8,8,128]{3,2,1,0:T(8,128)S(1)}, f32[4,8,8,128]{3,2,1,0:T(8,128)S(1)}, u32[]{:S(2)}, u32[]{:S(2)}) collective-permute-start(f32[4,8,8,128]{3,2,1,0:T(8,128)S(1)} %get-tuple-element.8.refs_0_), channel_id=1, source_target_pairs={{0,2},{1,3},{2,0},{3,1},{4,6},{5,7},{6,4},{7,5},{8,10},{9,11},{10,... | collective-permute-start | bytes 393224 | tf_op jit(solution)/shard_map/ppermute | solution.py:26
  53.5 1.6 %collective-permute-start.10 = (f32[4,8,8,128]{3,2,1,0:T(8,128)S(1)}, f32[4,8,8,128]{3,2,1,0:T(8,128)S(1)}, u32[]{:S(2)}, u32[]{:S(2)}) collective-permute-start(f32[4,8,8,128]{3,2,1,0:T(8,128)S(1)} %get-tuple-element.8.refs_0_), channel_id=1, source_target_pairs={{0,14},{1,15},{2,4},{3,5},{4,2},{5,3},{6,8},{7,9},{8,6},{9,7},{10,... | collective-permute-start | bytes 393224 | tf_op jit(solution)/shard_map/ppermute | solution.py:26
  55.1 0.0 collective-permute-done.13.refs_4_
  55.1 0.0 collective-permute-done.12.refs_3_
  55.1 0.8 collective-permute-start.17
  55.9 1.3 %collective-permute-done.11.refs_2_ = f32[4,8,8,128]{3,2,1,0:T(8,128)S(1)} collective-permute-done((f32[4,8,8,128]{3,2,1,0:T(8,128)S(1)}, f32[4,8,8,128]{3,2,1,0:T(8,128)S(1)}, u32[]{:S(2)}, u32[]{:S(2)}) %collective-permute-start.11) | collective-permute-done | bytes 131104 | tf_op jit(solution)/shard_map/ppermute | solution.py:26
  57.2 0.9 collective-permute-start.16
  58.1 3.8 %collective-permute-done.10.refs_1_ = f32[4,8,8,128]{3,2,1,0:T(8,128)S(1)} collective-permute-done((f32[4,8,8,128]{3,2,1,0:T(8,128)S(1)}, f32[4,8,8,128]{3,2,1,0:T(8,128)S(1)}, u32[]{:S(2)}, u32[]{:S(2)}) %collective-permute-start.10) | collective-permute-done | bytes 131104 | tf_op jit(solution)/shard_map/ppermute | solution.py:26
  61.9 1.1 %collective-permute-start.15 = (f32[4,8,8,128]{3,2,1,0:T(8,128)S(1)}, f32[4,8,8,128]{3,2,1,0:T(8,128)S(1)}, u32[]{:S(2)}, u32[]{:S(2)}) collective-permute-start(f32[4,8,8,128]{3,2,1,0:T(8,128)S(1)} %collective-permute-done.10.refs_1_), channel_id=1, source_target_pairs={{0,1},{1,0},{2,3},{3,2},{4,5},{5,4},{6,7},{7,6},{8,9},{9,8},{10,11... | collective-permute-start | bytes 393224 | tf_op jit(solution)/shard_map/ppermute | solution.py:26
  63.0 0.0 collective-permute-done.14.refs_5_
  63.0 0.0 collective-permute-done.17.refs_8_
  63.0 0.0 collective-permute-done.16.refs_7_
  63.0 1.0 collective-permute-done.15.refs_6_
  64.0 9.4 %shard_map.71.own = f32[4,8,8,128]{3,2,1,0:T(8,128)S(1)} custom-call(s32[1]{0:T(128)} %bitcast.3.index_ref, f32[4,8,8,128]{3,2,1,0:T(8,128)S(1)} %get-tuple-element.8.refs_0_, f32[4,8,8,128]{3,2,1,0:T(8,128)S(1)} %collective-permute-done.10.refs_1_, f32[4,8,8,128]{3,2,1,0:T(8,128)S(1)} %collective-permute-done.11.refs_2_, ...), custom_call_target="tpu_custom_call" | custom-call | tf_op jit(solution)/shard_map/pallas_call | solution.py:291
  73.4 1.3 %collective-permute-start.19 = (f32[4,8,8,128]{3,2,1,0:T(8,128)S(1)}, f32[4,8,8,128]{3,2,1,0:T(8,128)S(1)}, u32[]{:S(2)}, u32[]{:S(2)}) collective-permute-start(f32[4,8,8,128]{3,2,1,0:T(8,128)S(1)} %shard_map.71.own), channel_id=1, source_target_pairs={{16,0},{32,16},{48,32},{64,48},{80,64},{96,80},{112,96},{128,112},... | collective-permute-start | bytes 393224 | tf_op jit(solution)/shard_map/ppermute | solution.py:32
  74.7 5.3 %collective-permute-done.19.right = f32[4,8,8,128]{3,2,1,0:T(8,128)S(1)} collective-permute-done((f32[4,8,8,128]{3,2,1,0:T(8,128)S(1)}, f32[4,8,8,128]{3,2,1,0:T(8,128)S(1)}, u32[]{:S(2)}, u32[]{:S(2)}) %collective-permute-start.19) | collective-permute-done | bytes 131104 | tf_op jit(solution)/shard_map/ppermute | solution.py:32
  80.0 0.9 shard_map.73
  80.9 13.8 %all-to-all-start = ((f32[256,2,128]{2,1,0:T(2,128)}), f32[256,2,128]{2,1,0:T(2,128)S(1)}, u32[]{:S(2)}, u32[]{:S(2)}) async-start(f32[256,2,128]{2,1,0:T(2,128)} %shard_map.73), calls=%async_computation | async-start | bytes 524288 | tf_op jit(solution)/shard_map/all_to_all | solution.py:308
  94.6 3.4 %collective-permute-start.18 = (f32[4,8,8,128]{3,2,1,0:T(8,128)S(1)}, f32[4,8,8,128]{3,2,1,0:T(8,128)S(1)}, u32[]{:S(2)}, u32[]{:S(2)}) collective-permute-start(f32[4,8,8,128]{3,2,1,0:T(8,128)S(1)} %shard_map.71.own), channel_id=1, source_target_pairs={{0,16},{16,32},{32,48},{48,64},{64,80},{80,96},{96,112},{112,128},... | collective-permute-start | bytes 393224 | tf_op jit(solution)/shard_map/ppermute | solution.py:32
  98.0 5.0 %collective-permute-done.18.left = f32[4,8,8,128]{3,2,1,0:T(8,128)S(1)} collective-permute-done((f32[4,8,8,128]{3,2,1,0:T(8,128)S(1)}, f32[4,8,8,128]{3,2,1,0:T(8,128)S(1)}, u32[]{:S(2)}, u32[]{:S(2)}) %collective-permute-start.18) | collective-permute-done | bytes 131104 | tf_op jit(solution)/shard_map/ppermute | solution.py:32
  103.1 1.2 %shard_map.72 = f32[4,64,128]{2,1,0:T(8,128)} custom-call(s32[1]{0:T(128)} %bitcast.refs_0_.index_ref, s32[1,2]{1,0:T(1,128)S(1)} %bitcast.9, f32[1,2]{1,0:T(1,128)S(1)} %bitcast.11, f32[4,8,8,128]{3,2,1,0:T(8,128)S(1)} %shard_map.71.own, f32[4,8,8,128]{3,2,1,0:T(8,128)S(1)} %collective-permute-done.18.left, f32[4,8,8,128]{3,2,1,0:T(8,128)S(1)} %collective-permute-done.19.right), custom_call_target="tpu_custom_call" | custom-call | tf_op jit(solution)/shard_map/pallas_call | solution.py:309
  104.3 6.1 %all-to-all-done.refs_1_ = f32[256,2,128]{2,1,0:T(2,128)S(1)} async-done(((f32[256,2,128]{2,1,0:T(2,128)}), f32[256,2,128]{2,1,0:T(2,128)S(1)}, u32[]{:S(2)}, u32[]{:S(2)}) %all-to-all-start) | async-done | bytes 262176 | tf_op jit(solution)/shard_map/all_to_all | solution.py:308
  110.3 0.7 shard_map.74
  (9 shorter events, 0.1 us)
Async XLA Ops:
  0.6 24.1 %copy-start = (bf16[256,256]{1,0:T(8,128)(2,1)S(1)}, bf16[256,256]{1,0:T(8,128)(2,1)}, u32[]{:S(2)}) copy-start(bf16[256,256]{1,0:T(8,128)(2,1)} %constant.56.clone.refs_9_.refs_11_) | copy-start | bytes 393220
  0.6 0.9 copy-start.7
  1.6 0.9 copy-start.8
  2.9 9.6 %collective-permute-start.3 = (f32[2,4,8,8,128]{4,3,2,1,0:T(8,128)S(1)}, f32[2,4,8,8,128]{4,3,2,1,0:T(8,128)S(1)}, u32[]{:S(2)}, u32[]{:S(2)}) collective-permute-start(f32[2,4,8,8,128]{4,3,2,1,0:T(8,128)S(1)} %shard_map.68.refs_0_), channel_id=1, source_target_pairs={{0,4},{1,5},{2,6},{3,7},{4,0},{5,1},{6,2},{7,3},{8,12},{9,13},{10,... | collective-permute-start | bytes 786440 | tf_op jit(solution)/shard_map/ppermute | solution.py:26
  5.1 7.9 %collective-permute-start.2 = (f32[2,4,8,8,128]{4,3,2,1,0:T(8,128)S(1)}, f32[2,4,8,8,128]{4,3,2,1,0:T(8,128)S(1)}, u32[]{:S(2)}, u32[]{:S(2)}) collective-permute-start(f32[2,4,8,8,128]{4,3,2,1,0:T(8,128)S(1)} %shard_map.68.refs_0_), channel_id=1, source_target_pairs={{0,12},{1,13},{2,14},{3,15},{4,8},{5,9},{6,10},{7,11},{8,4},{9,5},... | collective-permute-start | bytes 786440 | tf_op jit(solution)/shard_map/ppermute | solution.py:26
  7.0 8.2 %collective-permute-start.1 = (f32[2,4,8,8,128]{4,3,2,1,0:T(8,128)S(1)}, f32[2,4,8,8,128]{4,3,2,1,0:T(8,128)S(1)}, u32[]{:S(2)}, u32[]{:S(2)}) collective-permute-start(f32[2,4,8,8,128]{4,3,2,1,0:T(8,128)S(1)} %shard_map.68.refs_0_), channel_id=1, source_target_pairs={{0,2},{1,3},{2,0},{3,1},{4,6},{5,7},{6,4},{7,5},{8,10},{9,11},{10,... | collective-permute-start | bytes 786440 | tf_op jit(solution)/shard_map/ppermute | solution.py:26
  9.7 11.9 %collective-permute-start = (f32[2,4,8,8,128]{4,3,2,1,0:T(8,128)S(1)}, f32[2,4,8,8,128]{4,3,2,1,0:T(8,128)S(1)}, u32[]{:S(2)}, u32[]{:S(2)}) collective-permute-start(f32[2,4,8,8,128]{4,3,2,1,0:T(8,128)S(1)} %shard_map.68.refs_0_), channel_id=1, source_target_pairs={{0,14},{1,15},{2,4},{3,5},{4,2},{5,3},{6,8},{7,9},{8,6},{9,7},{10,... | collective-permute-start | bytes 786440 | tf_op jit(solution)/shard_map/ppermute | solution.py:26
  10.4 13.6 %collective-permute-start.4 = (f32[2,4,8,8,128]{4,3,2,1,0:T(8,128)S(1)}, f32[2,4,8,8,128]{4,3,2,1,0:T(8,128)S(1)}, u32[]{:S(2)}, u32[]{:S(2)}) collective-permute-start(f32[2,4,8,8,128]{4,3,2,1,0:T(8,128)S(1)} %shard_map.68.refs_0_), channel_id=1, source_target_pairs={{0,1},{1,0},{2,3},{3,2},{4,5},{5,4},{6,7},{7,6},{8,9},{9,8},{10,11... | collective-permute-start | bytes 786440 | tf_op jit(solution)/shard_map/ppermute | solution.py:26
  13.0 11.7 %collective-permute-start.7 = (f32[2,4,8,8,128]{4,3,2,1,0:T(8,128)S(1)}, f32[2,4,8,8,128]{4,3,2,1,0:T(8,128)S(1)}, u32[]{:S(2)}, u32[]{:S(2)}) collective-permute-start(f32[2,4,8,8,128]{4,3,2,1,0:T(8,128)S(1)} %broadcast_select_fusion), channel_id=1, source_target_pairs={{0,1},{1,0},{2,3},{3,2},{4,5},{5,4},{6,7},{7,6},{8,9},{9,8},{10,11... | collective-permute-start | bytes 786440 | tf_op jit(solution)/shard_map/ppermute | solution.py:26
  15.1 9.6 %collective-permute-start.6 = (f32[2,4,8,8,128]{4,3,2,1,0:T(8,128)S(1)}, f32[2,4,8,8,128]{4,3,2,1,0:T(8,128)S(1)}, u32[]{:S(2)}, u32[]{:S(2)}) collective-permute-start(f32[2,4,8,8,128]{4,3,2,1,0:T(8,128)S(1)} %collective-permute-done.1.refs_2_), channel_id=1, source_target_pairs={{0,1},{1,0},{2,3},{3,2},{4,5},{5,4},{6,7},{7,6},{8,9},{9,8},{10,11... | collective-permute-start | bytes 786440 | tf_op jit(solution)/shard_map/ppermute | solution.py:26
  18.9 0.7 copy-start.1
  21.7 3.1 %collective-permute-start.5 = (f32[2,4,8,8,128]{4,3,2,1,0:T(8,128)S(1)}, f32[2,4,8,8,128]{4,3,2,1,0:T(8,128)S(1)}, u32[]{:S(2)}, u32[]{:S(2)}) collective-permute-start(f32[2,4,8,8,128]{4,3,2,1,0:T(8,128)S(1)} %collective-permute-done.refs_1_), channel_id=1, source_target_pairs={{0,1},{1,0},{2,3},{3,2},{4,5},{5,4},{6,7},{7,6},{8,9},{9,8},{10,11... | collective-permute-start | bytes 786440 | tf_op jit(solution)/shard_map/ppermute | solution.py:26
  23.3 0.7 copy-start.3
  24.0 0.7 copy-start.5
  24.7 1.0 copy-start.2
  25.7 0.9 copy-start.4
  26.6 0.9 copy-start.6
  27.6 19.2 %copy-start.9 = (s32[2,1]{0,1:T(1,128)S(1)}, s32[2,1]{0,1:T(1,128)}, u32[]{:S(2)}) copy-start(s32[2,1]{0,1:T(1,128)} %param.7) | copy-start | bytes 28
  27.6 19.2 %copy-start.10 = (f32[2,1]{0,1:T(1,128)S(1)}, f32[2,1]{0,1:T(1,128)}, u32[]{:S(2)}) copy-start(f32[2,1]{0,1:T(1,128)} %param.8) | copy-start | bytes 28
  38.0 5.3 %collective-permute-start.9 = (f32[4,8,8,128]{3,2,1,0:T(8,128)S(1)}, f32[4,8,8,128]{3,2,1,0:T(8,128)S(1)}, u32[]{:S(2)}, u32[]{:S(2)}) collective-permute-start(f32[4,8,8,128]{3,2,1,0:T(8,128)S(1)} %get-tuple-element.7.refs_3_), channel_id=1, source_target_pairs={{16,32},{32,16},{48,64},{64,48},{80,96},{96,80},{112,128},{128,112... | collective-permute-start | bytes 393224 | tf_op jit(solution)/shard_map/ppermute | solution.py:26
  38.7 8.1 %collective-permute-start.8 = (f32[4,8,8,128]{3,2,1,0:T(8,128)S(1)}, f32[4,8,8,128]{3,2,1,0:T(8,128)S(1)}, u32[]{:S(2)}, u32[]{:S(2)}) collective-permute-start(f32[4,8,8,128]{3,2,1,0:T(8,128)S(1)} %get-tuple-element.7.refs_3_), channel_id=1, source_target_pairs={{0,16},{16,0},{32,48},{48,32},{64,80},{80,64},{96,112},{112,96},{1... | collective-permute-start | bytes 393224 | tf_op jit(solution)/shard_map/ppermute | solution.py:26
  47.4 7.7 %collective-permute-start.13 = (f32[4,8,8,128]{3,2,1,0:T(8,128)S(1)}, f32[4,8,8,128]{3,2,1,0:T(8,128)S(1)}, u32[]{:S(2)}, u32[]{:S(2)}) collective-permute-start(f32[4,8,8,128]{3,2,1,0:T(8,128)S(1)} %get-tuple-element.8.refs_0_), channel_id=1, source_target_pairs={{0,4},{1,5},{2,6},{3,7},{4,0},{5,1},{6,2},{7,3},{8,12},{9,13},{10,... | collective-permute-start | bytes 393224 | tf_op jit(solution)/shard_map/ppermute | solution.py:26
  48.2 6.9 %collective-permute-start.12 = (f32[4,8,8,128]{3,2,1,0:T(8,128)S(1)}, f32[4,8,8,128]{3,2,1,0:T(8,128)S(1)}, u32[]{:S(2)}, u32[]{:S(2)}) collective-permute-start(f32[4,8,8,128]{3,2,1,0:T(8,128)S(1)} %get-tuple-element.8.refs_0_), channel_id=1, source_target_pairs={{0,12},{1,13},{2,14},{3,15},{4,8},{5,9},{6,10},{7,11},{8,4},{9,5},... | collective-permute-start | bytes 393224 | tf_op jit(solution)/shard_map/ppermute | solution.py:26
  49.1 13.8 %collective-permute-start.14 = (f32[4,8,8,128]{3,2,1,0:T(8,128)S(1)}, f32[4,8,8,128]{3,2,1,0:T(8,128)S(1)}, u32[]{:S(2)}, u32[]{:S(2)}) collective-permute-start(f32[4,8,8,128]{3,2,1,0:T(8,128)S(1)} %get-tuple-element.8.refs_0_), channel_id=1, source_target_pairs={{0,1},{1,0},{2,3},{3,2},{4,5},{5,4},{6,7},{7,6},{8,9},{9,8},{10,11... | collective-permute-start | bytes 393224 | tf_op jit(solution)/shard_map/ppermute | solution.py:26
  50.7 6.6 %collective-permute-start.11 = (f32[4,8,8,128]{3,2,1,0:T(8,128)S(1)}, f32[4,8,8,128]{3,2,1,0:T(8,128)S(1)}, u32[]{:S(2)}, u32[]{:S(2)}) collective-permute-start(f32[4,8,8,128]{3,2,1,0:T(8,128)S(1)} %get-tuple-element.8.refs_0_), channel_id=1, source_target_pairs={{0,2},{1,3},{2,0},{3,1},{4,6},{5,7},{6,4},{7,5},{8,10},{9,11},{10,... | collective-permute-start | bytes 393224 | tf_op jit(solution)/shard_map/ppermute | solution.py:26
  53.5 8.4 %collective-permute-start.10 = (f32[4,8,8,128]{3,2,1,0:T(8,128)S(1)}, f32[4,8,8,128]{3,2,1,0:T(8,128)S(1)}, u32[]{:S(2)}, u32[]{:S(2)}) collective-permute-start(f32[4,8,8,128]{3,2,1,0:T(8,128)S(1)} %get-tuple-element.8.refs_0_), channel_id=1, source_target_pairs={{0,14},{1,15},{2,4},{3,5},{4,2},{5,3},{6,8},{7,9},{8,6},{9,7},{10,... | collective-permute-start | bytes 393224 | tf_op jit(solution)/shard_map/ppermute | solution.py:26
  55.1 7.9 %collective-permute-start.17 = (f32[4,8,8,128]{3,2,1,0:T(8,128)S(1)}, f32[4,8,8,128]{3,2,1,0:T(8,128)S(1)}, u32[]{:S(2)}, u32[]{:S(2)}) collective-permute-start(f32[4,8,8,128]{3,2,1,0:T(8,128)S(1)} %broadcast_select_fusion.1), channel_id=1, source_target_pairs={{0,1},{1,0},{2,3},{3,2},{4,5},{5,4},{6,7},{7,6},{8,9},{9,8},{10,11... | collective-permute-start | bytes 393224 | tf_op jit(solution)/shard_map/ppermute | solution.py:26
  57.2 5.8 %collective-permute-start.16 = (f32[4,8,8,128]{3,2,1,0:T(8,128)S(1)}, f32[4,8,8,128]{3,2,1,0:T(8,128)S(1)}, u32[]{:S(2)}, u32[]{:S(2)}) collective-permute-start(f32[4,8,8,128]{3,2,1,0:T(8,128)S(1)} %collective-permute-done.11.refs_2_), channel_id=1, source_target_pairs={{0,1},{1,0},{2,3},{3,2},{4,5},{5,4},{6,7},{7,6},{8,9},{9,8},{10,11... | collective-permute-start | bytes 393224 | tf_op jit(solution)/shard_map/ppermute | solution.py:26
  61.9 2.1 %collective-permute-start.15 = (f32[4,8,8,128]{3,2,1,0:T(8,128)S(1)}, f32[4,8,8,128]{3,2,1,0:T(8,128)S(1)}, u32[]{:S(2)}, u32[]{:S(2)}) collective-permute-start(f32[4,8,8,128]{3,2,1,0:T(8,128)S(1)} %collective-permute-done.10.refs_1_), channel_id=1, source_target_pairs={{0,1},{1,0},{2,3},{3,2},{4,5},{5,4},{6,7},{7,6},{8,9},{9,8},{10,11... | collective-permute-start | bytes 393224 | tf_op jit(solution)/shard_map/ppermute | solution.py:26
  73.4 6.6 %collective-permute-start.19 = (f32[4,8,8,128]{3,2,1,0:T(8,128)S(1)}, f32[4,8,8,128]{3,2,1,0:T(8,128)S(1)}, u32[]{:S(2)}, u32[]{:S(2)}) collective-permute-start(f32[4,8,8,128]{3,2,1,0:T(8,128)S(1)} %shard_map.71.own), channel_id=1, source_target_pairs={{16,0},{32,16},{48,32},{64,48},{80,64},{96,80},{112,96},{128,112},... | collective-permute-start | bytes 393224 | tf_op jit(solution)/shard_map/ppermute | solution.py:32
  80.9 29.4 %all-to-all-start = ((f32[256,2,128]{2,1,0:T(2,128)}), f32[256,2,128]{2,1,0:T(2,128)S(1)}, u32[]{:S(2)}, u32[]{:S(2)}) async-start(f32[256,2,128]{2,1,0:T(2,128)} %shard_map.73), calls=%async_computation | async-start | bytes 524288 | tf_op jit(solution)/shard_map/all_to_all | solution.py:308
  94.6 8.4 %collective-permute-start.18 = (f32[4,8,8,128]{3,2,1,0:T(8,128)S(1)}, f32[4,8,8,128]{3,2,1,0:T(8,128)S(1)}, u32[]{:S(2)}, u32[]{:S(2)}) collective-permute-start(f32[4,8,8,128]{3,2,1,0:T(8,128)S(1)} %shard_map.71.own), channel_id=1, source_target_pairs={{0,16},{16,32},{32,48},{48,64},{64,80},{80,96},{96,112},{112,128},... | collective-permute-start | bytes 393224 | tf_op jit(solution)/shard_map/ppermute | solution.py:32

commit v5 on v4

--- a/solution.py
+++ b/solution.py
@@ -1,6 +1,5 @@
 import jax
 import jax.numpy as jnp
-import numpy as np
 from jax import lax
 from jax.experimental import pallas as pl
 from jax.experimental.pallas import tpu as pltpu
@@ -90,8 +89,13 @@
 
 
 def z_neighbours(lanes):
-    before = np.roll(np.eye(lanes), 1, axis=1)
-    return jnp.asarray(np.tile(np.concatenate([before + before.T, before], axis=1), (2, 1)), jnp.bfloat16)
+    shape = (2 * lanes, 2 * lanes)
+    source = lax.rem(lax.broadcasted_iota(jnp.int32, shape, 0), lanes)
+    column = lax.broadcasted_iota(jnp.int32, shape, 1)
+    ahead = lax.rem(lax.rem(column, lanes) - source + lanes, lanes)
+    before = jnp.where(ahead == 1, 1.0, 0.0)
+    after = jnp.where(ahead == lanes - 1, 1.0, 0.0) * jnp.where(column < lanes, 1.0, 0.0)
+    return (before + after).astype(jnp.bfloat16)
 
 
 def gather(field, around, before, matrix, row, count):
@@ -108,6 +112,14 @@
 
 
 def take_steps(field, mobile, mobile_before, matrix, z_around, z_before, length):
+    matrix[...] = z_neighbours(field.shape[-1])
+
+    def shift_row(row, carried):
+        mobile_before[row] = z_shifted(mobile[row], 1)
+        return carried
+
+    lax.fori_loop(0, length, shift_row, 0, unroll=UNROLL)
+
     def at(row):
         here, before = field[row], z_before[row]
         square = here * here
@@ -151,25 +163,20 @@
 
 
 def first_kernel(index_ref, *refs):
-    pieces, matrix, out, mobile, mobile_before, *scratch = refs[:9], *refs[9:]
-    window, rows = scratch[0], out.shape[0]
+    pieces, out, mobile, window, *scratch = refs[:9], *refs[9:]
+    rows = out.shape[0]
     fill(window, index_ref[0], [piece.at[0] for piece in pieces], rows)
     fill(mobile, index_ref[0], [piece.at[1] for piece in pieces], rows)
 
-    def shift_row(row, carried):
-        mobile_before[row] = z_shifted(mobile[row], 1)
-        return carried
-
-    lax.fori_loop(0, 9 * rows, shift_row, 0, unroll=UNROLL)
-    take_steps(window, mobile, mobile_before, matrix, *scratch[1:], 9 * rows)
+    take_steps(window, mobile, *scratch, 9 * rows)
     out[...] = window[pl.ds(4 * rows, rows)]
 
 
 def later_kernel(index_ref, *refs):
-    pieces, mobile, mobile_before, matrix, out, *scratch = refs[:9], *refs[9:]
-    window, rows = scratch[0], out.shape[0]
+    pieces, mobile, out, window, *scratch = refs[:9], *refs[9:]
+    rows = out.shape[0]
     fill(window, index_ref[0], pieces, rows)
-    take_steps(window, mobile, mobile_before, matrix, *scratch[1:], 9 * rows)
+    take_steps(window, mobile, *scratch, 9 * rows)
     out[...] = window[pl.ds(4 * rows, rows)]
 
 
@@ -248,8 +255,9 @@
     rows, depth, lanes = field.shape[1:]
     slab = (rows, depth // SUBLANES, SUBLANES, lanes)
     wide = (9 * rows,) + slab[1:]
-    windows = [pltpu.VMEM(wide, jnp.float32)] * 3
-    matrix = z_neighbours(lanes)
+    windows = [pltpu.VMEM(wide, jnp.float32)] * 2
+    windows += [pltpu.VMEM((2 * lanes, 2 * lanes), jnp.bfloat16)]
+    windows += [pltpu.VMEM(wide, jnp.float32)] * 2
     image_count, domain_count = lax.axis_size("image"), lax.axis_size("domain")
     image_index = lax.axis_index("image")[None]
     index = lax.axis_index("domain")
@@ -267,14 +275,14 @@
         ],
         compiler_params=PARAMS,
     )(field[0], mobility)
-    phase, *mobiles = pl.pallas_call(
+    phase, mobile = pl.pallas_call(
         first_kernel,
-        out_shape=(shaped(*slab), shaped(*wide), shaped(*wide)),
-        in_specs=[SMEM] + [VMEM] * 10,
-        out_specs=(VMEM, VMEM, VMEM),
+        out_shape=(shaped(*slab), shaped(*wide)),
+        in_specs=[SMEM] + [VMEM] * 9,
+        out_specs=(VMEM,) * 2,
         scratch_shapes=windows,
         compiler_params=PARAMS,
-    )(index[None], *halo_pieces(packed, index), matrix)
+    )(index[None], *halo_pieces(packed, index))
 
     totals = []
     for cycle in range(CYCLES - 1):
@@ -291,11 +299,11 @@
         phase = pl.pallas_call(
             later_kernel,
             out_shape=shaped(*slab),
-            in_specs=[SMEM] + [VMEM] * 12,
+            in_specs=[SMEM] + [VMEM] * 10,
             out_specs=VMEM,
             scratch_shapes=windows,
             compiler_params=PARAMS,
-        )(index[None], *halo_pieces(phase, index), *mobiles, matrix)
+        )(index[None], *halo_pieces(phase, index), mobile)
     right = passed_along(phase, -1)
     left = passed_along(phase, 1)
     everyone = pl.pallas_call(

time: 111 us -> 109 us (0.982)
  local copies, waits for them, and re-layouts: 6.79 us -> 1.81 us
  waiting for transfers between devices: 28.5 us -> 30.1 us
    unnamed x22 -> x8, local copies, waits for them, and re-layouts: 6.79 us -> 1.81 us
    ppermute x18, waiting for transfers between devices: 12.1 us -> 13.7 us  [exchanged(): lax.ppermute(value, axis, [(i, j) for i, j in pairs if 0 <= j < size])]
  transfers between devices with their start and end apart: 21 -> 21, of which waited for: 9 -> 10; matrix products, arithmetic and copies ran while one was open for 0% -> 0% of each run, Pallas kernels for 1% -> 1%
where the time goes in v5:
time: 109 us
  starting transfers between devices  51.6 us (47%)
  waiting for transfers between devices  30.1 us (28%)
  Pallas kernels  24.7 us (23%)
  local copies, waits for them, and re-layouts  1.81 us (2%)
    ppermute x18, starting transfers between devices, exchanged(): lax.ppermute(value, axis, [(i, j) for i, j in pairs if 0 <= j < size])  33.2 us
    all_to_all x1, starting transfers between devices, cycles(): gaps = lax.all_to_all(everyone, ('image', 'domain'), 0, 0)  13.8 us
    ppermute x18, waiting for transfers between devices, exchanged(): lax.ppermute(value, axis, [(i, j) for i, j in pairs if 0 <= j < size])  13.7 us
    pallas_call x1, Pallas kernels, cycles(): pl.pallas_call(first_kernel, out_shape=(shaped(*slab), shaped(*wide)), in...  10.5 us
    pallas_call x1, Pallas kernels, cycles(): pl.pallas_call(later_kernel, out_shape=shaped(*slab), in_specs=[SMEM] + [...  10.4 us
    ppermute x2, waiting for transfers between devices, passed_along(): lax.ppermute(value, 'image', [(i, i + steps) for i in range(first, last)])  10.3 us
    all_to_all x1, waiting for transfers between devices, cycles(): gaps = lax.all_to_all(everyone, ('image', 'domain'), 0, 0)  6.04 us
    ppermute x2, starting transfers between devices, passed_along(): lax.ppermute(value, 'image', [(i, i + steps) for i in range(first, last)])  4.69 us
  transfers between devices with their start and end apart: 21, of which 10 were waited for; matrix products, arithmetic and copies ran while one was open for 0% of the time, Pallas kernels for 1%

profile of v5, /device:TPU:1, one launch (start us, length us, event | category | flops | bytes accessed | tf_op | source)
XLA Modules:
  0.0 108.9 jit_solution(5568521939710836280)
XLA Ops:
  0.6 0.0 copy-start
  0.6 0.9 copy-done
  1.5 0.0 copy-start.1
  1.5 0.9 copy-done.1
  2.4 0.4 shard_map.59.refs_0_
  2.8 2.2 %collective-permute-start.3 = (f32[2,4,8,8,128]{4,3,2,1,0:T(8,128)S(1)}, f32[2,4,8,8,128]{4,3,2,1,0:T(8,128)S(1)}, u32[]{:S(2)}, u32[]{:S(2)}) collective-permute-start(f32[2,4,8,8,128]{4,3,2,1,0:T(8,128)S(1)} %shard_map.59.refs_0_), channel_id=1, source_target_pairs={{0,4},{1,5},{2,6},{3,7},{4,0},{5,1},{6,2},{7,3},{8,12},{9,13},{10,... | collective-permute-start | bytes 786440 | tf_op jit(solution)/shard_map/ppermute | solution.py:25
  5.0 1.9 %collective-permute-start.2 = (f32[2,4,8,8,128]{4,3,2,1,0:T(8,128)S(1)}, f32[2,4,8,8,128]{4,3,2,1,0:T(8,128)S(1)}, u32[]{:S(2)}, u32[]{:S(2)}) collective-permute-start(f32[2,4,8,8,128]{4,3,2,1,0:T(8,128)S(1)} %shard_map.59.refs_0_), channel_id=1, source_target_pairs={{0,12},{1,13},{2,14},{3,15},{4,8},{5,9},{6,10},{7,11},{8,4},{9,5},... | collective-permute-start | bytes 786440 | tf_op jit(solution)/shard_map/ppermute | solution.py:25
  6.9 2.7 %collective-permute-start.1 = (f32[2,4,8,8,128]{4,3,2,1,0:T(8,128)S(1)}, f32[2,4,8,8,128]{4,3,2,1,0:T(8,128)S(1)}, u32[]{:S(2)}, u32[]{:S(2)}) collective-permute-start(f32[2,4,8,8,128]{4,3,2,1,0:T(8,128)S(1)} %shard_map.59.refs_0_), channel_id=1, source_target_pairs={{0,2},{1,3},{2,0},{3,1},{4,6},{5,7},{6,4},{7,5},{8,10},{9,11},{10,... | collective-permute-start | bytes 786440 | tf_op jit(solution)/shard_map/ppermute | solution.py:25
  9.7 0.7 collective-permute-start
  10.4 2.0 %collective-permute-start.4 = (f32[2,4,8,8,128]{4,3,2,1,0:T(8,128)S(1)}, f32[2,4,8,8,128]{4,3,2,1,0:T(8,128)S(1)}, u32[]{:S(2)}, u32[]{:S(2)}) collective-permute-start(f32[2,4,8,8,128]{4,3,2,1,0:T(8,128)S(1)} %shard_map.59.refs_0_), channel_id=1, source_target_pairs={{0,1},{1,0},{2,3},{3,2},{4,5},{5,4},{6,7},{7,6},{8,9},{9,8},{10,11... | collective-permute-start | bytes 786440 | tf_op jit(solution)/shard_map/ppermute | solution.py:25
  12.4 0.0 collective-permute-done.3.refs_4_
  12.4 0.5 collective-permute-done.2.refs_3_
  12.9 2.1 %collective-permute-start.7 = (f32[2,4,8,8,128]{4,3,2,1,0:T(8,128)S(1)}, f32[2,4,8,8,128]{4,3,2,1,0:T(8,128)S(1)}, u32[]{:S(2)}, u32[]{:S(2)}) collective-permute-start(f32[2,4,8,8,128]{4,3,2,1,0:T(8,128)S(1)} %broadcast_select_fusion), channel_id=1, source_target_pairs={{0,1},{1,0},{2,3},{3,2},{4,5},{5,4},{6,7},{7,6},{8,9},{9,8},{10,11... | collective-permute-start | bytes 786440 | tf_op jit(solution)/shard_map/ppermute | solution.py:25
  15.1 0.0 collective-permute-done.1.refs_2_
  15.1 3.8 %collective-permute-start.6 = (f32[2,4,8,8,128]{4,3,2,1,0:T(8,128)S(1)}, f32[2,4,8,8,128]{4,3,2,1,0:T(8,128)S(1)}, u32[]{:S(2)}, u32[]{:S(2)}) collective-permute-start(f32[2,4,8,8,128]{4,3,2,1,0:T(8,128)S(1)} %collective-permute-done.1.refs_2_), channel_id=1, source_target_pairs={{0,1},{1,0},{2,3},{3,2},{4,5},{5,4},{6,7},{7,6},{8,9},{9,8},{10,11... | collective-permute-start | bytes 786440 | tf_op jit(solution)/shard_map/ppermute | solution.py:25
  18.9 2.8 %collective-permute-done.refs_1_ = f32[2,4,8,8,128]{4,3,2,1,0:T(8,128)S(1)} collective-permute-done((f32[2,4,8,8,128]{4,3,2,1,0:T(8,128)S(1)}, f32[2,4,8,8,128]{4,3,2,1,0:T(8,128)S(1)}, u32[]{:S(2)}, u32[]{:S(2)}) %collective-permute-start) | collective-permute-done | bytes 262176 | tf_op jit(solution)/shard_map/ppermute | solution.py:25
  21.6 1.7 %collective-permute-start.5 = (f32[2,4,8,8,128]{4,3,2,1,0:T(8,128)S(1)}, f32[2,4,8,8,128]{4,3,2,1,0:T(8,128)S(1)}, u32[]{:S(2)}, u32[]{:S(2)}) collective-permute-start(f32[2,4,8,8,128]{4,3,2,1,0:T(8,128)S(1)} %collective-permute-done.refs_1_), channel_id=1, source_target_pairs={{0,1},{1,0},{2,3},{3,2},{4,5},{5,4},{6,7},{7,6},{8,9},{9,8},{10,11... | collective-permute-start | bytes 786440 | tf_op jit(solution)/shard_map/ppermute | solution.py:25
  23.3 0.0 collective-permute-done.4.refs_5_
  23.3 0.0 collective-permute-done.7.refs_8_
  23.3 0.0 collective-permute-done.6.refs_7_
  23.3 1.1 %collective-permute-done.5.refs_6_ = f32[2,4,8,8,128]{4,3,2,1,0:T(8,128)S(1)} collective-permute-done((f32[2,4,8,8,128]{4,3,2,1,0:T(8,128)S(1)}, f32[2,4,8,8,128]{4,3,2,1,0:T(8,128)S(1)}, u32[]{:S(2)}, u32[]{:S(2)}) %collective-permute-start.5) | collective-permute-done | bytes 262176 | tf_op jit(solution)/shard_map/ppermute | solution.py:25
  24.4 0.0 copy-start.2
  24.4 0.0 copy-start.3
  24.4 10.5 %shard_map.60 = (f32[4,8,8,128]{3,2,1,0:T(8,128)S(1)}, f32[36,8,8,128]{3,2,1,0:T(8,128)S(1)}) custom-call(s32[1]{0:T(128)} %bitcast.3.index_ref, f32[2,4,8,8,128]{4,3,2,1,0:T(8,128)S(1)} %shard_map.59.refs_0_, f32[2,4,8,8,128]{4,3,2,1,0:T(8,128)S(1)} %collective-permute-done.refs_1_, f32[2,4,8,8,128]{4,3,2,1,0:T(8,128)S(1)} %collective-permute-done.1.refs_2_, ...), custom_call_target="tpu_custom_call" | custom-call | tf_op jit(solution)/shard_map/pallas_call | solution.py:278
  34.9 0.7 collective-permute-start.9
  35.6 4.6 %collective-permute-start.8 = (f32[4,8,8,128]{3,2,1,0:T(8,128)S(1)}, f32[4,8,8,128]{3,2,1,0:T(8,128)S(1)}, u32[]{:S(2)}, u32[]{:S(2)}) collective-permute-start(f32[4,8,8,128]{3,2,1,0:T(8,128)S(1)} %get-tuple-element.6.refs_3_), channel_id=1, source_target_pairs={{0,16},{16,0},{32,48},{48,32},{64,80},{80,64},{96,112},{112,96},{1... | collective-permute-start | bytes 393224 | tf_op jit(solution)/shard_map/ppermute | solution.py:25
  40.2 0.0 collective-permute-done.9.refs_5_
  40.2 3.2 %collective-permute-done.8.refs_4_ = f32[4,8,8,128]{3,2,1,0:T(8,128)S(1)} collective-permute-done((f32[4,8,8,128]{3,2,1,0:T(8,128)S(1)}, f32[4,8,8,128]{3,2,1,0:T(8,128)S(1)}, u32[]{:S(2)}, u32[]{:S(2)}) %collective-permute-start.8) | collective-permute-done | bytes 131104 | tf_op jit(solution)/shard_map/ppermute | solution.py:25
  43.4 0.0 copy-done.2
  43.4 0.0 copy-done.3
  43.4 0.6 shard_map.61
  44.0 0.8 collective-permute-start.13
  44.8 1.0 collective-permute-start.12
  45.8 1.8 %collective-permute-start.14 = (f32[4,8,8,128]{3,2,1,0:T(8,128)S(1)}, f32[4,8,8,128]{3,2,1,0:T(8,128)S(1)}, u32[]{:S(2)}, u32[]{:S(2)}) collective-permute-start(f32[4,8,8,128]{3,2,1,0:T(8,128)S(1)} %get-tuple-element.7.refs_0_), channel_id=1, source_target_pairs={{0,1},{1,0},{2,3},{3,2},{4,5},{5,4},{6,7},{7,6},{8,9},{9,8},{10,11... | collective-permute-start | bytes 393224 | tf_op jit(solution)/shard_map/ppermute | solution.py:25
  47.6 2.8 %collective-permute-start.11 = (f32[4,8,8,128]{3,2,1,0:T(8,128)S(1)}, f32[4,8,8,128]{3,2,1,0:T(8,128)S(1)}, u32[]{:S(2)}, u32[]{:S(2)}) collective-permute-start(f32[4,8,8,128]{3,2,1,0:T(8,128)S(1)} %get-tuple-element.7.refs_0_), channel_id=1, source_target_pairs={{0,2},{1,3},{2,0},{3,1},{4,6},{5,7},{6,4},{7,5},{8,10},{9,11},{10,... | collective-permute-start | bytes 393224 | tf_op jit(solution)/shard_map/ppermute | solution.py:25
  50.4 1.6 %collective-permute-start.10 = (f32[4,8,8,128]{3,2,1,0:T(8,128)S(1)}, f32[4,8,8,128]{3,2,1,0:T(8,128)S(1)}, u32[]{:S(2)}, u32[]{:S(2)}) collective-permute-start(f32[4,8,8,128]{3,2,1,0:T(8,128)S(1)} %get-tuple-element.7.refs_0_), channel_id=1, source_target_pairs={{0,14},{1,15},{2,4},{3,5},{4,2},{5,3},{6,8},{7,9},{8,6},{9,7},{10,... | collective-permute-start | bytes 393224 | tf_op jit(solution)/shard_map/ppermute | solution.py:25
  52.0 0.0 collective-permute-done.13.refs_4_
  52.0 0.0 collective-permute-done.12.refs_3_
  52.0 0.8 collective-permute-start.17
  52.8 1.3 %collective-permute-done.11.refs_2_ = f32[4,8,8,128]{3,2,1,0:T(8,128)S(1)} collective-permute-done((f32[4,8,8,128]{3,2,1,0:T(8,128)S(1)}, f32[4,8,8,128]{3,2,1,0:T(8,128)S(1)}, u32[]{:S(2)}, u32[]{:S(2)}) %collective-permute-start.11) | collective-permute-done | bytes 131104 | tf_op jit(solution)/shard_map/ppermute | solution.py:25
  54.2 0.9 collective-permute-start.16
  55.0 3.8 %collective-permute-done.10.refs_1_ = f32[4,8,8,128]{3,2,1,0:T(8,128)S(1)} collective-permute-done((f32[4,8,8,128]{3,2,1,0:T(8,128)S(1)}, f32[4,8,8,128]{3,2,1,0:T(8,128)S(1)}, u32[]{:S(2)}, u32[]{:S(2)}) %collective-permute-start.10) | collective-permute-done | bytes 131104 | tf_op jit(solution)/shard_map/ppermute | solution.py:25
  58.8 1.1 %collective-permute-start.15 = (f32[4,8,8,128]{3,2,1,0:T(8,128)S(1)}, f32[4,8,8,128]{3,2,1,0:T(8,128)S(1)}, u32[]{:S(2)}, u32[]{:S(2)}) collective-permute-start(f32[4,8,8,128]{3,2,1,0:T(8,128)S(1)} %collective-permute-done.10.refs_1_), channel_id=1, source_target_pairs={{0,1},{1,0},{2,3},{3,2},{4,5},{5,4},{6,7},{7,6},{8,9},{9,8},{10,11... | collective-permute-start | bytes 393224 | tf_op jit(solution)/shard_map/ppermute | solution.py:25
  59.9 0.0 collective-permute-done.14.refs_5_
  59.9 0.0 collective-permute-done.17.refs_8_
  59.9 0.0 collective-permute-done.16.refs_7_
  59.9 1.0 collective-permute-done.15.refs_6_
  60.9 10.4 %shard_map.62.own = f32[4,8,8,128]{3,2,1,0:T(8,128)S(1)} custom-call(s32[1]{0:T(128)} %bitcast.3.index_ref, f32[4,8,8,128]{3,2,1,0:T(8,128)S(1)} %get-tuple-element.7.refs_0_, f32[4,8,8,128]{3,2,1,0:T(8,128)S(1)} %collective-permute-done.10.refs_1_, f32[4,8,8,128]{3,2,1,0:T(8,128)S(1)} %collective-permute-done.11.refs_2_, ...), custom_call_target="tpu_custom_call" | custom-call | tf_op jit(solution)/shard_map/pallas_call | solution.py:299
  71.3 1.3 %collective-permute-start.19 = (f32[4,8,8,128]{3,2,1,0:T(8,128)S(1)}, f32[4,8,8,128]{3,2,1,0:T(8,128)S(1)}, u32[]{:S(2)}, u32[]{:S(2)}) collective-permute-start(f32[4,8,8,128]{3,2,1,0:T(8,128)S(1)} %shard_map.62.own), channel_id=1, source_target_pairs={{16,0},{32,16},{48,32},{64,48},{80,64},{96,80},{112,96},{128,112},... | collective-permute-start | bytes 393224 | tf_op jit(solution)/shard_map/ppermute | solution.py:31
  72.6 5.3 %collective-permute-done.19.right = f32[4,8,8,128]{3,2,1,0:T(8,128)S(1)} collective-permute-done((f32[4,8,8,128]{3,2,1,0:T(8,128)S(1)}, f32[4,8,8,128]{3,2,1,0:T(8,128)S(1)}, u32[]{:S(2)}, u32[]{:S(2)}) %collective-permute-start.19) | collective-permute-done | bytes 131104 | tf_op jit(solution)/shard_map/ppermute | solution.py:31
  77.9 0.9 shard_map.64
  78.8 13.8 %all-to-all-start = ((f32[256,2,128]{2,1,0:T(2,128)}), f32[256,2,128]{2,1,0:T(2,128)S(1)}, u32[]{:S(2)}, u32[]{:S(2)}) async-start(f32[256,2,128]{2,1,0:T(2,128)} %shard_map.64), calls=%async_computation | async-start | bytes 524288 | tf_op jit(solution)/shard_map/all_to_all | solution.py:316
  92.6 3.4 %collective-permute-start.18 = (f32[4,8,8,128]{3,2,1,0:T(8,128)S(1)}, f32[4,8,8,128]{3,2,1,0:T(8,128)S(1)}, u32[]{:S(2)}, u32[]{:S(2)}) collective-permute-start(f32[4,8,8,128]{3,2,1,0:T(8,128)S(1)} %shard_map.62.own), channel_id=1, source_target_pairs={{0,16},{16,32},{32,48},{48,64},{64,80},{80,96},{96,112},{112,128},... | collective-permute-start | bytes 393224 | tf_op jit(solution)/shard_map/ppermute | solution.py:31
  96.0 5.0 %collective-permute-done.18.left = f32[4,8,8,128]{3,2,1,0:T(8,128)S(1)} collective-permute-done((f32[4,8,8,128]{3,2,1,0:T(8,128)S(1)}, f32[4,8,8,128]{3,2,1,0:T(8,128)S(1)}, u32[]{:S(2)}, u32[]{:S(2)}) %collective-permute-start.18) | collective-permute-done | bytes 131104 | tf_op jit(solution)/shard_map/ppermute | solution.py:31
  101.0 1.2 %shard_map.63 = f32[4,64,128]{2,1,0:T(8,128)} custom-call(s32[1]{0:T(128)} %bitcast.refs_0_.index_ref, s32[1,2]{1,0:T(1,128)S(1)} %bitcast.9, f32[1,2]{1,0:T(1,128)S(1)} %bitcast.11, f32[4,8,8,128]{3,2,1,0:T(8,128)S(1)} %shard_map.62.own, f32[4,8,8,128]{3,2,1,0:T(8,128)S(1)} %collective-permute-done.18.left, f32[4,8,8,128]{3,2,1,0:T(8,128)S(1)} %collective-permute-done.19.right), custom_call_target="tpu_custom_call" | custom-call | tf_op jit(solution)/shard_map/pallas_call | solution.py:317
  102.2 6.0 %all-to-all-done.refs_1_ = f32[256,2,128]{2,1,0:T(2,128)S(1)} async-done(((f32[256,2,128]{2,1,0:T(2,128)}), f32[256,2,128]{2,1,0:T(2,128)S(1)}, u32[]{:S(2)}, u32[]{:S(2)}) %all-to-all-start) | async-done | bytes 262176 | tf_op jit(solution)/shard_map/all_to_all | solution.py:316
  108.3 0.7 shard_map.65
  (2 shorter events, 0.0 us)
Async XLA Ops:
  0.6 0.9 copy-start
  1.5 0.9 copy-start.1
  2.8 9.6 %collective-permute-start.3 = (f32[2,4,8,8,128]{4,3,2,1,0:T(8,128)S(1)}, f32[2,4,8,8,128]{4,3,2,1,0:T(8,128)S(1)}, u32[]{:S(2)}, u32[]{:S(2)}) collective-permute-start(f32[2,4,8,8,128]{4,3,2,1,0:T(8,128)S(1)} %shard_map.59.refs_0_), channel_id=1, source_target_pairs={{0,4},{1,5},{2,6},{3,7},{4,0},{5,1},{6,2},{7,3},{8,12},{9,13},{10,... | collective-permute-start | bytes 786440 | tf_op jit(solution)/shard_map/ppermute | solution.py:25
  5.0 7.9 %collective-permute-start.2 = (f32[2,4,8,8,128]{4,3,2,1,0:T(8,128)S(1)}, f32[2,4,8,8,128]{4,3,2,1,0:T(8,128)S(1)}, u32[]{:S(2)}, u32[]{:S(2)}) collective-permute-start(f32[2,4,8,8,128]{4,3,2,1,0:T(8,128)S(1)} %shard_map.59.refs_0_), channel_id=1, source_target_pairs={{0,12},{1,13},{2,14},{3,15},{4,8},{5,9},{6,10},{7,11},{8,4},{9,5},... | collective-permute-start | bytes 786440 | tf_op jit(solution)/shard_map/ppermute | solution.py:25
  6.9 8.2 %collective-permute-start.1 = (f32[2,4,8,8,128]{4,3,2,1,0:T(8,128)S(1)}, f32[2,4,8,8,128]{4,3,2,1,0:T(8,128)S(1)}, u32[]{:S(2)}, u32[]{:S(2)}) collective-permute-start(f32[2,4,8,8,128]{4,3,2,1,0:T(8,128)S(1)} %shard_map.59.refs_0_), channel_id=1, source_target_pairs={{0,2},{1,3},{2,0},{3,1},{4,6},{5,7},{6,4},{7,5},{8,10},{9,11},{10,... | collective-permute-start | bytes 786440 | tf_op jit(solution)/shard_map/ppermute | solution.py:25
  9.7 11.9 %collective-permute-start = (f32[2,4,8,8,128]{4,3,2,1,0:T(8,128)S(1)}, f32[2,4,8,8,128]{4,3,2,1,0:T(8,128)S(1)}, u32[]{:S(2)}, u32[]{:S(2)}) collective-permute-start(f32[2,4,8,8,128]{4,3,2,1,0:T(8,128)S(1)} %shard_map.59.refs_0_), channel_id=1, source_target_pairs={{0,14},{1,15},{2,4},{3,5},{4,2},{5,3},{6,8},{7,9},{8,6},{9,7},{10,... | collective-permute-start | bytes 786440 | tf_op jit(solution)/shard_map/ppermute | solution.py:25
  10.4 12.9 %collective-permute-start.4 = (f32[2,4,8,8,128]{4,3,2,1,0:T(8,128)S(1)}, f32[2,4,8,8,128]{4,3,2,1,0:T(8,128)S(1)}, u32[]{:S(2)}, u32[]{:S(2)}) collective-permute-start(f32[2,4,8,8,128]{4,3,2,1,0:T(8,128)S(1)} %shard_map.59.refs_0_), channel_id=1, source_target_pairs={{0,1},{1,0},{2,3},{3,2},{4,5},{5,4},{6,7},{7,6},{8,9},{9,8},{10,11... | collective-permute-start | bytes 786440 | tf_op jit(solution)/shard_map/ppermute | solution.py:25
  12.9 10.3 %collective-permute-start.7 = (f32[2,4,8,8,128]{4,3,2,1,0:T(8,128)S(1)}, f32[2,4,8,8,128]{4,3,2,1,0:T(8,128)S(1)}, u32[]{:S(2)}, u32[]{:S(2)}) collective-permute-start(f32[2,4,8,8,128]{4,3,2,1,0:T(8,128)S(1)} %broadcast_select_fusion), channel_id=1, source_target_pairs={{0,1},{1,0},{2,3},{3,2},{4,5},{5,4},{6,7},{7,6},{8,9},{9,8},{10,11... | collective-permute-start | bytes 786440 | tf_op jit(solution)/shard_map/ppermute | solution.py:25
  15.1 8.2 %collective-permute-start.6 = (f32[2,4,8,8,128]{4,3,2,1,0:T(8,128)S(1)}, f32[2,4,8,8,128]{4,3,2,1,0:T(8,128)S(1)}, u32[]{:S(2)}, u32[]{:S(2)}) collective-permute-start(f32[2,4,8,8,128]{4,3,2,1,0:T(8,128)S(1)} %collective-permute-done.1.refs_2_), channel_id=1, source_target_pairs={{0,1},{1,0},{2,3},{3,2},{4,5},{5,4},{6,7},{7,6},{8,9},{9,8},{10,11... | collective-permute-start | bytes 786440 | tf_op jit(solution)/shard_map/ppermute | solution.py:25
  21.6 2.8 %collective-permute-start.5 = (f32[2,4,8,8,128]{4,3,2,1,0:T(8,128)S(1)}, f32[2,4,8,8,128]{4,3,2,1,0:T(8,128)S(1)}, u32[]{:S(2)}, u32[]{:S(2)}) collective-permute-start(f32[2,4,8,8,128]{4,3,2,1,0:T(8,128)S(1)} %collective-permute-done.refs_1_), channel_id=1, source_target_pairs={{0,1},{1,0},{2,3},{3,2},{4,5},{5,4},{6,7},{7,6},{8,9},{9,8},{10,11... | collective-permute-start | bytes 786440 | tf_op jit(solution)/shard_map/ppermute | solution.py:25
  24.4 19.0 %copy-start.2 = (s32[2,1]{0,1:T(1,128)S(1)}, s32[2,1]{0,1:T(1,128)}, u32[]{:S(2)}) copy-start(s32[2,1]{0,1:T(1,128)} %param.6) | copy-start | bytes 28
  24.4 19.0 %copy-start.3 = (f32[2,1]{0,1:T(1,128)S(1)}, f32[2,1]{0,1:T(1,128)}, u32[]{:S(2)}) copy-start(f32[2,1]{0,1:T(1,128)} %param.7) | copy-start | bytes 28
  34.9 5.3 %collective-permute-start.9 = (f32[4,8,8,128]{3,2,1,0:T(8,128)S(1)}, f32[4,8,8,128]{3,2,1,0:T(8,128)S(1)}, u32[]{:S(2)}, u32[]{:S(2)}) collective-permute-start(f32[4,8,8,128]{3,2,1,0:T(8,128)S(1)} %get-tuple-element.6.refs_3_), channel_id=1, source_target_pairs={{16,32},{32,16},{48,64},{64,48},{80,96},{96,80},{112,128},{128,112... | collective-permute-start | bytes 393224 | tf_op jit(solution)/shard_map/ppermute | solution.py:25
  35.6 7.8 %collective-permute-start.8 = (f32[4,8,8,128]{3,2,1,0:T(8,128)S(1)}, f32[4,8,8,128]{3,2,1,0:T(8,128)S(1)}, u32[]{:S(2)}, u32[]{:S(2)}) collective-permute-start(f32[4,8,8,128]{3,2,1,0:T(8,128)S(1)} %get-tuple-element.6.refs_3_), channel_id=1, source_target_pairs={{0,16},{16,0},{32,48},{48,32},{64,80},{80,64},{96,112},{112,96},{1... | collective-permute-start | bytes 393224 | tf_op jit(solution)/shard_map/ppermute | solution.py:25
  44.0 7.9 %collective-permute-start.13 = (f32[4,8,8,128]{3,2,1,0:T(8,128)S(1)}, f32[4,8,8,128]{3,2,1,0:T(8,128)S(1)}, u32[]{:S(2)}, u32[]{:S(2)}) collective-permute-start(f32[4,8,8,128]{3,2,1,0:T(8,128)S(1)} %get-tuple-element.7.refs_0_), channel_id=1, source_target_pairs={{0,4},{1,5},{2,6},{3,7},{4,0},{5,1},{6,2},{7,3},{8,12},{9,13},{10,... | collective-permute-start | bytes 393224 | tf_op jit(solution)/shard_map/ppermute | solution.py:25
  44.8 7.2 %collective-permute-start.12 = (f32[4,8,8,128]{3,2,1,0:T(8,128)S(1)}, f32[4,8,8,128]{3,2,1,0:T(8,128)S(1)}, u32[]{:S(2)}, u32[]{:S(2)}) collective-permute-start(f32[4,8,8,128]{3,2,1,0:T(8,128)S(1)} %get-tuple-element.7.refs_0_), channel_id=1, source_target_pairs={{0,12},{1,13},{2,14},{3,15},{4,8},{5,9},{6,10},{7,11},{8,4},{9,5},... | collective-permute-start | bytes 393224 | tf_op jit(solution)/shard_map/ppermute | solution.py:25
  45.8 14.1 %collective-permute-start.14 = (f32[4,8,8,128]{3,2,1,0:T(8,128)S(1)}, f32[4,8,8,128]{3,2,1,0:T(8,128)S(1)}, u32[]{:S(2)}, u32[]{:S(2)}) collective-permute-start(f32[4,8,8,128]{3,2,1,0:T(8,128)S(1)} %get-tuple-element.7.refs_0_), channel_id=1, source_target_pairs={{0,1},{1,0},{2,3},{3,2},{4,5},{5,4},{6,7},{7,6},{8,9},{9,8},{10,11... | collective-permute-start | bytes 393224 | tf_op jit(solution)/shard_map/ppermute | solution.py:25
  47.6 6.6 %collective-permute-start.11 = (f32[4,8,8,128]{3,2,1,0:T(8,128)S(1)}, f32[4,8,8,128]{3,2,1,0:T(8,128)S(1)}, u32[]{:S(2)}, u32[]{:S(2)}) collective-permute-start(f32[4,8,8,128]{3,2,1,0:T(8,128)S(1)} %get-tuple-element.7.refs_0_), channel_id=1, source_target_pairs={{0,2},{1,3},{2,0},{3,1},{4,6},{5,7},{6,4},{7,5},{8,10},{9,11},{10,... | collective-permute-start | bytes 393224 | tf_op jit(solution)/shard_map/ppermute | solution.py:25
  50.4 8.4 %collective-permute-start.10 = (f32[4,8,8,128]{3,2,1,0:T(8,128)S(1)}, f32[4,8,8,128]{3,2,1,0:T(8,128)S(1)}, u32[]{:S(2)}, u32[]{:S(2)}) collective-permute-start(f32[4,8,8,128]{3,2,1,0:T(8,128)S(1)} %get-tuple-element.7.refs_0_), channel_id=1, source_target_pairs={{0,14},{1,15},{2,4},{3,5},{4,2},{5,3},{6,8},{7,9},{8,6},{9,7},{10,... | collective-permute-start | bytes 393224 | tf_op jit(solution)/shard_map/ppermute | solution.py:25
  52.0 7.9 %collective-permute-start.17 = (f32[4,8,8,128]{3,2,1,0:T(8,128)S(1)}, f32[4,8,8,128]{3,2,1,0:T(8,128)S(1)}, u32[]{:S(2)}, u32[]{:S(2)}) collective-permute-start(f32[4,8,8,128]{3,2,1,0:T(8,128)S(1)} %broadcast_select_fusion.1), channel_id=1, source_target_pairs={{0,1},{1,0},{2,3},{3,2},{4,5},{5,4},{6,7},{7,6},{8,9},{9,8},{10,11... | collective-permute-start | bytes 393224 | tf_op jit(solution)/shard_map/ppermute | solution.py:25
  54.2 5.8 %collective-permute-start.16 = (f32[4,8,8,128]{3,2,1,0:T(8,128)S(1)}, f32[4,8,8,128]{3,2,1,0:T(8,128)S(1)}, u32[]{:S(2)}, u32[]{:S(2)}) collective-permute-start(f32[4,8,8,128]{3,2,1,0:T(8,128)S(1)} %collective-permute-done.11.refs_2_), channel_id=1, source_target_pairs={{0,1},{1,0},{2,3},{3,2},{4,5},{5,4},{6,7},{7,6},{8,9},{9,8},{10,11... | collective-permute-start | bytes 393224 | tf_op jit(solution)/shard_map/ppermute | solution.py:25
  58.8 2.1 %collective-permute-start.15 = (f32[4,8,8,128]{3,2,1,0:T(8,128)S(1)}, f32[4,8,8,128]{3,2,1,0:T(8,128)S(1)}, u32[]{:S(2)}, u32[]{:S(2)}) collective-permute-start(f32[4,8,8,128]{3,2,1,0:T(8,128)S(1)} %collective-permute-done.10.refs_1_), channel_id=1, source_target_pairs={{0,1},{1,0},{2,3},{3,2},{4,5},{5,4},{6,7},{7,6},{8,9},{9,8},{10,11... | collective-permute-start | bytes 393224 | tf_op jit(solution)/shard_map/ppermute | solution.py:25
  71.3 6.6 %collective-permute-start.19 = (f32[4,8,8,128]{3,2,1,0:T(8,128)S(1)}, f32[4,8,8,128]{3,2,1,0:T(8,128)S(1)}, u32[]{:S(2)}, u32[]{:S(2)}) collective-permute-start(f32[4,8,8,128]{3,2,1,0:T(8,128)S(1)} %shard_map.62.own), channel_id=1, source_target_pairs={{16,0},{32,16},{48,32},{64,48},{80,64},{96,80},{112,96},{128,112},... | collective-permute-start | bytes 393224 | tf_op jit(solution)/shard_map/ppermute | solution.py:31
  78.8 29.5 %all-to-all-start = ((f32[256,2,128]{2,1,0:T(2,128)}), f32[256,2,128]{2,1,0:T(2,128)S(1)}, u32[]{:S(2)}, u32[]{:S(2)}) async-start(f32[256,2,128]{2,1,0:T(2,128)} %shard_map.64), calls=%async_computation | async-start | bytes 524288 | tf_op jit(solution)/shard_map/all_to_all | solution.py:316
  92.6 8.4 %collective-permute-start.18 = (f32[4,8,8,128]{3,2,1,0:T(8,128)S(1)}, f32[4,8,8,128]{3,2,1,0:T(8,128)S(1)}, u32[]{:S(2)}, u32[]{:S(2)}) collective-permute-start(f32[4,8,8,128]{3,2,1,0:T(8,128)S(1)} %shard_map.62.own), channel_id=1, source_target_pairs={{0,16},{16,32},{32,48},{48,64},{64,80},{80,96},{96,112},{112,128},... | collective-permute-start | bytes 393224 | tf_op jit(solution)/shard_map/ppermute | solution.py:31

commit v6 on v5

--- a/solution.py
+++ b/solution.py
@@ -16,6 +16,7 @@
 
 VMEM = pl.BlockSpec(memory_space=pltpu.VMEM)
 SMEM = pl.BlockSpec(memory_space=pltpu.SMEM)
+HBM = pl.BlockSpec(memory_space=pltpu.HBM)
 PARAMS = pltpu.CompilerParams(vmem_limit_bytes=16 << 20)
 
 
@@ -114,12 +115,6 @@
 def take_steps(field, mobile, mobile_before, matrix, z_around, z_before, length):
     matrix[...] = z_neighbours(field.shape[-1])
 
-    def shift_row(row, carried):
-        mobile_before[row] = z_shifted(mobile[row], 1)
-        return carried
-
-    lax.fori_loop(0, length, shift_row, 0, unroll=UNROLL)
-
     def at(row):
         here, before = field[row], z_before[row]
         square = here * here
@@ -162,21 +157,29 @@
             fold(held.at[i, row], out, (i, row), 0.5 * time_step if i else None)
 
 
+def shift_kernel(mobile, mobile_before):
+    def shift_row(row, carried):
+        mobile_before[row] = z_shifted(mobile[row], 1)
+        return carried
+
+    lax.fori_loop(0, mobile.shape[0], shift_row, 0, unroll=UNROLL)
+
+
 def first_kernel(index_ref, *refs):
-    pieces, out, mobile, window, *scratch = refs[:9], *refs[9:]
+    pieces, out, mobile, window, mobile_before, *scratch = refs[:9], *refs[9:]
     rows = out.shape[0]
     fill(window, index_ref[0], [piece.at[0] for piece in pieces], rows)
     fill(mobile, index_ref[0], [piece.at[1] for piece in pieces], rows)
-
-    take_steps(window, mobile, *scratch, 9 * rows)
+    shift_kernel(mobile, mobile_before)
+    take_steps(window, mobile, mobile_before, *scratch, 9 * rows)
     out[...] = window[pl.ds(4 * rows, rows)]
 
 
 def later_kernel(index_ref, *refs):
-    pieces, mobile, out, window, *scratch = refs[:9], *refs[9:]
+    pieces, mobile, mobile_before, out, window, *scratch = refs[:9], *refs[9:]
     rows = out.shape[0]
     fill(window, index_ref[0], pieces, rows)
-    take_steps(window, mobile, *scratch, 9 * rows)
+    take_steps(window, mobile, mobile_before, *scratch, 9 * rows)
     out[...] = window[pl.ds(4 * rows, rows)]
 
 
@@ -212,11 +215,16 @@
     when(from_left == even, write, across)
 
 
-def gap_kernel(own, right, *refs):
-    *earlier, everyone = refs
-    rows = [ref[...] for ref in earlier] + [squares_of(own, right)]
-    for cycle, row in enumerate(rows):
-        everyone[:, cycle : cycle + 1] = jnp.broadcast_to(row[None], (everyone.shape[0], *row.shape))
+def halves(rows):
+    lanes = rows[0].shape[-1]
+    lane = lax.broadcasted_iota(jnp.int32, rows[0].shape, 1)
+    first, second = (row + pltpu.roll(row, lanes // 2, 1) for row in rows)
+    return jnp.where(lane < lanes // 2, first, second)
+
+
+def gap_kernel(own, right, earlier, everyone):
+    row = halves((earlier[...], squares_of(own, right)))
+    everyone[...] = jnp.broadcast_to(row[None], everyone.shape)
 
 
 def final_mix_kernel(index_ref, lower_ref, weight_ref, own, left, right, out):
@@ -236,14 +244,17 @@
 
 
 def length_kernel(cells, images, index_ref, gaps, length):
-    each = jnp.sum(gaps[...].reshape(images, -1, CYCLES, gaps.shape[-1]), axis=1)
-    distance = jnp.sqrt(jnp.sum(each, axis=-1, keepdims=True) / cells + epsilon)
-    position = lax.broadcasted_iota(jnp.int32, distance.shape, 0)
-    reached = jnp.sum(jnp.where(position < index_ref[0], distance, 0.0), axis=0)
+    lanes = gaps.shape[-1]
+    each = jnp.sum(gaps[...].reshape(images, -1, lanes), axis=1)
+    early = lax.broadcasted_iota(jnp.int32, each.shape, 1) < lanes // 2
+    position = lax.broadcasted_iota(jnp.int32, each.shape, 0)
     lane = lax.broadcasted_iota(jnp.int32, length.shape, 1)
     result = jnp.zeros(length.shape, jnp.float32)
-    for cycle in range(CYCLES):
-        result = jnp.where(lane == cycle, reached[cycle : cycle + 1], result)
+    for cycle, chosen in enumerate((early, jnp.logical_not(early))):
+        total = jnp.sum(jnp.where(chosen, each, 0.0), axis=1, keepdims=True)
+        distance = jnp.sqrt(total / cells + epsilon)
+        reached = jnp.sum(jnp.where(position[:, :1] < index_ref[0], distance, 0.0), axis=0, keepdims=True)
+        result = jnp.where(lane == cycle, reached, result)
     length[...] = result
 
 
@@ -255,9 +266,8 @@
     rows, depth, lanes = field.shape[1:]
     slab = (rows, depth // SUBLANES, SUBLANES, lanes)
     wide = (9 * rows,) + slab[1:]
-    windows = [pltpu.VMEM(wide, jnp.float32)] * 2
-    windows += [pltpu.VMEM((2 * lanes, 2 * lanes), jnp.bfloat16)]
-    windows += [pltpu.VMEM(wide, jnp.float32)] * 2
+    window = [pltpu.VMEM(wide, jnp.float32)]
+    scratch = [pltpu.VMEM((2 * lanes, 2 * lanes), jnp.bfloat16), *window, *window]
     image_count, domain_count = lax.axis_size("image"), lax.axis_size("domain")
     image_index = lax.axis_index("image")[None]
     index = lax.axis_index("domain")
@@ -267,7 +277,7 @@
     packed = pl.pallas_call(
         pack_kernel,
         out_shape=shaped(2, *slab),
-        in_specs=[pl.BlockSpec(memory_space=pltpu.HBM)] * 2,
+        in_specs=[HBM] * 2,
         out_specs=VMEM,
         scratch_shapes=[
             pltpu.VMEM((2, rows, depth, lanes), jnp.float32),
@@ -279,10 +289,17 @@
         first_kernel,
         out_shape=(shaped(*slab), shaped(*wide)),
         in_specs=[SMEM] + [VMEM] * 9,
-        out_specs=(VMEM,) * 2,
-        scratch_shapes=windows,
+        out_specs=(VMEM, VMEM),
+        scratch_shapes=[*window, *window, *scratch],
         compiler_params=PARAMS,
     )(index[None], *halo_pieces(packed, index))
+    mobile_before = pl.pallas_call(
+        shift_kernel,
+        out_shape=shaped(*wide),
+        in_specs=[VMEM],
+        out_specs=VMEM,
+        compiler_params=PARAMS,
+    )(mobile)
 
     totals = []
     for cycle in range(CYCLES - 1):
@@ -299,17 +316,17 @@
         phase = pl.pallas_call(
             later_kernel,
             out_shape=shaped(*slab),
-            in_specs=[SMEM] + [VMEM] * 10,
+            in_specs=[SMEM] + [VMEM] * 11,
             out_specs=VMEM,
-            scratch_shapes=windows,
+            scratch_shapes=[*window, *scratch],
             compiler_params=PARAMS,
-        )(index[None], *halo_pieces(phase, index), mobile)
+        )(index[None], *halo_pieces(phase, index), mobile, mobile_before)
     right = passed_along(phase, -1)
     left = passed_along(phase, 1)
     everyone = pl.pallas_call(
         gap_kernel,
-        out_shape=shaped(image_count * domain_count, CYCLES, lanes),
-        in_specs=[VMEM] * (2 + len(totals)),
+        out_shape=shaped(image_count * domain_count, 1, lanes),
+        in_specs=[VMEM] * 3,
         out_specs=VMEM,
         compiler_params=PARAMS,
     )(phase, right, *totals)

time: 109 us -> 106 us (0.972)
  waiting for transfers between devices: 30.1 us -> 26.7 us
    all_to_all x1, waiting for transfers between devices: 6.04 us -> 4.54 us  [cycles(): gaps = lax.all_to_all(everyone, ('image', 'domain'), 0, 0)]
  transfers between devices with their start and end apart: 21 -> 21, of which waited for: 10 -> 10; matrix products, arithmetic and copies ran while one was open for 0% -> 0% of each run, Pallas kernels for 1% -> 2%
where the time goes in v6:
time: 106 us
  starting transfers between devices  51.4 us (48%)
  waiting for transfers between devices  26.7 us (25%)
  Pallas kernels  24.8 us (23%)
  local copies, waits for them, and re-layouts  1.81 us (2%)
    ppermute x18, starting transfers between devices, exchanged(): lax.ppermute(value, axis, [(i, j) for i, j in pairs if 0 <= j < size])  33 us
    all_to_all x1, starting transfers between devices, cycles(): gaps = lax.all_to_all(everyone, ('image', 'domain'), 0, 0)  13.7 us
    ppermute x18, waiting for transfers between devices, exchanged(): lax.ppermute(value, axis, [(i, j) for i, j in pairs if 0 <= j < size])  13 us
    pallas_call x1, Pallas kernels, cycles(): pl.pallas_call(first_kernel, out_shape=(shaped(*slab), shaped(*wide)), in...  10.6 us
    pallas_call x1, Pallas kernels, cycles(): pl.pallas_call(later_kernel, out_shape=shaped(*slab), in_specs=[SMEM] + [...  9.63 us
    ppermute x2, waiting for transfers between devices, passed_along(): lax.ppermute(value, 'image', [(i, i + steps) for i in range(first, last)])  9.23 us
    ppermute x2, starting transfers between devices, passed_along(): lax.ppermute(value, 'image', [(i, i + steps) for i in range(first, last)])  4.69 us
    all_to_all x1, waiting for transfers between devices, cycles(): gaps = lax.all_to_all(everyone, ('image', 'domain'), 0, 0)  4.54 us
  transfers between devices with their start and end apart: 21, of which 10 were waited for; matrix products, arithmetic and copies ran while one was open for 0% of the time, Pallas kernels for 2%

profile of v6, /device:TPU:1, one launch (start us, length us, event | category | flops | bytes accessed | tf_op | source)
XLA Modules:
  0.0 105.6 jit_solution(16584274391131534142)
XLA Ops:
  0.6 0.0 copy-start
  0.6 0.9 copy-done
  1.5 0.0 copy-start.1
  1.5 0.9 copy-done.1
  2.4 0.4 shard_map.59.refs_0_
  2.8 2.2 %collective-permute-start.3 = (f32[2,4,8,8,128]{4,3,2,1,0:T(8,128)S(1)}, f32[2,4,8,8,128]{4,3,2,1,0:T(8,128)S(1)}, u32[]{:S(2)}, u32[]{:S(2)}) collective-permute-start(f32[2,4,8,8,128]{4,3,2,1,0:T(8,128)S(1)} %shard_map.59.refs_0_), channel_id=1, source_target_pairs={{0,4},{1,5},{2,6},{3,7},{4,0},{5,1},{6,2},{7,3},{8,12},{9,13},{10,... | collective-permute-start | bytes 786440 | tf_op jit(solution)/shard_map/ppermute | solution.py:26
  5.0 1.9 %collective-permute-start.2 = (f32[2,4,8,8,128]{4,3,2,1,0:T(8,128)S(1)}, f32[2,4,8,8,128]{4,3,2,1,0:T(8,128)S(1)}, u32[]{:S(2)}, u32[]{:S(2)}) collective-permute-start(f32[2,4,8,8,128]{4,3,2,1,0:T(8,128)S(1)} %shard_map.59.refs_0_), channel_id=1, source_target_pairs={{0,12},{1,13},{2,14},{3,15},{4,8},{5,9},{6,10},{7,11},{8,4},{9,5},... | collective-permute-start | bytes 786440 | tf_op jit(solution)/shard_map/ppermute | solution.py:26
  6.9 2.7 %collective-permute-start.1 = (f32[2,4,8,8,128]{4,3,2,1,0:T(8,128)S(1)}, f32[2,4,8,8,128]{4,3,2,1,0:T(8,128)S(1)}, u32[]{:S(2)}, u32[]{:S(2)}) collective-permute-start(f32[2,4,8,8,128]{4,3,2,1,0:T(8,128)S(1)} %shard_map.59.refs_0_), channel_id=1, source_target_pairs={{0,2},{1,3},{2,0},{3,1},{4,6},{5,7},{6,4},{7,5},{8,10},{9,11},{10,... | collective-permute-start | bytes 786440 | tf_op jit(solution)/shard_map/ppermute | solution.py:26
  9.7 0.7 collective-permute-start
  10.4 2.0 %collective-permute-start.4 = (f32[2,4,8,8,128]{4,3,2,1,0:T(8,128)S(1)}, f32[2,4,8,8,128]{4,3,2,1,0:T(8,128)S(1)}, u32[]{:S(2)}, u32[]{:S(2)}) collective-permute-start(f32[2,4,8,8,128]{4,3,2,1,0:T(8,128)S(1)} %shard_map.59.refs_0_), channel_id=1, source_target_pairs={{0,1},{1,0},{2,3},{3,2},{4,5},{5,4},{6,7},{7,6},{8,9},{9,8},{10,11... | collective-permute-start | bytes 786440 | tf_op jit(solution)/shard_map/ppermute | solution.py:26
  12.4 0.0 collective-permute-done.3.refs_4_
  12.4 0.5 collective-permute-done.2.refs_3_
  12.9 2.1 %collective-permute-start.7 = (f32[2,4,8,8,128]{4,3,2,1,0:T(8,128)S(1)}, f32[2,4,8,8,128]{4,3,2,1,0:T(8,128)S(1)}, u32[]{:S(2)}, u32[]{:S(2)}) collective-permute-start(f32[2,4,8,8,128]{4,3,2,1,0:T(8,128)S(1)} %broadcast_select_fusion), channel_id=1, source_target_pairs={{0,1},{1,0},{2,3},{3,2},{4,5},{5,4},{6,7},{7,6},{8,9},{9,8},{10,11... | collective-permute-start | bytes 786440 | tf_op jit(solution)/shard_map/ppermute | solution.py:26
  15.1 0.0 collective-permute-done.1.refs_2_
  15.1 3.8 %collective-permute-start.6 = (f32[2,4,8,8,128]{4,3,2,1,0:T(8,128)S(1)}, f32[2,4,8,8,128]{4,3,2,1,0:T(8,128)S(1)}, u32[]{:S(2)}, u32[]{:S(2)}) collective-permute-start(f32[2,4,8,8,128]{4,3,2,1,0:T(8,128)S(1)} %collective-permute-done.1.refs_2_), channel_id=1, source_target_pairs={{0,1},{1,0},{2,3},{3,2},{4,5},{5,4},{6,7},{7,6},{8,9},{9,8},{10,11... | collective-permute-start | bytes 786440 | tf_op jit(solution)/shard_map/ppermute | solution.py:26
  18.9 2.8 %collective-permute-done.refs_1_ = f32[2,4,8,8,128]{4,3,2,1,0:T(8,128)S(1)} collective-permute-done((f32[2,4,8,8,128]{4,3,2,1,0:T(8,128)S(1)}, f32[2,4,8,8,128]{4,3,2,1,0:T(8,128)S(1)}, u32[]{:S(2)}, u32[]{:S(2)}) %collective-permute-start) | collective-permute-done | bytes 262176 | tf_op jit(solution)/shard_map/ppermute | solution.py:26
  21.6 1.7 %collective-permute-start.5 = (f32[2,4,8,8,128]{4,3,2,1,0:T(8,128)S(1)}, f32[2,4,8,8,128]{4,3,2,1,0:T(8,128)S(1)}, u32[]{:S(2)}, u32[]{:S(2)}) collective-permute-start(f32[2,4,8,8,128]{4,3,2,1,0:T(8,128)S(1)} %collective-permute-done.refs_1_), channel_id=1, source_target_pairs={{0,1},{1,0},{2,3},{3,2},{4,5},{5,4},{6,7},{7,6},{8,9},{9,8},{10,11... | collective-permute-start | bytes 786440 | tf_op jit(solution)/shard_map/ppermute | solution.py:26
  23.3 0.0 collective-permute-done.4.refs_5_
  23.3 0.0 collective-permute-done.7.refs_8_
  23.3 0.0 collective-permute-done.6.refs_7_
  23.3 1.1 %collective-permute-done.5.refs_6_ = f32[2,4,8,8,128]{4,3,2,1,0:T(8,128)S(1)} collective-permute-done((f32[2,4,8,8,128]{4,3,2,1,0:T(8,128)S(1)}, f32[2,4,8,8,128]{4,3,2,1,0:T(8,128)S(1)}, u32[]{:S(2)}, u32[]{:S(2)}) %collective-permute-start.5) | collective-permute-done | bytes 262176 | tf_op jit(solution)/shard_map/ppermute | solution.py:26
  24.4 0.0 copy-start.2
  24.4 0.0 copy-start.3
  24.4 10.6 %shard_map.60 = (f32[4,8,8,128]{3,2,1,0:T(8,128)S(1)}, f32[36,8,8,128]{3,2,1,0:T(8,128)S(1)}) custom-call(s32[1]{0:T(128)} %bitcast.3.index_ref, f32[2,4,8,8,128]{4,3,2,1,0:T(8,128)S(1)} %shard_map.59.refs_0_, f32[2,4,8,8,128]{4,3,2,1,0:T(8,128)S(1)} %collective-permute-done.refs_1_, f32[2,4,8,8,128]{4,3,2,1,0:T(8,128)S(1)} %collective-permute-done.1.refs_2_, ...), custom_call_target="tpu_custom_call" | custom-call | tf_op jit(solution)/shard_map/pallas_call | solution.py:288
  35.0 0.7 collective-permute-start.9
  35.7 4.6 %collective-permute-start.8 = (f32[4,8,8,128]{3,2,1,0:T(8,128)S(1)}, f32[4,8,8,128]{3,2,1,0:T(8,128)S(1)}, u32[]{:S(2)}, u32[]{:S(2)}) collective-permute-start(f32[4,8,8,128]{3,2,1,0:T(8,128)S(1)} %get-tuple-element.6.refs_3_), channel_id=1, source_target_pairs={{0,16},{16,0},{32,48},{48,32},{64,80},{80,64},{96,112},{112,96},{1... | collective-permute-start | bytes 393224 | tf_op jit(solution)/shard_map/ppermute | solution.py:26
  40.3 0.0 collective-permute-done.9.refs_5_
  40.3 3.2 %collective-permute-done.8.refs_4_ = f32[4,8,8,128]{3,2,1,0:T(8,128)S(1)} collective-permute-done((f32[4,8,8,128]{3,2,1,0:T(8,128)S(1)}, f32[4,8,8,128]{3,2,1,0:T(8,128)S(1)}, u32[]{:S(2)}, u32[]{:S(2)}) %collective-permute-start.8) | collective-permute-done | bytes 131104 | tf_op jit(solution)/shard_map/ppermute | solution.py:26
  43.5 0.0 copy-done.2
  43.5 0.0 copy-done.3
  43.5 0.6 shard_map.61
  44.1 0.8 collective-permute-start.13
  44.9 1.0 collective-permute-start.12
  45.9 1.8 %collective-permute-start.14 = (f32[4,8,8,128]{3,2,1,0:T(8,128)S(1)}, f32[4,8,8,128]{3,2,1,0:T(8,128)S(1)}, u32[]{:S(2)}, u32[]{:S(2)}) collective-permute-start(f32[4,8,8,128]{3,2,1,0:T(8,128)S(1)} %get-tuple-element.7.refs_0_), channel_id=1, source_target_pairs={{0,1},{1,0},{2,3},{3,2},{4,5},{5,4},{6,7},{7,6},{8,9},{9,8},{10,11... | collective-permute-start | bytes 393224 | tf_op jit(solution)/shard_map/ppermute | solution.py:26
  47.7 2.8 %collective-permute-start.11 = (f32[4,8,8,128]{3,2,1,0:T(8,128)S(1)}, f32[4,8,8,128]{3,2,1,0:T(8,128)S(1)}, u32[]{:S(2)}, u32[]{:S(2)}) collective-permute-start(f32[4,8,8,128]{3,2,1,0:T(8,128)S(1)} %get-tuple-element.7.refs_0_), channel_id=1, source_target_pairs={{0,2},{1,3},{2,0},{3,1},{4,6},{5,7},{6,4},{7,5},{8,10},{9,11},{10,... | collective-permute-start | bytes 393224 | tf_op jit(solution)/shard_map/ppermute | solution.py:26
  50.5 1.6 %collective-permute-start.10 = (f32[4,8,8,128]{3,2,1,0:T(8,128)S(1)}, f32[4,8,8,128]{3,2,1,0:T(8,128)S(1)}, u32[]{:S(2)}, u32[]{:S(2)}) collective-permute-start(f32[4,8,8,128]{3,2,1,0:T(8,128)S(1)} %get-tuple-element.7.refs_0_), channel_id=1, source_target_pairs={{0,14},{1,15},{2,4},{3,5},{4,2},{5,3},{6,8},{7,9},{8,6},{9,7},{10,... | collective-permute-start | bytes 393224 | tf_op jit(solution)/shard_map/ppermute | solution.py:26
  52.1 0.0 collective-permute-done.13.refs_4_
  52.1 0.0 collective-permute-done.12.refs_3_
  52.1 0.6 collective-permute-start.17
  52.7 1.5 %collective-permute-done.11.refs_2_ = f32[4,8,8,128]{3,2,1,0:T(8,128)S(1)} collective-permute-done((f32[4,8,8,128]{3,2,1,0:T(8,128)S(1)}, f32[4,8,8,128]{3,2,1,0:T(8,128)S(1)}, u32[]{:S(2)}, u32[]{:S(2)}) %collective-permute-start.11) | collective-permute-done | bytes 131104 | tf_op jit(solution)/shard_map/ppermute | solution.py:26
  54.3 0.9 collective-permute-start.16
  55.1 3.7 %collective-permute-done.10.refs_1_ = f32[4,8,8,128]{3,2,1,0:T(8,128)S(1)} collective-permute-done((f32[4,8,8,128]{3,2,1,0:T(8,128)S(1)}, f32[4,8,8,128]{3,2,1,0:T(8,128)S(1)}, u32[]{:S(2)}, u32[]{:S(2)}) %collective-permute-start.10) | collective-permute-done | bytes 131104 | tf_op jit(solution)/shard_map/ppermute | solution.py:26
  58.9 1.1 %collective-permute-start.15 = (f32[4,8,8,128]{3,2,1,0:T(8,128)S(1)}, f32[4,8,8,128]{3,2,1,0:T(8,128)S(1)}, u32[]{:S(2)}, u32[]{:S(2)}) collective-permute-start(f32[4,8,8,128]{3,2,1,0:T(8,128)S(1)} %collective-permute-done.10.refs_1_), channel_id=1, source_target_pairs={{0,1},{1,0},{2,3},{3,2},{4,5},{5,4},{6,7},{7,6},{8,9},{9,8},{10,11... | collective-permute-start | bytes 393224 | tf_op jit(solution)/shard_map/ppermute | solution.py:26
  60.0 0.9 shard_map.62.refs_10_
  60.9 0.0 collective-permute-done.14.refs_5_
  60.9 0.0 collective-permute-done.17.refs_8_
  60.9 0.0 collective-permute-done.16.refs_7_
  60.9 0.1 collective-permute-done.15.refs_6_
  61.0 9.6 %shard_map.63.own = f32[4,8,8,128]{3,2,1,0:T(8,128)S(1)} custom-call(s32[1]{0:T(128)} %bitcast.3.index_ref, f32[4,8,8,128]{3,2,1,0:T(8,128)S(1)} %get-tuple-element.7.refs_0_, f32[4,8,8,128]{3,2,1,0:T(8,128)S(1)} %collective-permute-done.10.refs_1_, f32[4,8,8,128]{3,2,1,0:T(8,128)S(1)} %collective-permute-done.11.refs_2_, ...), custom_call_target="tpu_custom_call" | custom-call | tf_op jit(solution)/shard_map/pallas_call | solution.py:316
  70.6 1.3 %collective-permute-start.19 = (f32[4,8,8,128]{3,2,1,0:T(8,128)S(1)}, f32[4,8,8,128]{3,2,1,0:T(8,128)S(1)}, u32[]{:S(2)}, u32[]{:S(2)}) collective-permute-start(f32[4,8,8,128]{3,2,1,0:T(8,128)S(1)} %shard_map.63.own), channel_id=1, source_target_pairs={{16,0},{32,16},{48,32},{64,48},{80,64},{96,80},{112,96},{128,112},... | collective-permute-start | bytes 393224 | tf_op jit(solution)/shard_map/ppermute | solution.py:32
  71.9 5.3 %collective-permute-done.19.right = f32[4,8,8,128]{3,2,1,0:T(8,128)S(1)} collective-permute-done((f32[4,8,8,128]{3,2,1,0:T(8,128)S(1)}, f32[4,8,8,128]{3,2,1,0:T(8,128)S(1)}, u32[]{:S(2)}, u32[]{:S(2)}) %collective-permute-start.19) | collective-permute-done | bytes 131104 | tf_op jit(solution)/shard_map/ppermute | solution.py:32
  77.2 0.8 shard_map.65
  78.1 13.7 %all-to-all-start = ((f32[256,1,128]{2,1,0:T(1,128)}), f32[256,1,128]{2,1,0:T(1,128)S(1)}, u32[]{:S(2)}, u32[]{:S(2)}) async-start(f32[256,1,128]{2,1,0:T(1,128)} %shard_map.65), calls=%async_computation | async-start | bytes 262144 | tf_op jit(solution)/shard_map/all_to_all | solution.py:333
  91.8 3.4 %collective-permute-start.18 = (f32[4,8,8,128]{3,2,1,0:T(8,128)S(1)}, f32[4,8,8,128]{3,2,1,0:T(8,128)S(1)}, u32[]{:S(2)}, u32[]{:S(2)}) collective-permute-start(f32[4,8,8,128]{3,2,1,0:T(8,128)S(1)} %shard_map.63.own), channel_id=1, source_target_pairs={{0,16},{16,32},{32,48},{48,64},{64,80},{80,96},{96,112},{112,128},... | collective-permute-start | bytes 393224 | tf_op jit(solution)/shard_map/ppermute | solution.py:32
  95.2 3.9 %collective-permute-done.18.left = f32[4,8,8,128]{3,2,1,0:T(8,128)S(1)} collective-permute-done((f32[4,8,8,128]{3,2,1,0:T(8,128)S(1)}, f32[4,8,8,128]{3,2,1,0:T(8,128)S(1)}, u32[]{:S(2)}, u32[]{:S(2)}) %collective-permute-start.18) | collective-permute-done | bytes 131104 | tf_op jit(solution)/shard_map/ppermute | solution.py:32
  99.1 1.2 %shard_map.64 = f32[4,64,128]{2,1,0:T(8,128)} custom-call(s32[1]{0:T(128)} %bitcast.refs_0_.index_ref, s32[1,2]{1,0:T(1,128)S(1)} %bitcast.9, f32[1,2]{1,0:T(1,128)S(1)} %bitcast.11, f32[4,8,8,128]{3,2,1,0:T(8,128)S(1)} %shard_map.63.own, f32[4,8,8,128]{3,2,1,0:T(8,128)S(1)} %collective-permute-done.18.left, f32[4,8,8,128]{3,2,1,0:T(8,128)S(1)} %collective-permute-done.19.right), custom_call_target="tpu_custom_call" | custom-call | tf_op jit(solution)/shard_map/pallas_call | solution.py:334
  100.4 4.5 %all-to-all-done.refs_1_ = f32[256,1,128]{2,1,0:T(1,128)S(1)} async-done(((f32[256,1,128]{2,1,0:T(1,128)}), f32[256,1,128]{2,1,0:T(1,128)S(1)}, u32[]{:S(2)}, u32[]{:S(2)}) %all-to-all-start) | async-done | bytes 131104 | tf_op jit(solution)/shard_map/all_to_all | solution.py:333
  104.9 0.7 shard_map.66
  (2 shorter events, 0.0 us)
Async XLA Ops:
  0.6 0.9 copy-start
  1.5 0.9 copy-start.1
  2.8 9.6 %collective-permute-start.3 = (f32[2,4,8,8,128]{4,3,2,1,0:T(8,128)S(1)}, f32[2,4,8,8,128]{4,3,2,1,0:T(8,128)S(1)}, u32[]{:S(2)}, u32[]{:S(2)}) collective-permute-start(f32[2,4,8,8,128]{4,3,2,1,0:T(8,128)S(1)} %shard_map.59.refs_0_), channel_id=1, source_target_pairs={{0,4},{1,5},{2,6},{3,7},{4,0},{5,1},{6,2},{7,3},{8,12},{9,13},{10,... | collective-permute-start | bytes 786440 | tf_op jit(solution)/shard_map/ppermute | solution.py:26
  5.0 7.9 %collective-permute-start.2 = (f32[2,4,8,8,128]{4,3,2,1,0:T(8,128)S(1)}, f32[2,4,8,8,128]{4,3,2,1,0:T(8,128)S(1)}, u32[]{:S(2)}, u32[]{:S(2)}) collective-permute-start(f32[2,4,8,8,128]{4,3,2,1,0:T(8,128)S(1)} %shard_map.59.refs_0_), channel_id=1, source_target_pairs={{0,12},{1,13},{2,14},{3,15},{4,8},{5,9},{6,10},{7,11},{8,4},{9,5},... | collective-permute-start | bytes 786440 | tf_op jit(solution)/shard_map/ppermute | solution.py:26
  6.9 8.2 %collective-permute-start.1 = (f32[2,4,8,8,128]{4,3,2,1,0:T(8,128)S(1)}, f32[2,4,8,8,128]{4,3,2,1,0:T(8,128)S(1)}, u32[]{:S(2)}, u32[]{:S(2)}) collective-permute-start(f32[2,4,8,8,128]{4,3,2,1,0:T(8,128)S(1)} %shard_map.59.refs_0_), channel_id=1, source_target_pairs={{0,2},{1,3},{2,0},{3,1},{4,6},{5,7},{6,4},{7,5},{8,10},{9,11},{10,... | collective-permute-start | bytes 786440 | tf_op jit(solution)/shard_map/ppermute | solution.py:26
  9.7 11.9 %collective-permute-start = (f32[2,4,8,8,128]{4,3,2,1,0:T(8,128)S(1)}, f32[2,4,8,8,128]{4,3,2,1,0:T(8,128)S(1)}, u32[]{:S(2)}, u32[]{:S(2)}) collective-permute-start(f32[2,4,8,8,128]{4,3,2,1,0:T(8,128)S(1)} %shard_map.59.refs_0_), channel_id=1, source_target_pairs={{0,14},{1,15},{2,4},{3,5},{4,2},{5,3},{6,8},{7,9},{8,6},{9,7},{10,... | collective-permute-start | bytes 786440 | tf_op jit(solution)/shard_map/ppermute | solution.py:26
  10.4 12.9 %collective-permute-start.4 = (f32[2,4,8,8,128]{4,3,2,1,0:T(8,128)S(1)}, f32[2,4,8,8,128]{4,3,2,1,0:T(8,128)S(1)}, u32[]{:S(2)}, u32[]{:S(2)}) collective-permute-start(f32[2,4,8,8,128]{4,3,2,1,0:T(8,128)S(1)} %shard_map.59.refs_0_), channel_id=1, source_target_pairs={{0,1},{1,0},{2,3},{3,2},{4,5},{5,4},{6,7},{7,6},{8,9},{9,8},{10,11... | collective-permute-start | bytes 786440 | tf_op jit(solution)/shard_map/ppermute | solution.py:26
  12.9 10.3 %collective-permute-start.7 = (f32[2,4,8,8,128]{4,3,2,1,0:T(8,128)S(1)}, f32[2,4,8,8,128]{4,3,2,1,0:T(8,128)S(1)}, u32[]{:S(2)}, u32[]{:S(2)}) collective-permute-start(f32[2,4,8,8,128]{4,3,2,1,0:T(8,128)S(1)} %broadcast_select_fusion), channel_id=1, source_target_pairs={{0,1},{1,0},{2,3},{3,2},{4,5},{5,4},{6,7},{7,6},{8,9},{9,8},{10,11... | collective-permute-start | bytes 786440 | tf_op jit(solution)/shard_map/ppermute | solution.py:26
  15.1 8.2 %collective-permute-start.6 = (f32[2,4,8,8,128]{4,3,2,1,0:T(8,128)S(1)}, f32[2,4,8,8,128]{4,3,2,1,0:T(8,128)S(1)}, u32[]{:S(2)}, u32[]{:S(2)}) collective-permute-start(f32[2,4,8,8,128]{4,3,2,1,0:T(8,128)S(1)} %collective-permute-done.1.refs_2_), channel_id=1, source_target_pairs={{0,1},{1,0},{2,3},{3,2},{4,5},{5,4},{6,7},{7,6},{8,9},{9,8},{10,11... | collective-permute-start | bytes 786440 | tf_op jit(solution)/shard_map/ppermute | solution.py:26
  21.6 2.8 %collective-permute-start.5 = (f32[2,4,8,8,128]{4,3,2,1,0:T(8,128)S(1)}, f32[2,4,8,8,128]{4,3,2,1,0:T(8,128)S(1)}, u32[]{:S(2)}, u32[]{:S(2)}) collective-permute-start(f32[2,4,8,8,128]{4,3,2,1,0:T(8,128)S(1)} %collective-permute-done.refs_1_), channel_id=1, source_target_pairs={{0,1},{1,0},{2,3},{3,2},{4,5},{5,4},{6,7},{7,6},{8,9},{9,8},{10,11... | collective-permute-start | bytes 786440 | tf_op jit(solution)/shard_map/ppermute | solution.py:26
  24.4 19.1 %copy-start.2 = (s32[2,1]{0,1:T(1,128)S(1)}, s32[2,1]{0,1:T(1,128)}, u32[]{:S(2)}) copy-start(s32[2,1]{0,1:T(1,128)} %param.6) | copy-start | bytes 28
  24.4 19.1 %copy-start.3 = (f32[2,1]{0,1:T(1,128)S(1)}, f32[2,1]{0,1:T(1,128)}, u32[]{:S(2)}) copy-start(f32[2,1]{0,1:T(1,128)} %param.7) | copy-start | bytes 28
  35.0 5.3 %collective-permute-start.9 = (f32[4,8,8,128]{3,2,1,0:T(8,128)S(1)}, f32[4,8,8,128]{3,2,1,0:T(8,128)S(1)}, u32[]{:S(2)}, u32[]{:S(2)}) collective-permute-start(f32[4,8,8,128]{3,2,1,0:T(8,128)S(1)} %get-tuple-element.6.refs_3_), channel_id=1, source_target_pairs={{16,32},{32,16},{48,64},{64,48},{80,96},{96,80},{112,128},{128,112... | collective-permute-start | bytes 393224 | tf_op jit(solution)/shard_map/ppermute | solution.py:26
  35.7 7.8 %collective-permute-start.8 = (f32[4,8,8,128]{3,2,1,0:T(8,128)S(1)}, f32[4,8,8,128]{3,2,1,0:T(8,128)S(1)}, u32[]{:S(2)}, u32[]{:S(2)}) collective-permute-start(f32[4,8,8,128]{3,2,1,0:T(8,128)S(1)} %get-tuple-element.6.refs_3_), channel_id=1, source_target_pairs={{0,16},{16,0},{32,48},{48,32},{64,80},{80,64},{96,112},{112,96},{1... | collective-permute-start | bytes 393224 | tf_op jit(solution)/shard_map/ppermute | solution.py:26
  44.1 7.9 %collective-permute-start.13 = (f32[4,8,8,128]{3,2,1,0:T(8,128)S(1)}, f32[4,8,8,128]{3,2,1,0:T(8,128)S(1)}, u32[]{:S(2)}, u32[]{:S(2)}) collective-permute-start(f32[4,8,8,128]{3,2,1,0:T(8,128)S(1)} %get-tuple-element.7.refs_0_), channel_id=1, source_target_pairs={{0,4},{1,5},{2,6},{3,7},{4,0},{5,1},{6,2},{7,3},{8,12},{9,13},{10,... | collective-permute-start | bytes 393224 | tf_op jit(solution)/shard_map/ppermute | solution.py:26
  44.9 7.2 %collective-permute-start.12 = (f32[4,8,8,128]{3,2,1,0:T(8,128)S(1)}, f32[4,8,8,128]{3,2,1,0:T(8,128)S(1)}, u32[]{:S(2)}, u32[]{:S(2)}) collective-permute-start(f32[4,8,8,128]{3,2,1,0:T(8,128)S(1)} %get-tuple-element.7.refs_0_), channel_id=1, source_target_pairs={{0,12},{1,13},{2,14},{3,15},{4,8},{5,9},{6,10},{7,11},{8,4},{9,5},... | collective-permute-start | bytes 393224 | tf_op jit(solution)/shard_map/ppermute | solution.py:26
  45.9 15.0 %collective-permute-start.14 = (f32[4,8,8,128]{3,2,1,0:T(8,128)S(1)}, f32[4,8,8,128]{3,2,1,0:T(8,128)S(1)}, u32[]{:S(2)}, u32[]{:S(2)}) collective-permute-start(f32[4,8,8,128]{3,2,1,0:T(8,128)S(1)} %get-tuple-element.7.refs_0_), channel_id=1, source_target_pairs={{0,1},{1,0},{2,3},{3,2},{4,5},{5,4},{6,7},{7,6},{8,9},{9,8},{10,11... | collective-permute-start | bytes 393224 | tf_op jit(solution)/shard_map/ppermute | solution.py:26
  47.7 6.6 %collective-permute-start.11 = (f32[4,8,8,128]{3,2,1,0:T(8,128)S(1)}, f32[4,8,8,128]{3,2,1,0:T(8,128)S(1)}, u32[]{:S(2)}, u32[]{:S(2)}) collective-permute-start(f32[4,8,8,128]{3,2,1,0:T(8,128)S(1)} %get-tuple-element.7.refs_0_), channel_id=1, source_target_pairs={{0,2},{1,3},{2,0},{3,1},{4,6},{5,7},{6,4},{7,5},{8,10},{9,11},{10,... | collective-permute-start | bytes 393224 | tf_op jit(solution)/shard_map/ppermute | solution.py:26
  50.5 8.4 %collective-permute-start.10 = (f32[4,8,8,128]{3,2,1,0:T(8,128)S(1)}, f32[4,8,8,128]{3,2,1,0:T(8,128)S(1)}, u32[]{:S(2)}, u32[]{:S(2)}) collective-permute-start(f32[4,8,8,128]{3,2,1,0:T(8,128)S(1)} %get-tuple-element.7.refs_0_), channel_id=1, source_target_pairs={{0,14},{1,15},{2,4},{3,5},{4,2},{5,3},{6,8},{7,9},{8,6},{9,7},{10,... | collective-permute-start | bytes 393224 | tf_op jit(solution)/shard_map/ppermute | solution.py:26
  52.1 8.8 %collective-permute-start.17 = (f32[4,8,8,128]{3,2,1,0:T(8,128)S(1)}, f32[4,8,8,128]{3,2,1,0:T(8,128)S(1)}, u32[]{:S(2)}, u32[]{:S(2)}) collective-permute-start(f32[4,8,8,128]{3,2,1,0:T(8,128)S(1)} %broadcast_select_fusion.1), channel_id=1, source_target_pairs={{0,1},{1,0},{2,3},{3,2},{4,5},{5,4},{6,7},{7,6},{8,9},{9,8},{10,11... | collective-permute-start | bytes 393224 | tf_op jit(solution)/shard_map/ppermute | solution.py:26
  54.3 6.7 %collective-permute-start.16 = (f32[4,8,8,128]{3,2,1,0:T(8,128)S(1)}, f32[4,8,8,128]{3,2,1,0:T(8,128)S(1)}, u32[]{:S(2)}, u32[]{:S(2)}) collective-permute-start(f32[4,8,8,128]{3,2,1,0:T(8,128)S(1)} %collective-permute-done.11.refs_2_), channel_id=1, source_target_pairs={{0,1},{1,0},{2,3},{3,2},{4,5},{5,4},{6,7},{7,6},{8,9},{9,8},{10,11... | collective-permute-start | bytes 393224 | tf_op jit(solution)/shard_map/ppermute | solution.py:26
  58.9 2.1 %collective-permute-start.15 = (f32[4,8,8,128]{3,2,1,0:T(8,128)S(1)}, f32[4,8,8,128]{3,2,1,0:T(8,128)S(1)}, u32[]{:S(2)}, u32[]{:S(2)}) collective-permute-start(f32[4,8,8,128]{3,2,1,0:T(8,128)S(1)} %collective-permute-done.10.refs_1_), channel_id=1, source_target_pairs={{0,1},{1,0},{2,3},{3,2},{4,5},{5,4},{6,7},{7,6},{8,9},{9,8},{10,11... | collective-permute-start | bytes 393224 | tf_op jit(solution)/shard_map/ppermute | solution.py:26
  70.6 6.6 %collective-permute-start.19 = (f32[4,8,8,128]{3,2,1,0:T(8,128)S(1)}, f32[4,8,8,128]{3,2,1,0:T(8,128)S(1)}, u32[]{:S(2)}, u32[]{:S(2)}) collective-permute-start(f32[4,8,8,128]{3,2,1,0:T(8,128)S(1)} %shard_map.63.own), channel_id=1, source_target_pairs={{16,0},{32,16},{48,32},{64,48},{80,64},{96,80},{112,96},{128,112},... | collective-permute-start | bytes 393224 | tf_op jit(solution)/shard_map/ppermute | solution.py:32
  78.1 26.8 %all-to-all-start = ((f32[256,1,128]{2,1,0:T(1,128)}), f32[256,1,128]{2,1,0:T(1,128)S(1)}, u32[]{:S(2)}, u32[]{:S(2)}) async-start(f32[256,1,128]{2,1,0:T(1,128)} %shard_map.65), calls=%async_computation | async-start | bytes 262144 | tf_op jit(solution)/shard_map/all_to_all | solution.py:333
  91.8 7.3 %collective-permute-start.18 = (f32[4,8,8,128]{3,2,1,0:T(8,128)S(1)}, f32[4,8,8,128]{3,2,1,0:T(8,128)S(1)}, u32[]{:S(2)}, u32[]{:S(2)}) collective-permute-start(f32[4,8,8,128]{3,2,1,0:T(8,128)S(1)} %shard_map.63.own), channel_id=1, source_target_pairs={{0,16},{16,32},{32,48},{48,64},{64,80},{80,96},{96,112},{112,128},... | collective-permute-start | bytes 393224 | tf_op jit(solution)/shard_map/ppermute | solution.py:32

commit v7 on v6

--- a/solution.py
+++ b/solution.py
@@ -44,15 +44,21 @@
     return lambda i, size: (i - side(i, stride) * stride) % size
 
 
+CORE_STARTS = ("core_inside_two", "core_across_two", "core_chosen")
+
+
 def halo_pieces(own, index):
     straight = []
     for partner, stride in zip((partner_across, partner_inside) * 2, (2, 2, 4, 4)):
         straight.append(exchanged(own, "domain", partner(stride)))
-    *twos, across, inside = straight
+    across_two, inside_two, across, inside = straight
+    beside = exchanged(own, "domain", partner_inside(1))
+    others = {}
+    for name, piece in zip(CORE_STARTS[:2], (inside_two, across_two)):
+        others[name] = exchanged(piece, "domain", partner_inside(1))
     chosen = jnp.where(side(index, 4) == side(index, 1), inside, across)
-    beside = exchanged(own, "domain", partner_inside(1))
-    others = [exchanged(piece, "domain", partner_inside(1)) for piece in (*twos, chosen)]
-    return [own, *straight, beside, *others]
+    last = exchanged(chosen, "domain", partner_inside(1))
+    return [own, *straight, beside, others[CORE_STARTS[1]], others[CORE_STARTS[0]], last]
 
 
 def slab_offsets(index):

time: 106 us -> 106 us (level)
  no operation moved by 1% of the time
where the time goes in v7:
time: 106 us
  starting transfers between devices  51.4 us (48%)
  waiting for transfers between devices  26.7 us (25%)
  Pallas kernels  24.8 us (23%)
  local copies, waits for them, and re-layouts  1.81 us (2%)
    ppermute x18, starting transfers between devices, exchanged(): lax.ppermute(value, axis, [(i, j) for i, j in pairs if 0 <= j < size])  33 us
    all_to_all x1, starting transfers between devices, cycles(): gaps = lax.all_to_all(everyone, ('image', 'domain'), 0, 0)  13.7 us
    ppermute x18, waiting for transfers between devices, exchanged(): lax.ppermute(value, axis, [(i, j) for i, j in pairs if 0 <= j < size])  13 us
    pallas_call x1, Pallas kernels, cycles(): pl.pallas_call(first_kernel, out_shape=(shaped(*slab), shaped(*wide)), in...  10.6 us
    pallas_call x1, Pallas kernels, cycles(): pl.pallas_call(later_kernel, out_shape=shaped(*slab), in_specs=[SMEM] + [...  9.63 us
    ppermute x2, waiting for transfers between devices, passed_along(): lax.ppermute(value, 'image', [(i, i + steps) for i in range(first, last)])  9.23 us
    ppermute x2, starting transfers between devices, passed_along(): lax.ppermute(value, 'image', [(i, i + steps) for i in range(first, last)])  4.69 us
    all_to_all x1, waiting for transfers between devices, cycles(): gaps = lax.all_to_all(everyone, ('image', 'domain'), 0, 0)  4.54 us
  transfers between devices with their start and end apart: 21, of which 10 were waited for; matrix products, arithmetic and copies ran while one was open for 0% of the time, Pallas kernels for 2%

profile of v7, /device:TPU:1, one launch (start us, length us, event | category | flops | bytes accessed | tf_op | source)
XLA Modules:
  0.0 105.6 jit_solution(16584274391131534142)
XLA Ops:
  0.6 0.0 copy-start
  0.6 0.9 copy-done
  1.5 0.0 copy-start.1
  1.5 0.9 copy-done.1
  2.4 0.4 shard_map.59.refs_0_
  2.8 2.2 %collective-permute-start.3 = (f32[2,4,8,8,128]{4,3,2,1,0:T(8,128)S(1)}, f32[2,4,8,8,128]{4,3,2,1,0:T(8,128)S(1)}, u32[]{:S(2)}, u32[]{:S(2)}) collective-permute-start(f32[2,4,8,8,128]{4,3,2,1,0:T(8,128)S(1)} %shard_map.59.refs_0_), channel_id=1, source_target_pairs={{0,4},{1,5},{2,6},{3,7},{4,0},{5,1},{6,2},{7,3},{8,12},{9,13},{10,... | collective-permute-start | bytes 786440 | tf_op jit(solution)/shard_map/ppermute | solution.py:26
  5.0 1.9 %collective-permute-start.2 = (f32[2,4,8,8,128]{4,3,2,1,0:T(8,128)S(1)}, f32[2,4,8,8,128]{4,3,2,1,0:T(8,128)S(1)}, u32[]{:S(2)}, u32[]{:S(2)}) collective-permute-start(f32[2,4,8,8,128]{4,3,2,1,0:T(8,128)S(1)} %shard_map.59.refs_0_), channel_id=1, source_target_pairs={{0,12},{1,13},{2,14},{3,15},{4,8},{5,9},{6,10},{7,11},{8,4},{9,5},... | collective-permute-start | bytes 786440 | tf_op jit(solution)/shard_map/ppermute | solution.py:26
  6.9 2.7 %collective-permute-start.1 = (f32[2,4,8,8,128]{4,3,2,1,0:T(8,128)S(1)}, f32[2,4,8,8,128]{4,3,2,1,0:T(8,128)S(1)}, u32[]{:S(2)}, u32[]{:S(2)}) collective-permute-start(f32[2,4,8,8,128]{4,3,2,1,0:T(8,128)S(1)} %shard_map.59.refs_0_), channel_id=1, source_target_pairs={{0,2},{1,3},{2,0},{3,1},{4,6},{5,7},{6,4},{7,5},{8,10},{9,11},{10,... | collective-permute-start | bytes 786440 | tf_op jit(solution)/shard_map/ppermute | solution.py:26
  9.7 0.7 collective-permute-start
  10.4 2.0 %collective-permute-start.4 = (f32[2,4,8,8,128]{4,3,2,1,0:T(8,128)S(1)}, f32[2,4,8,8,128]{4,3,2,1,0:T(8,128)S(1)}, u32[]{:S(2)}, u32[]{:S(2)}) collective-permute-start(f32[2,4,8,8,128]{4,3,2,1,0:T(8,128)S(1)} %shard_map.59.refs_0_), channel_id=1, source_target_pairs={{0,1},{1,0},{2,3},{3,2},{4,5},{5,4},{6,7},{7,6},{8,9},{9,8},{10,11... | collective-permute-start | bytes 786440 | tf_op jit(solution)/shard_map/ppermute | solution.py:26
  12.4 0.0 collective-permute-done.3.refs_4_
  12.4 0.5 collective-permute-done.2.refs_3_
  12.9 2.1 %collective-permute-start.7 = (f32[2,4,8,8,128]{4,3,2,1,0:T(8,128)S(1)}, f32[2,4,8,8,128]{4,3,2,1,0:T(8,128)S(1)}, u32[]{:S(2)}, u32[]{:S(2)}) collective-permute-start(f32[2,4,8,8,128]{4,3,2,1,0:T(8,128)S(1)} %broadcast_select_fusion), channel_id=1, source_target_pairs={{0,1},{1,0},{2,3},{3,2},{4,5},{5,4},{6,7},{7,6},{8,9},{9,8},{10,11... | collective-permute-start | bytes 786440 | tf_op jit(solution)/shard_map/ppermute | solution.py:26
  15.1 0.0 collective-permute-done.1.refs_2_
  15.1 3.8 %collective-permute-start.6 = (f32[2,4,8,8,128]{4,3,2,1,0:T(8,128)S(1)}, f32[2,4,8,8,128]{4,3,2,1,0:T(8,128)S(1)}, u32[]{:S(2)}, u32[]{:S(2)}) collective-permute-start(f32[2,4,8,8,128]{4,3,2,1,0:T(8,128)S(1)} %collective-permute-done.1.refs_2_), channel_id=1, source_target_pairs={{0,1},{1,0},{2,3},{3,2},{4,5},{5,4},{6,7},{7,6},{8,9},{9,8},{10,11... | collective-permute-start | bytes 786440 | tf_op jit(solution)/shard_map/ppermute | solution.py:26
  18.9 2.8 %collective-permute-done.refs_1_ = f32[2,4,8,8,128]{4,3,2,1,0:T(8,128)S(1)} collective-permute-done((f32[2,4,8,8,128]{4,3,2,1,0:T(8,128)S(1)}, f32[2,4,8,8,128]{4,3,2,1,0:T(8,128)S(1)}, u32[]{:S(2)}, u32[]{:S(2)}) %collective-permute-start) | collective-permute-done | bytes 262176 | tf_op jit(solution)/shard_map/ppermute | solution.py:26
  21.6 1.7 %collective-permute-start.5 = (f32[2,4,8,8,128]{4,3,2,1,0:T(8,128)S(1)}, f32[2,4,8,8,128]{4,3,2,1,0:T(8,128)S(1)}, u32[]{:S(2)}, u32[]{:S(2)}) collective-permute-start(f32[2,4,8,8,128]{4,3,2,1,0:T(8,128)S(1)} %collective-permute-done.refs_1_), channel_id=1, source_target_pairs={{0,1},{1,0},{2,3},{3,2},{4,5},{5,4},{6,7},{7,6},{8,9},{9,8},{10,11... | collective-permute-start | bytes 786440 | tf_op jit(solution)/shard_map/ppermute | solution.py:26
  23.3 0.0 collective-permute-done.4.refs_5_
  23.3 0.0 collective-permute-done.7.refs_8_
  23.3 0.0 collective-permute-done.6.refs_7_
  23.3 1.1 %collective-permute-done.5.refs_6_ = f32[2,4,8,8,128]{4,3,2,1,0:T(8,128)S(1)} collective-permute-done((f32[2,4,8,8,128]{4,3,2,1,0:T(8,128)S(1)}, f32[2,4,8,8,128]{4,3,2,1,0:T(8,128)S(1)}, u32[]{:S(2)}, u32[]{:S(2)}) %collective-permute-start.5) | collective-permute-done | bytes 262176 | tf_op jit(solution)/shard_map/ppermute | solution.py:26
  24.4 0.0 copy-start.2
  24.4 0.0 copy-start.3
  24.4 10.6 %shard_map.60 = (f32[4,8,8,128]{3,2,1,0:T(8,128)S(1)}, f32[36,8,8,128]{3,2,1,0:T(8,128)S(1)}) custom-call(s32[1]{0:T(128)} %bitcast.3.index_ref, f32[2,4,8,8,128]{4,3,2,1,0:T(8,128)S(1)} %shard_map.59.refs_0_, f32[2,4,8,8,128]{4,3,2,1,0:T(8,128)S(1)} %collective-permute-done.refs_1_, f32[2,4,8,8,128]{4,3,2,1,0:T(8,128)S(1)} %collective-permute-done.1.refs_2_, ...), custom_call_target="tpu_custom_call" | custom-call | tf_op jit(solution)/shard_map/pallas_call | solution.py:294
  35.0 0.7 collective-permute-start.9
  35.7 4.6 %collective-permute-start.8 = (f32[4,8,8,128]{3,2,1,0:T(8,128)S(1)}, f32[4,8,8,128]{3,2,1,0:T(8,128)S(1)}, u32[]{:S(2)}, u32[]{:S(2)}) collective-permute-start(f32[4,8,8,128]{3,2,1,0:T(8,128)S(1)} %get-tuple-element.6.refs_3_), channel_id=1, source_target_pairs={{0,16},{16,0},{32,48},{48,32},{64,80},{80,64},{96,112},{112,96},{1... | collective-permute-start | bytes 393224 | tf_op jit(solution)/shard_map/ppermute | solution.py:26
  40.3 0.0 collective-permute-done.9.refs_5_
  40.3 3.2 %collective-permute-done.8.refs_4_ = f32[4,8,8,128]{3,2,1,0:T(8,128)S(1)} collective-permute-done((f32[4,8,8,128]{3,2,1,0:T(8,128)S(1)}, f32[4,8,8,128]{3,2,1,0:T(8,128)S(1)}, u32[]{:S(2)}, u32[]{:S(2)}) %collective-permute-start.8) | collective-permute-done | bytes 131104 | tf_op jit(solution)/shard_map/ppermute | solution.py:26
  43.5 0.0 copy-done.2
  43.5 0.0 copy-done.3
  43.5 0.6 shard_map.61
  44.1 0.8 collective-permute-start.13
  44.9 1.0 collective-permute-start.12
  45.9 1.8 %collective-permute-start.14 = (f32[4,8,8,128]{3,2,1,0:T(8,128)S(1)}, f32[4,8,8,128]{3,2,1,0:T(8,128)S(1)}, u32[]{:S(2)}, u32[]{:S(2)}) collective-permute-start(f32[4,8,8,128]{3,2,1,0:T(8,128)S(1)} %get-tuple-element.7.refs_0_), channel_id=1, source_target_pairs={{0,1},{1,0},{2,3},{3,2},{4,5},{5,4},{6,7},{7,6},{8,9},{9,8},{10,11... | collective-permute-start | bytes 393224 | tf_op jit(solution)/shard_map/ppermute | solution.py:26
  47.7 2.8 %collective-permute-start.11 = (f32[4,8,8,128]{3,2,1,0:T(8,128)S(1)}, f32[4,8,8,128]{3,2,1,0:T(8,128)S(1)}, u32[]{:S(2)}, u32[]{:S(2)}) collective-permute-start(f32[4,8,8,128]{3,2,1,0:T(8,128)S(1)} %get-tuple-element.7.refs_0_), channel_id=1, source_target_pairs={{0,2},{1,3},{2,0},{3,1},{4,6},{5,7},{6,4},{7,5},{8,10},{9,11},{10,... | collective-permute-start | bytes 393224 | tf_op jit(solution)/shard_map/ppermute | solution.py:26
  50.5 1.6 %collective-permute-start.10 = (f32[4,8,8,128]{3,2,1,0:T(8,128)S(1)}, f32[4,8,8,128]{3,2,1,0:T(8,128)S(1)}, u32[]{:S(2)}, u32[]{:S(2)}) collective-permute-start(f32[4,8,8,128]{3,2,1,0:T(8,128)S(1)} %get-tuple-element.7.refs_0_), channel_id=1, source_target_pairs={{0,14},{1,15},{2,4},{3,5},{4,2},{5,3},{6,8},{7,9},{8,6},{9,7},{10,... | collective-permute-start | bytes 393224 | tf_op jit(solution)/shard_map/ppermute | solution.py:26
  52.1 0.0 collective-permute-done.13.refs_4_
  52.1 0.0 collective-permute-done.12.refs_3_
  52.1 0.6 collective-permute-start.17
  52.7 1.5 %collective-permute-done.11.refs_2_ = f32[4,8,8,128]{3,2,1,0:T(8,128)S(1)} collective-permute-done((f32[4,8,8,128]{3,2,1,0:T(8,128)S(1)}, f32[4,8,8,128]{3,2,1,0:T(8,128)S(1)}, u32[]{:S(2)}, u32[]{:S(2)}) %collective-permute-start.11) | collective-permute-done | bytes 131104 | tf_op jit(solution)/shard_map/ppermute | solution.py:26
  54.3 0.9 collective-permute-start.16
  55.1 3.7 %collective-permute-done.10.refs_1_ = f32[4,8,8,128]{3,2,1,0:T(8,128)S(1)} collective-permute-done((f32[4,8,8,128]{3,2,1,0:T(8,128)S(1)}, f32[4,8,8,128]{3,2,1,0:T(8,128)S(1)}, u32[]{:S(2)}, u32[]{:S(2)}) %collective-permute-start.10) | collective-permute-done | bytes 131104 | tf_op jit(solution)/shard_map/ppermute | solution.py:26
  58.9 1.1 %collective-permute-start.15 = (f32[4,8,8,128]{3,2,1,0:T(8,128)S(1)}, f32[4,8,8,128]{3,2,1,0:T(8,128)S(1)}, u32[]{:S(2)}, u32[]{:S(2)}) collective-permute-start(f32[4,8,8,128]{3,2,1,0:T(8,128)S(1)} %collective-permute-done.10.refs_1_), channel_id=1, source_target_pairs={{0,1},{1,0},{2,3},{3,2},{4,5},{5,4},{6,7},{7,6},{8,9},{9,8},{10,11... | collective-permute-start | bytes 393224 | tf_op jit(solution)/shard_map/ppermute | solution.py:26
  60.0 0.9 shard_map.62.refs_10_
  60.9 0.0 collective-permute-done.14.refs_5_
  60.9 0.0 collective-permute-done.17.refs_8_
  60.9 0.0 collective-permute-done.16.refs_7_
  60.9 0.1 collective-permute-done.15.refs_6_
  61.0 9.6 %shard_map.63.own = f32[4,8,8,128]{3,2,1,0:T(8,128)S(1)} custom-call(s32[1]{0:T(128)} %bitcast.3.index_ref, f32[4,8,8,128]{3,2,1,0:T(8,128)S(1)} %get-tuple-element.7.refs_0_, f32[4,8,8,128]{3,2,1,0:T(8,128)S(1)} %collective-permute-done.10.refs_1_, f32[4,8,8,128]{3,2,1,0:T(8,128)S(1)} %collective-permute-done.11.refs_2_, ...), custom_call_target="tpu_custom_call" | custom-call | tf_op jit(solution)/shard_map/pallas_call | solution.py:322
  70.6 1.3 %collective-permute-start.19 = (f32[4,8,8,128]{3,2,1,0:T(8,128)S(1)}, f32[4,8,8,128]{3,2,1,0:T(8,128)S(1)}, u32[]{:S(2)}, u32[]{:S(2)}) collective-permute-start(f32[4,8,8,128]{3,2,1,0:T(8,128)S(1)} %shard_map.63.own), channel_id=1, source_target_pairs={{16,0},{32,16},{48,32},{64,48},{80,64},{96,80},{112,96},{128,112},... | collective-permute-start | bytes 393224 | tf_op jit(solution)/shard_map/ppermute | solution.py:32
  71.9 5.3 %collective-permute-done.19.right = f32[4,8,8,128]{3,2,1,0:T(8,128)S(1)} collective-permute-done((f32[4,8,8,128]{3,2,1,0:T(8,128)S(1)}, f32[4,8,8,128]{3,2,1,0:T(8,128)S(1)}, u32[]{:S(2)}, u32[]{:S(2)}) %collective-permute-start.19) | collective-permute-done | bytes 131104 | tf_op jit(solution)/shard_map/ppermute | solution.py:32
  77.2 0.8 shard_map.65
  78.1 13.7 %all-to-all-start = ((f32[256,1,128]{2,1,0:T(1,128)}), f32[256,1,128]{2,1,0:T(1,128)S(1)}, u32[]{:S(2)}, u32[]{:S(2)}) async-start(f32[256,1,128]{2,1,0:T(1,128)} %shard_map.65), calls=%async_computation | async-start | bytes 262144 | tf_op jit(solution)/shard_map/all_to_all | solution.py:339
  91.8 3.4 %collective-permute-start.18 = (f32[4,8,8,128]{3,2,1,0:T(8,128)S(1)}, f32[4,8,8,128]{3,2,1,0:T(8,128)S(1)}, u32[]{:S(2)}, u32[]{:S(2)}) collective-permute-start(f32[4,8,8,128]{3,2,1,0:T(8,128)S(1)} %shard_map.63.own), channel_id=1, source_target_pairs={{0,16},{16,32},{32,48},{48,64},{64,80},{80,96},{96,112},{112,128},... | collective-permute-start | bytes 393224 | tf_op jit(solution)/shard_map/ppermute | solution.py:32
  95.2 3.9 %collective-permute-done.18.left = f32[4,8,8,128]{3,2,1,0:T(8,128)S(1)} collective-permute-done((f32[4,8,8,128]{3,2,1,0:T(8,128)S(1)}, f32[4,8,8,128]{3,2,1,0:T(8,128)S(1)}, u32[]{:S(2)}, u32[]{:S(2)}) %collective-permute-start.18) | collective-permute-done | bytes 131104 | tf_op jit(solution)/shard_map/ppermute | solution.py:32
  99.1 1.2 %shard_map.64 = f32[4,64,128]{2,1,0:T(8,128)} custom-call(s32[1]{0:T(128)} %bitcast.refs_0_.index_ref, s32[1,2]{1,0:T(1,128)S(1)} %bitcast.9, f32[1,2]{1,0:T(1,128)S(1)} %bitcast.11, f32[4,8,8,128]{3,2,1,0:T(8,128)S(1)} %shard_map.63.own, f32[4,8,8,128]{3,2,1,0:T(8,128)S(1)} %collective-permute-done.18.left, f32[4,8,8,128]{3,2,1,0:T(8,128)S(1)} %collective-permute-done.19.right), custom_call_target="tpu_custom_call" | custom-call | tf_op jit(solution)/shard_map/pallas_call | solution.py:340
  100.4 4.5 %all-to-all-done.refs_1_ = f32[256,1,128]{2,1,0:T(1,128)S(1)} async-done(((f32[256,1,128]{2,1,0:T(1,128)}), f32[256,1,128]{2,1,0:T(1,128)S(1)}, u32[]{:S(2)}, u32[]{:S(2)}) %all-to-all-start) | async-done | bytes 131104 | tf_op jit(solution)/shard_map/all_to_all | solution.py:339
  104.9 0.7 shard_map.66
  (2 shorter events, 0.0 us)
Async XLA Ops:
  0.6 0.9 copy-start
  1.5 0.9 copy-start.1
  2.8 9.6 %collective-permute-start.3 = (f32[2,4,8,8,128]{4,3,2,1,0:T(8,128)S(1)}, f32[2,4,8,8,128]{4,3,2,1,0:T(8,128)S(1)}, u32[]{:S(2)}, u32[]{:S(2)}) collective-permute-start(f32[2,4,8,8,128]{4,3,2,1,0:T(8,128)S(1)} %shard_map.59.refs_0_), channel_id=1, source_target_pairs={{0,4},{1,5},{2,6},{3,7},{4,0},{5,1},{6,2},{7,3},{8,12},{9,13},{10,... | collective-permute-start | bytes 786440 | tf_op jit(solution)/shard_map/ppermute | solution.py:26
  5.0 7.9 %collective-permute-start.2 = (f32[2,4,8,8,128]{4,3,2,1,0:T(8,128)S(1)}, f32[2,4,8,8,128]{4,3,2,1,0:T(8,128)S(1)}, u32[]{:S(2)}, u32[]{:S(2)}) collective-permute-start(f32[2,4,8,8,128]{4,3,2,1,0:T(8,128)S(1)} %shard_map.59.refs_0_), channel_id=1, source_target_pairs={{0,12},{1,13},{2,14},{3,15},{4,8},{5,9},{6,10},{7,11},{8,4},{9,5},... | collective-permute-start | bytes 786440 | tf_op jit(solution)/shard_map/ppermute | solution.py:26
  6.9 8.2 %collective-permute-start.1 = (f32[2,4,8,8,128]{4,3,2,1,0:T(8,128)S(1)}, f32[2,4,8,8,128]{4,3,2,1,0:T(8,128)S(1)}, u32[]{:S(2)}, u32[]{:S(2)}) collective-permute-start(f32[2,4,8,8,128]{4,3,2,1,0:T(8,128)S(1)} %shard_map.59.refs_0_), channel_id=1, source_target_pairs={{0,2},{1,3},{2,0},{3,1},{4,6},{5,7},{6,4},{7,5},{8,10},{9,11},{10,... | collective-permute-start | bytes 786440 | tf_op jit(solution)/shard_map/ppermute | solution.py:26
  9.7 11.9 %collective-permute-start = (f32[2,4,8,8,128]{4,3,2,1,0:T(8,128)S(1)}, f32[2,4,8,8,128]{4,3,2,1,0:T(8,128)S(1)}, u32[]{:S(2)}, u32[]{:S(2)}) collective-permute-start(f32[2,4,8,8,128]{4,3,2,1,0:T(8,128)S(1)} %shard_map.59.refs_0_), channel_id=1, source_target_pairs={{0,14},{1,15},{2,4},{3,5},{4,2},{5,3},{6,8},{7,9},{8,6},{9,7},{10,... | collective-permute-start | bytes 786440 | tf_op jit(solution)/shard_map/ppermute | solution.py:26
  10.4 12.9 %collective-permute-start.4 = (f32[2,4,8,8,128]{4,3,2,1,0:T(8,128)S(1)}, f32[2,4,8,8,128]{4,3,2,1,0:T(8,128)S(1)}, u32[]{:S(2)}, u32[]{:S(2)}) collective-permute-start(f32[2,4,8,8,128]{4,3,2,1,0:T(8,128)S(1)} %shard_map.59.refs_0_), channel_id=1, source_target_pairs={{0,1},{1,0},{2,3},{3,2},{4,5},{5,4},{6,7},{7,6},{8,9},{9,8},{10,11... | collective-permute-start | bytes 786440 | tf_op jit(solution)/shard_map/ppermute | solution.py:26
  12.9 10.3 %collective-permute-start.7 = (f32[2,4,8,8,128]{4,3,2,1,0:T(8,128)S(1)}, f32[2,4,8,8,128]{4,3,2,1,0:T(8,128)S(1)}, u32[]{:S(2)}, u32[]{:S(2)}) collective-permute-start(f32[2,4,8,8,128]{4,3,2,1,0:T(8,128)S(1)} %broadcast_select_fusion), channel_id=1, source_target_pairs={{0,1},{1,0},{2,3},{3,2},{4,5},{5,4},{6,7},{7,6},{8,9},{9,8},{10,11... | collective-permute-start | bytes 786440 | tf_op jit(solution)/shard_map/ppermute | solution.py:26
  15.1 8.2 %collective-permute-start.6 = (f32[2,4,8,8,128]{4,3,2,1,0:T(8,128)S(1)}, f32[2,4,8,8,128]{4,3,2,1,0:T(8,128)S(1)}, u32[]{:S(2)}, u32[]{:S(2)}) collective-permute-start(f32[2,4,8,8,128]{4,3,2,1,0:T(8,128)S(1)} %collective-permute-done.1.refs_2_), channel_id=1, source_target_pairs={{0,1},{1,0},{2,3},{3,2},{4,5},{5,4},{6,7},{7,6},{8,9},{9,8},{10,11... | collective-permute-start | bytes 786440 | tf_op jit(solution)/shard_map/ppermute | solution.py:26
  21.6 2.8 %collective-permute-start.5 = (f32[2,4,8,8,128]{4,3,2,1,0:T(8,128)S(1)}, f32[2,4,8,8,128]{4,3,2,1,0:T(8,128)S(1)}, u32[]{:S(2)}, u32[]{:S(2)}) collective-permute-start(f32[2,4,8,8,128]{4,3,2,1,0:T(8,128)S(1)} %collective-permute-done.refs_1_), channel_id=1, source_target_pairs={{0,1},{1,0},{2,3},{3,2},{4,5},{5,4},{6,7},{7,6},{8,9},{9,8},{10,11... | collective-permute-start | bytes 786440 | tf_op jit(solution)/shard_map/ppermute | solution.py:26
  24.4 19.1 %copy-start.2 = (s32[2,1]{0,1:T(1,128)S(1)}, s32[2,1]{0,1:T(1,128)}, u32[]{:S(2)}) copy-start(s32[2,1]{0,1:T(1,128)} %param.6) | copy-start | bytes 28
  24.4 19.1 %copy-start.3 = (f32[2,1]{0,1:T(1,128)S(1)}, f32[2,1]{0,1:T(1,128)}, u32[]{:S(2)}) copy-start(f32[2,1]{0,1:T(1,128)} %param.7) | copy-start | bytes 28
  35.0 5.3 %collective-permute-start.9 = (f32[4,8,8,128]{3,2,1,0:T(8,128)S(1)}, f32[4,8,8,128]{3,2,1,0:T(8,128)S(1)}, u32[]{:S(2)}, u32[]{:S(2)}) collective-permute-start(f32[4,8,8,128]{3,2,1,0:T(8,128)S(1)} %get-tuple-element.6.refs_3_), channel_id=1, source_target_pairs={{16,32},{32,16},{48,64},{64,48},{80,96},{96,80},{112,128},{128,112... | collective-permute-start | bytes 393224 | tf_op jit(solution)/shard_map/ppermute | solution.py:26
  35.7 7.8 %collective-permute-start.8 = (f32[4,8,8,128]{3,2,1,0:T(8,128)S(1)}, f32[4,8,8,128]{3,2,1,0:T(8,128)S(1)}, u32[]{:S(2)}, u32[]{:S(2)}) collective-permute-start(f32[4,8,8,128]{3,2,1,0:T(8,128)S(1)} %get-tuple-element.6.refs_3_), channel_id=1, source_target_pairs={{0,16},{16,0},{32,48},{48,32},{64,80},{80,64},{96,112},{112,96},{1... | collective-permute-start | bytes 393224 | tf_op jit(solution)/shard_map/ppermute | solution.py:26
  44.1 7.9 %collective-permute-start.13 = (f32[4,8,8,128]{3,2,1,0:T(8,128)S(1)}, f32[4,8,8,128]{3,2,1,0:T(8,128)S(1)}, u32[]{:S(2)}, u32[]{:S(2)}) collective-permute-start(f32[4,8,8,128]{3,2,1,0:T(8,128)S(1)} %get-tuple-element.7.refs_0_), channel_id=1, source_target_pairs={{0,4},{1,5},{2,6},{3,7},{4,0},{5,1},{6,2},{7,3},{8,12},{9,13},{10,... | collective-permute-start | bytes 393224 | tf_op jit(solution)/shard_map/ppermute | solution.py:26
  44.9 7.2 %collective-permute-start.12 = (f32[4,8,8,128]{3,2,1,0:T(8,128)S(1)}, f32[4,8,8,128]{3,2,1,0:T(8,128)S(1)}, u32[]{:S(2)}, u32[]{:S(2)}) collective-permute-start(f32[4,8,8,128]{3,2,1,0:T(8,128)S(1)} %get-tuple-element.7.refs_0_), channel_id=1, source_target_pairs={{0,12},{1,13},{2,14},{3,15},{4,8},{5,9},{6,10},{7,11},{8,4},{9,5},... | collective-permute-start | bytes 393224 | tf_op jit(solution)/shard_map/ppermute | solution.py:26
  45.9 15.0 %collective-permute-start.14 = (f32[4,8,8,128]{3,2,1,0:T(8,128)S(1)}, f32[4,8,8,128]{3,2,1,0:T(8,128)S(1)}, u32[]{:S(2)}, u32[]{:S(2)}) collective-permute-start(f32[4,8,8,128]{3,2,1,0:T(8,128)S(1)} %get-tuple-element.7.refs_0_), channel_id=1, source_target_pairs={{0,1},{1,0},{2,3},{3,2},{4,5},{5,4},{6,7},{7,6},{8,9},{9,8},{10,11... | collective-permute-start | bytes 393224 | tf_op jit(solution)/shard_map/ppermute | solution.py:26
  47.7 6.6 %collective-permute-start.11 = (f32[4,8,8,128]{3,2,1,0:T(8,128)S(1)}, f32[4,8,8,128]{3,2,1,0:T(8,128)S(1)}, u32[]{:S(2)}, u32[]{:S(2)}) collective-permute-start(f32[4,8,8,128]{3,2,1,0:T(8,128)S(1)} %get-tuple-element.7.refs_0_), channel_id=1, source_target_pairs={{0,2},{1,3},{2,0},{3,1},{4,6},{5,7},{6,4},{7,5},{8,10},{9,11},{10,... | collective-permute-start | bytes 393224 | tf_op jit(solution)/shard_map/ppermute | solution.py:26
  50.5 8.4 %collective-permute-start.10 = (f32[4,8,8,128]{3,2,1,0:T(8,128)S(1)}, f32[4,8,8,128]{3,2,1,0:T(8,128)S(1)}, u32[]{:S(2)}, u32[]{:S(2)}) collective-permute-start(f32[4,8,8,128]{3,2,1,0:T(8,128)S(1)} %get-tuple-element.7.refs_0_), channel_id=1, source_target_pairs={{0,14},{1,15},{2,4},{3,5},{4,2},{5,3},{6,8},{7,9},{8,6},{9,7},{10,... | collective-permute-start | bytes 393224 | tf_op jit(solution)/shard_map/ppermute | solution.py:26
  52.1 8.8 %collective-permute-start.17 = (f32[4,8,8,128]{3,2,1,0:T(8,128)S(1)}, f32[4,8,8,128]{3,2,1,0:T(8,128)S(1)}, u32[]{:S(2)}, u32[]{:S(2)}) collective-permute-start(f32[4,8,8,128]{3,2,1,0:T(8,128)S(1)} %broadcast_select_fusion.1), channel_id=1, source_target_pairs={{0,1},{1,0},{2,3},{3,2},{4,5},{5,4},{6,7},{7,6},{8,9},{9,8},{10,11... | collective-permute-start | bytes 393224 | tf_op jit(solution)/shard_map/ppermute | solution.py:26
  54.3 6.7 %collective-permute-start.16 = (f32[4,8,8,128]{3,2,1,0:T(8,128)S(1)}, f32[4,8,8,128]{3,2,1,0:T(8,128)S(1)}, u32[]{:S(2)}, u32[]{:S(2)}) collective-permute-start(f32[4,8,8,128]{3,2,1,0:T(8,128)S(1)} %collective-permute-done.11.refs_2_), channel_id=1, source_target_pairs={{0,1},{1,0},{2,3},{3,2},{4,5},{5,4},{6,7},{7,6},{8,9},{9,8},{10,11... | collective-permute-start | bytes 393224 | tf_op jit(solution)/shard_map/ppermute | solution.py:26
  58.9 2.1 %collective-permute-start.15 = (f32[4,8,8,128]{3,2,1,0:T(8,128)S(1)}, f32[4,8,8,128]{3,2,1,0:T(8,128)S(1)}, u32[]{:S(2)}, u32[]{:S(2)}) collective-permute-start(f32[4,8,8,128]{3,2,1,0:T(8,128)S(1)} %collective-permute-done.10.refs_1_), channel_id=1, source_target_pairs={{0,1},{1,0},{2,3},{3,2},{4,5},{5,4},{6,7},{7,6},{8,9},{9,8},{10,11... | collective-permute-start | bytes 393224 | tf_op jit(solution)/shard_map/ppermute | solution.py:26
  70.6 6.6 %collective-permute-start.19 = (f32[4,8,8,128]{3,2,1,0:T(8,128)S(1)}, f32[4,8,8,128]{3,2,1,0:T(8,128)S(1)}, u32[]{:S(2)}, u32[]{:S(2)}) collective-permute-start(f32[4,8,8,128]{3,2,1,0:T(8,128)S(1)} %shard_map.63.own), channel_id=1, source_target_pairs={{16,0},{32,16},{48,32},{64,48},{80,64},{96,80},{112,96},{128,112},... | collective-permute-start | bytes 393224 | tf_op jit(solution)/shard_map/ppermute | solution.py:32
  78.1 26.8 %all-to-all-start = ((f32[256,1,128]{2,1,0:T(1,128)}), f32[256,1,128]{2,1,0:T(1,128)S(1)}, u32[]{:S(2)}, u32[]{:S(2)}) async-start(f32[256,1,128]{2,1,0:T(1,128)} %shard_map.65), calls=%async_computation | async-start | bytes 262144 | tf_op jit(solution)/shard_map/all_to_all | solution.py:339
  91.8 7.3 %collective-permute-start.18 = (f32[4,8,8,128]{3,2,1,0:T(8,128)S(1)}, f32[4,8,8,128]{3,2,1,0:T(8,128)S(1)}, u32[]{:S(2)}, u32[]{:S(2)}) collective-permute-start(f32[4,8,8,128]{3,2,1,0:T(8,128)S(1)} %shard_map.63.own), channel_id=1, source_target_pairs={{0,16},{16,32},{32,48},{48,64},{64,80},{80,96},{96,112},{112,128},... | collective-permute-start | bytes 393224 | tf_op jit(solution)/shard_map/ppermute | solution.py:32
